TPU v7x, 512 devices: a whole 4x8x8 slice. The times are simulated.
512 devices in a mesh: seq: 32 (over y, x), head: 16 (over z, core).
Axes of the slice: x: 4, y: 8, z: 8, core: 2. Of those that a mesh axis runs over, the one named last changes fastest.
Arguments:
- x_input: bfloat16 [4096, 16384], P('seq', 'head'), may hold values from -6 to 6
- z_input: bfloat16 [4096, 16384], P('seq', 'head'), may hold values from -52 to 52
- bc_input: bfloat16 [2, 4096, 128], P(None, 'seq'), may hold values from -2.09375 to 2.09375
- dt_raw: float32 [128, 4096], P('head', 'seq'), may hold values from -1.5 to 4.5
- dt_bias: float32 [128], P('head'), may hold values from -4.2 to 0.3
- a_log: float32 [128], P('head')
- d_skip: float32 [128], P('head'), may hold values from 0.5 to 1.5
- conv_x: float32 [4, 16384], P(None, 'head'), may hold values from -3 to 3
- convolution_bc_taps: float32 [2, 4, 128], replicated, may hold values from -3 to 3
- rescale_factor: float32 [16384], P('head'), may hold values from 0.5 to 1.5
- grad_out: bfloat16 [4096, 16384], P('seq', 'head'), may hold values from -40 to 40
Outputs:
- grad_x: bfloat16 [4096, 16384], P('seq', 'head')
- grad_z: bfloat16 [4096, 16384], P('seq', 'head')
- grad_bc: bfloat16 [2, 4096, 128], P(None, ('seq', 'head'))
- grad_dt: float32 [128, 4096], P('head', 'seq')
All inputs are finite; a program needn't handle non-finite values.
Results may differ from a plain program's by a relative error of at most 0.0086.
Values may be sent and summed in bfloat16 or wider, within the bound.
A program may use at most 64 MiB of HBM per device.

v0:
```python
import jax
import jax.numpy as jnp
from jax import lax
from jax.sharding import PartitionSpec as P

INNER = 16384


EPS = 1e-05


def entering(part, axis, combine, identity, reverse):
    count = lax.axis_size(axis)
    place = lax.axis_index(axis)
    ahead = count - 1 - place if reverse else place
    gathered = jax.tree.map(lambda a: lax.all_gather(a, axis), part)
    state = jax.tree.map(lambda a, e: jnp.zeros_like(a) + jnp.asarray(e, a.dtype), part, identity)

    def one(hop, state):
        source = count - 1 - hop if reverse else hop
        return combine(
            state, jax.tree.map(lambda a: lax.dynamic_index_in_dim(a, source, 0, False), gathered)
        )

    return lax.fori_loop(0, ahead, one, state)


def passed_along(block, axis, distance):
    devices = range(lax.axis_size(axis))
    route = [(i - distance, i) for i in devices if i - distance in devices]
    return lax.ppermute(block, axis, route)


def silu_grad(value):
    sigma = jax.nn.sigmoid(value)
    return sigma * (1.0 + value * (1.0 - sigma))


def conv_rows(extended, weight_matrix):
    length = extended.shape[-2] - 3
    summed = weight_matrix[..., 0, :][..., None, :] * extended[..., 0:length, :]
    for offset in range(1, 4):
        summed = (
            summed
            + weight_matrix[..., offset, :][..., None, :]
            * extended[..., offset : offset + length, :]
        )
    return summed


def conv_back(extended, weight_matrix):
    length = extended.shape[-2] - 3
    summed = weight_matrix[..., 0, :][..., None, :] * extended[..., 3 : 3 + length, :]
    for offset in range(1, 4):
        summed = (
            summed
            + weight_matrix[..., offset, :][..., None, :]
            * extended[..., 3 - offset : 3 - offset + length, :]
        )
    return summed


def decay_of(cumul, causal):
    between = cumul[:, None] - cumul[None, :]
    return jnp.where(causal, jnp.exp(jnp.minimum(between, 0.0)), 0.0)


def weighted_rows(trailing_decay, step_size, b_rows):
    return ((trailing_decay * step_size)[:, None] * b_rows.astype(jnp.float32)).astype(jnp.bfloat16)


def head_forward(cumul, step_size, gram_matrix, x_head, state_low, c_rows, skip_gain, causal):
    decay_matrix = decay_of(cumul, causal)
    mixer_low = (gram_matrix * decay_matrix * step_size[None, :]).astype(jnp.bfloat16)
    intra_out = jnp.dot(mixer_low, x_head, preferred_element_type=jnp.float32)
    handed_forward = jnp.dot(c_rows, state_low, preferred_element_type=jnp.float32)
    return (
        intra_out
        + jnp.exp(cumul)[:, None] * handed_forward
        + skip_gain * x_head.astype(jnp.float32)
    )


def head_backward(
    cumul,
    step_size,
    gram_matrix,
    x_head,
    grad_head,
    state_low,
    state_exact,
    out_low,
    out_exact,
    b_rows,
    c_rows,
    skip_gain,
    decay_rate,
    causal,
):
    decay_matrix = decay_of(cumul, causal)
    mixer_low = (gram_matrix * decay_matrix * step_size[None, :]).astype(jnp.bfloat16)
    grad_mix = jnp.dot(grad_head, x_head.T, preferred_element_type=jnp.float32)
    decayed_grad = grad_mix * decay_matrix
    weighted_grad = decayed_grad * step_size[None, :]
    gram_grad = weighted_grad * gram_matrix
    lifted = jnp.exp(cumul)
    handed_forward = jnp.dot(c_rows, state_low, preferred_element_type=jnp.float32)
    reached = jnp.dot(x_head, out_low.T, preferred_element_type=jnp.float32)
    trailing_decay = jnp.exp(cumul[-1] - cumul)
    inner_b = jnp.sum(b_rows.astype(jnp.float32) * reached, axis=1)
    state_term = trailing_decay * step_size * inner_b
    grad_cumul = jnp.sum(gram_grad, axis=1) - jnp.sum(gram_grad, axis=0)
    grad_cumul = (
        grad_cumul
        + lifted * jnp.sum(grad_head.astype(jnp.float32) * handed_forward, axis=1)
        - state_term
    )
    end_grad = jnp.sum(state_term) + jnp.exp(cumul[-1]) * jnp.sum(out_exact * state_exact)
    grad_cumul = grad_cumul.at[-1].add(end_grad)
    grad_log = jnp.cumsum(grad_cumul[::-1])[::-1]
    grad_step = (
        jnp.sum(decayed_grad * gram_matrix, axis=0)
        + trailing_decay * inner_b
        + decay_rate * grad_log
    )
    weighted_b = weighted_rows(trailing_decay, step_size, b_rows)
    grad_x = jnp.dot(mixer_low.T, grad_head, preferred_element_type=jnp.float32)
    grad_x = (
        grad_x
        + skip_gain * grad_head.astype(jnp.float32)
        + jnp.dot(weighted_b, out_low, preferred_element_type=jnp.float32)
    )
    grad_c = lifted[:, None] * jnp.dot(grad_head, state_low.T, preferred_element_type=jnp.float32)
    grad_b = (trailing_decay * step_size)[:, None] * reached
    return (grad_x, grad_step, grad_c, grad_b, weighted_grad)


def block_prep(x_rows, b_rows, step_size, decay_rate):
    length = x_rows.shape[0]
    head_count = step_size.shape[0]
    cumul = jnp.cumsum(decay_rate[:, None] * step_size, axis=1)
    trailing_decay = jnp.exp(cumul[:, -1:] - cumul)
    x_heads = jnp.moveaxis(x_rows.reshape(length, head_count, -1), 1, 0)

    def one_head(head_items):
        weighted_b = weighted_rows(head_items[0], head_items[1], b_rows)
        return jnp.dot(weighted_b.T, head_items[2], preferred_element_type=jnp.float32)

    local_state = lax.map(one_head, (trailing_decay, step_size, x_heads))
    return (cumul, x_heads, local_state)


def block_mix(cumul, step_size, gram_matrix, x_heads, state_low, c_rows, skip_gain, causal):

    def one_head(head_items):
        return head_forward(
            head_items[0],
            head_items[1],
            gram_matrix,
            head_items[2],
            head_items[3],
            c_rows,
            head_items[4],
            causal,
        )

    outputs = lax.map(one_head, (cumul, step_size, x_heads, state_low, skip_gain))
    return jnp.moveaxis(outputs, 0, 1).reshape(outputs.shape[1], -1)


def carry_grad(cumul, c_rows, grad_heads):

    def one_head(head_items):
        lifted_c = (jnp.exp(head_items[0])[:, None] * c_rows.astype(jnp.float32)).astype(
            jnp.bfloat16
        )
        return jnp.dot(lifted_c.T, head_items[1], preferred_element_type=jnp.float32)

    return lax.map(one_head, (cumul, grad_heads))


def block_back(
    cumul,
    step_size,
    gram_matrix,
    x_heads,
    grad_heads,
    state_exact,
    out_exact,
    b_rows,
    c_rows,
    skip_gain,
    decay_rate,
    causal,
):
    length = b_rows.shape[0]
    nstate = b_rows.shape[1]
    state_low = state_exact.astype(jnp.bfloat16)
    out_low = out_exact.astype(jnp.bfloat16)

    def one_head(running, head_items):
        (
            cumulative_head,
            step_head,
            x_head,
            grad_head,
            low_in,
            exact_in,
            low_out,
            exact_out,
            skip_head,
            rate_head,
        ) = head_items
        grad_x, grad_step, grad_c, grad_b, weighted_grad = head_backward(
            cumulative_head,
            step_head,
            gram_matrix,
            x_head,
            grad_head,
            low_in,
            exact_in,
            low_out,
            exact_out,
            b_rows,
            c_rows,
            skip_head,
            rate_head,
            causal,
        )
        return (
            (running[0] + weighted_grad, running[1] + grad_c, running[2] + grad_b),
            (grad_x, grad_step),
        )

    initial = (
        jnp.zeros((length, length), jnp.float32),
        jnp.zeros((length, nstate), jnp.float32),
        jnp.zeros((length, nstate), jnp.float32),
    )
    (grad_sum, c_sum, b_sum), (grad_xs, grad_steps) = lax.scan(
        one_head,
        initial,
        (
            cumul,
            step_size,
            x_heads,
            grad_heads,
            state_low,
            state_exact,
            out_low,
            out_exact,
            skip_gain,
            decay_rate,
        ),
    )
    grad_c = c_sum + jnp.dot(grad_sum, b_rows.astype(jnp.float32), precision=lax.Precision.HIGHEST)
    grad_b = b_sum + jnp.dot(
        grad_sum.T, c_rows.astype(jnp.float32), precision=lax.Precision.HIGHEST
    )
    grad_x = jnp.moveaxis(grad_xs, 0, 1).reshape(length, -1)
    return (grad_x, jnp.stack([grad_b, grad_c]), grad_steps)


def pass_states(totals, states, reverse):
    factor = jnp.exp(totals)[:, None, None]

    def combine(earlier, latter):
        return (earlier[0] * latter[0], latter[0] * earlier[1] + latter[1])

    result = entering(
        (factor, states), "seq", combine, (jnp.ones_like(factor), jnp.zeros_like(states)), reverse
    )
    return result[1]


def shards(
    x_input,
    z_input,
    bc_input,
    dt_raw,
    dt_bias,
    a_log,
    d_skip,
    conv_x,
    convolution_bc_taps,
    rescale_factor,
    grad_out,
):
    length = x_input.shape[0]
    head_count = dt_raw.shape[0]
    decay_rate = -jnp.exp(a_log)
    step_size = jax.nn.softplus(dt_raw + dt_bias[:, None])
    causal = jnp.tril(jnp.ones((length, length), dtype=bool))
    rows_prior = passed_along((x_input[length - 3 :], bc_input[:, length - 3 :]), "seq", 1)
    x_ext = jnp.concatenate([rows_prior[0], x_input], axis=0)
    bc_ext = jnp.concatenate([rows_prior[1], bc_input], axis=1)
    x_pre = conv_rows(x_ext.astype(jnp.float32), conv_x)
    bc_pre = conv_rows(bc_ext.astype(jnp.float32), convolution_bc_taps)
    x_rows = jax.nn.silu(x_pre).astype(jnp.bfloat16)
    bc_rows = jax.nn.silu(bc_pre).astype(jnp.bfloat16)
    gram_matrix = jnp.dot(bc_rows[1], bc_rows[0].T, preferred_element_type=jnp.float32)
    cumul, x_heads, local_state = block_prep(x_rows, bc_rows[0], step_size, decay_rate)
    totals = cumul[:, -1]
    state_exact = pass_states(totals, local_state, False)
    mixed_out = block_mix(
        cumul,
        step_size,
        gram_matrix,
        x_heads,
        state_exact.astype(jnp.bfloat16),
        bc_rows[1],
        d_skip,
        causal,
    )
    z_rows = z_input.astype(jnp.float32)
    gate_value = jax.nn.silu(z_rows)
    gated = mixed_out * gate_value
    square_sum = lax.psum(jnp.sum(gated * gated, axis=1), "head")
    inv_rms = lax.rsqrt(square_sum / INNER + EPS)
    normed = gated * inv_rms[:, None]
    scaled = grad_out.astype(jnp.float32) * rescale_factor
    product_sum = lax.psum(jnp.sum(scaled * normed, axis=1), "head")
    mean_dot = product_sum / INNER
    grad_gated = inv_rms[:, None] * (scaled - normed * mean_dot[:, None])
    grad_z = (grad_gated * mixed_out * silu_grad(z_rows)).astype(jnp.bfloat16)
    grad_mixed = (grad_gated * gate_value).astype(jnp.bfloat16)
    grad_heads = jnp.moveaxis(grad_mixed.reshape(length, head_count, -1), 1, 0)
    state_grad = carry_grad(cumul, bc_rows[1], grad_heads)
    out_exact = pass_states(totals, state_grad, True)
    grad_x_rows, grad_bc_rows, grad_steps = block_back(
        cumul,
        step_size,
        gram_matrix,
        x_heads,
        grad_heads,
        state_exact,
        out_exact,
        bc_rows[0],
        bc_rows[1],
        d_skip,
        decay_rate,
        causal,
    )
    grad_x_pre = grad_x_rows * silu_grad(x_pre)
    row_share = length // lax.axis_size("head")
    first_row = lax.axis_index("head") * row_share
    grad_bc_all = lax.psum(grad_bc_rows, "head")
    grad_bc_pre = grad_bc_all * silu_grad(bc_pre)
    rows_next = passed_along((grad_x_pre[:3], grad_bc_pre[:, :3]), "seq", -1)
    grad_x = conv_back(jnp.concatenate([grad_x_pre, rows_next[0]], axis=0), conv_x).astype(
        jnp.bfloat16
    )
    grad_bc_full = conv_back(
        jnp.concatenate([grad_bc_pre, rows_next[1]], axis=1), convolution_bc_taps
    )
    grad_bc = lax.dynamic_slice_in_dim(grad_bc_full, first_row, row_share, 1).astype(jnp.bfloat16)
    grad_dt = grad_steps * jax.nn.sigmoid(dt_raw + dt_bias[:, None])
    return (grad_x, grad_z, grad_bc, grad_dt)


def solution(mesh):
    return jax.shard_map(
        shards,
        mesh=mesh,
        in_specs=(
            P("seq", "head"),
            P("seq", "head"),
            P(None, "seq", None),
            P("head", "seq"),
            P("head"),
            P("head"),
            P("head"),
            P(None, "head"),
            P(),
            P("head"),
            P("seq", "head"),
        ),
        out_specs=(
            P("seq", "head"),
            P("seq", "head"),
            P(None, ("seq", "head"), None),
            P("head", "seq"),
        ),
        check_vma=False,
    )
```

profile of v0, /device:TPU:1, one launch (start us, length us, event | category | flops | bytes accessed | tf_op | source)
XLA Modules:
  0.0 693.0 jit_solution(10006820068092498792)
XLA Ops:
  8.0 3.9 collective-permute-start
  12.7 3.1 collective-permute-start.1
  22.6 2.3 while.85
  25.8 1.3 dynamic-slice.7
  28.0 57.6 %all-reduce = f32[256]{0:T(256)S(1)} all-reduce(f32[256]{0:T(256)S(1)} %dynamic-update-slice.5), channel_id=2, replica_groups=mesh['seq'=32,'head'=16] {'seq'}, use_global_device_ids=true, to_apply=%add | all-reduce | flops 256 | bytes 2048
  85.9 89.4 %all-gather.6.cloned.1.call-done = f32[256,128,128]{2,1,0:T(8,128)} async-done(((f32[8,128,128]{2,1,0:T(8,128)}), f32[256,128,128]{2,1,0:T(8,128)}) %all-gather.6.cloned.1.call-update) | async-done | bytes 16777232 | tf_op jit(solution)/shard_map/all_gather | solution.py:16
  175.5 13.1 %while.89 = (s32[]{:T(128)}, f32[8,128,128]{2,1,0:T(8,128)S(1)}, f32[8,128]{1,0:T(8,128)S(1)}, f32[128,128]{1,0:T(8,128)S(1)}, f32[8,128]{1,0:T(8,128)S(1)}, /*i...) while((s32[]{:T(128)}, f32[8,128,128]{2,1,0:T(8,128)S(1)}, ...), condition=%wide.region_6.7_spmd.clone.clone, body=%wide.region_5.6_spmd.clone.sunk.clone | while | flops 8585218 | bytes 399477 | solution.py:167
  188.9 25.1 %psum.21 = f32[128]{0:T(128)S(1)} all-reduce(f32[128]{0:T(128)S(1)} %multiply_reduce_fusion.4), channel_id=1, replica_groups=mesh['seq'=32,'head'=16] {'head'}, use_global_device_ids=true, to_apply=%region_8.9 | all-reduce | flops 128 | bytes 1024 | tf_op jit(solution)/shard_map/psum | solution.py:318
  214.3 25.4 %psum.22 = f32[128]{0:T(128)S(1)} all-reduce(f32[128]{0:T(128)S(1)} %multiply_reduce_fusion.3), channel_id=1, replica_groups=mesh['seq'=32,'head'=16] {'head'}, use_global_device_ids=true, to_apply=%region_10.11 | all-reduce | flops 128 | bytes 1024 | tf_op jit(solution)/shard_map/psum | solution.py:322
  241.0 2.3 while.87
  244.3 175.6 %all-gather.8.cloned.1.call-done = f32[256,128,128]{2,1,0:T(8,128)} async-done(((f32[8,128,128]{2,1,0:T(8,128)}), f32[256,128,128]{2,1,0:T(8,128)}) %all-gather.8.cloned.1.call-update) | async-done | bytes 16777232 | tf_op jit(solution)/shard_map/all_gather | solution.py:16
  420.0 38.3 %while.88 = (s32[]{:T(128)}, f32[8,128,128]{2,1,0:T(8,128)S(1)}, s32[]{:T(128)}, f32[32,8,1,1]{1,3,2,0:T(1,128)S(1)}, f32[32,8,128,128]{3,2,1,0:T(8,128)}) while((s32[]{:T(128)}, f32[8,128,128]{2,1,0:T(8,128)S(1)}, s32[]{:T(128)}, f32[32,8,1,1]{1,3,2,0:T(1,128)S(1)}, f32[32,8,128,128]{3,2,1,0:T(8,128)}) %tuple.222), condition=%wide.region_14.15_spmd.clone, body=%wide.region_13.14_spmd.sunk.clone | while | flops 262150 | bytes 1573075 | solution.py:25
  459.0 112.0 %while.90 = (s32[]{:T(128)}, f32[128,128]{1,0:T(8,128)S(1)}, f32[128,128]{1,0:T(8,128)S(1)}, f32[128,128]{0,1:T(8,128)S(1)}, f32[8,128,128]{2,1,0:T(8,128)S(1)},...) while((s32[]{:T(128)}, f32[128,128]{1,0:T(8,128)S(1)}, ...), condition=%wide.region_24.25_spmd.clone.clone, body=%wide.region_15.24_spmd.clone.sunk.clone | while | flops 25854976 | bytes 1473321 | solution.py:240
  460.6 1.3 multiply_reduce_fusion.9
  465.9 1.3 dynamic_slice.354
  467.1 1.3 add_bitcast_fusion.3
  468.4 1.3 dynamic_update_slice.44
  474.6 1.3 multiply_reduce_fusion.9
  479.9 1.3 dynamic_slice.354
  481.1 1.3 add_bitcast_fusion.3
  482.4 1.3 dynamic_update_slice.44
  488.6 1.3 multiply_reduce_fusion.9
  493.9 1.3 dynamic_slice.354
  495.1 1.3 add_bitcast_fusion.3
  496.4 1.3 dynamic_update_slice.44
  502.6 1.3 multiply_reduce_fusion.9
  507.9 1.3 dynamic_slice.354
  509.1 1.3 add_bitcast_fusion.3
  510.4 1.3 dynamic_update_slice.44
  516.6 1.3 multiply_reduce_fusion.9
  521.9 1.3 dynamic_slice.354
  523.1 1.3 add_bitcast_fusion.3
  524.4 1.3 dynamic_update_slice.44
  530.6 1.3 multiply_reduce_fusion.9
  537.1 1.3 add_bitcast_fusion.3
  538.4 1.3 dynamic_update_slice.44
  544.6 1.3 multiply_reduce_fusion.9
  551.1 1.3 add_bitcast_fusion.3
  552.4 1.3 dynamic_update_slice.44
  558.6 1.3 multiply_reduce_fusion.9
  565.1 1.3 add_bitcast_fusion.3
  566.4 1.3 dynamic_update_slice.44
  572.5 1.3 collective-permute-start.2
  573.8 1.4 divide_multiply_fusion
  575.2 1.8 collective-permute-done.2
  577.9 102.6 %all-reduce.3.cloned.1.call-done = f32[2,128,128]{2,1,0:T(8,128)} async-done(((f32[2,128,128]{2,1,0:T(8,128)}), f32[2,128,128]{2,1,0:T(8,128)}) %all-reduce.3.cloned.1.call-update) | async-done | bytes 131088 | tf_op jit(solution)/shard_map/psum | solution.py:347
  681.5 1.3 collective-permute-start.3
  682.9 3.0 collective-permute-done.3
  (356 shorter events, 129.4 us)
Async XLA Ops:
  7.2 168.3 %copy-start.7 = (f32[8]{0:T(128)S(1)}, f32[8]{0:T(128)}, u32[]{:S(2)}) copy-start(f32[8]{0:T(128)} %param.31) | copy-start | bytes 100
  7.2 181.4 %copy-start = (bf16[128,1024]{1,0:T(8,128)(2,1)S(1)}, bf16[128,1024]{1,0:T(8,128)(2,1)}, u32[]{:S(2)}) copy-start(bf16[128,1024]{1,0:T(8,128)(2,1)} %param.26) | copy-start | bytes 786436
  7.2 206.8 %copy-start.4 = (f32[1024]{0:T(1024)S(1)}, f32[1024]{0:T(1024)}, u32[]{:S(2)}) copy-start(f32[1024]{0:T(1024)} %param.34) | copy-start | bytes 12292
  7.2 206.8 %copy-start.3 = (bf16[128,1024]{1,0:T(8,128)(2,1)S(1)}, bf16[128,1024]{1,0:T(8,128)(2,1)}, u32[]{:S(2)}) copy-start(bf16[128,1024]{1,0:T(8,128)(2,1)} %param.35) | copy-start | bytes 786436
  7.2 168.1 %all-gather.6.cloned.1.call-start = ((), (), s32[]{:S(2)}) async-start(), calls=%async_computation.1 | async-start | bytes 17301504 | tf_op jit(solution)/shard_map/all_gather | solution.py:16
  8.0 11.5 %collective-permute-start = (bf16[2,3,128]{2,1,0:T(4,128)(2,1)S(1)}, bf16[2,3,128]{2,1,0:T(4,128)(2,1)S(1)}, u32[]{:S(2)}, u32[]{:S(2)}) collective-permute-start(bf16[2,3,128]{2,1,0:T(4,128)(2,1)S(1)} %slice.125), channel_id=1, source_target_pairs={{0,16},{16,32},{32,48},{48,64},{64,80},{80,96},{96,112},{112,128},... | collective-permute-start | bytes 4616 | tf_op jit(solution)/shard_map/ppermute | solution.py:31
  12.7 8.5 %collective-permute-start.1 = (bf16[3,1024]{1,0:T(4,128)(2,1)S(1)}, bf16[3,1024]{1,0:T(4,128)(2,1)S(1)}, u32[]{:S(2)}, u32[]{:S(2)}) collective-permute-start(bf16[3,1024]{1,0:T(4,128)(2,1)S(1)} %slice.135), channel_id=1, source_target_pairs={{0,16},{16,32},{32,48},{48,64},{64,80},{80,96},{96,112},{112,128},... | collective-permute-start | bytes 18440 | tf_op jit(solution)/shard_map/ppermute | solution.py:31
  17.3 0.8 copy-start.6
  24.9 0.8 copy-start.1
  25.8 394.2 %all-gather.8.cloned.1.call-start = ((), (), s32[]{:S(2)}) async-start(), calls=%async_computation.2 | async-start | bytes 17301504 | tf_op jit(solution)/shard_map/all_gather | solution.py:16
  175.3 398.4 %copy-start.5 = (f32[8,128]{1,0:T(8,128)S(1)}, f32[8,128]{1,0:T(8,128)}, u32[]{:S(2)}) copy-start(f32[8,128]{1,0:T(8,128)} %param.28) | copy-start | bytes 12292
  243.3 0.8 copy-start.2
  244.1 436.4 %all-reduce.3.cloned.1.call-start = ((), (), s32[]{:S(2)}) async-start(), calls=%async_computation | async-start | bytes 262144 | tf_op jit(solution)/shard_map/psum | solution.py:347
  572.5 4.5 collective-permute-start.2
  681.5 4.4 collective-permute-start.3
Sparse Core Ops, SparseCore 0:
  25.9 149.3 all-gather.5
  244.2 175.6 all-gather.7
  572.4 108.0 all-reduce.2
where the time goes:
time: 700 us; the launch traced here: 693 us
  waiting for transfers between devices  373 us (53%)
  blocking collectives  108 us (15%)
  other arithmetic  78.7 us (11%)
  local copies, waits for them, and re-layouts  50 us (7%)
  matrix products  40.3 us (6%)
  loops' own time  18.7 us (3%)
  between operations  14.8 us (2%)
  starting transfers between devices  9.75 us (1%)
    all_gather x2, waiting for transfers between devices, entering(): gathered = jax.tree.map(lambda a: lax.all_gather(a, axis), part)  265 us
    psum x1, waiting for transfers between devices, shards(): grad_bc_all = lax.psum(grad_bc_rows, 'head')  103 us
    unnamed x1, blocking collectives  57.6 us
    add x31, other arithmetic, combine(): return (earlier[0] * latter[0], latter[0] * earlier[1] + latter[1])  36.9 us
    psum x1, blocking collectives, shards(): product_sum = lax.psum(jnp.sum(scaled * normed, axis=1), 'head')  25.4 us
    psum x1, blocking collectives, shards(): square_sum = lax.psum(jnp.sum(gated * gated, axis=1), 'head')  25.1 us
    dynamic_slice x24, local copies, waits for them, and re-layouts, block_mix(): lax.map(one_head, (cumul, step_size, x_heads, state_low, skip_gain))  24.8 us
    another operation x1, loops' own time, block_back(): lax.scan(one_head, initial, (cumul, step_size, x_heads, grad_heads, state...  16.9 us
  transfers between devices with their start and end apart: 7, of which 5 were waited for; matrix products, arithmetic and copies ran while one was open for 2% of the time, Pallas kernels for 0%

commit v1 on v0

v1 whole, which is shorter than its diff:
```python
import jax
import jax.numpy as jnp
from jax import lax
from jax.sharding import PartitionSpec as P

INNER = 16384


EPS = 1e-05
HIGH = lax.Precision.HIGHEST


def passed_along(block, axis, distance):
    devices = range(lax.axis_size(axis))
    route = [(i - distance, i) for i in devices if i - distance in devices]
    return lax.ppermute(block, axis, route)


def silu_grad(value):
    sigma = jax.nn.sigmoid(value)
    return sigma * (1.0 + value * (1.0 - sigma))


def conv_rows(extended, weight_matrix):
    length = extended.shape[-2] - 3
    summed = weight_matrix[..., 0, :][..., None, :] * extended[..., 0:length, :]
    for offset in range(1, 4):
        summed = (
            summed
            + weight_matrix[..., offset, :][..., None, :]
            * extended[..., offset : offset + length, :]
        )
    return summed


def conv_back(extended, weight_matrix):
    length = extended.shape[-2] - 3
    summed = weight_matrix[..., 0, :][..., None, :] * extended[..., 3 : 3 + length, :]
    for offset in range(1, 4):
        summed = (
            summed
            + weight_matrix[..., offset, :][..., None, :]
            * extended[..., 3 - offset : 3 - offset + length, :]
        )
    return summed


def to_pieces(state, count):
    heads, nstate, width = state.shape
    rows = nstate // count
    return jnp.moveaxis(state.reshape(heads, count, rows, width), 1, 0)


def from_pieces(pieces):
    count, heads, rows, width = pieces.shape
    return jnp.moveaxis(pieces, 0, 1).reshape(heads, count * rows, width)


def scan_forward(totals, local_state):
    count = lax.axis_size("seq")
    heads, nstate, width = local_state.shape
    pieces = to_pieces(local_state, count)
    rows = pieces.shape[2]
    tot_row = jnp.zeros((count, heads, 1, width), jnp.float32)
    tot_row = tot_row.at[:, :, 0, 0].set(jnp.broadcast_to(totals, (count, heads)))
    sent = jnp.concatenate([pieces, tot_row], axis=2)
    got = lax.all_to_all(sent, "seq", 0, 0, tiled=True)
    block_totals = got[:, :, rows, 0]
    running = jnp.cumsum(block_totals, axis=0)
    before = running - block_totals
    later = jnp.arange(count)[:, None] > jnp.arange(count)[None, :]
    gap = before.T[:, :, None] - running.T[:, None, :]
    weight = jnp.where(later[None], jnp.exp(jnp.minimum(gap, 0.0)), 0.0)
    data = got[:, :, :rows, :].reshape(count, heads, rows * width)
    scanned = jnp.einsum("hkj,jhx->khx", weight, data, precision=HIGH)
    back = lax.all_to_all(scanned.reshape(count, heads, rows, width), "seq", 0, 0, tiled=True)
    return from_pieces(back), weight


def scan_backward(weight, state_grad):
    count = lax.axis_size("seq")
    heads, nstate, width = state_grad.shape
    pieces = to_pieces(state_grad, count)
    rows = pieces.shape[2]
    got = lax.all_to_all(pieces, "seq", 0, 0, tiled=True)
    data = got.reshape(count, heads, rows * width)
    scanned = jnp.einsum("hjk,jhx->khx", weight, data, precision=HIGH)
    back = lax.all_to_all(scanned.reshape(count, heads, rows, width), "seq", 0, 0, tiled=True)
    return from_pieces(back)


def shards(
    x_input,
    z_input,
    bc_input,
    dt_raw,
    dt_bias,
    a_log,
    d_skip,
    conv_x,
    convolution_bc_taps,
    rescale_factor,
    grad_out,
):
    length = x_input.shape[0]
    channels = x_input.shape[1]
    head_count = dt_raw.shape[0]
    width = channels // head_count
    f32 = jnp.float32
    bf16 = jnp.bfloat16
    decay_rate = -jnp.exp(a_log)
    step_size = jax.nn.softplus(dt_raw + dt_bias[:, None])
    causal = jnp.tril(jnp.ones((length, length), dtype=bool))
    rows_prior = passed_along((x_input[length - 3 :], bc_input[:, length - 3 :]), "seq", 1)
    x_ext = jnp.concatenate([rows_prior[0], x_input], axis=0)
    bc_ext = jnp.concatenate([rows_prior[1], bc_input], axis=1)
    x_pre = conv_rows(x_ext.astype(f32), conv_x)
    bc_pre = conv_rows(bc_ext.astype(f32), convolution_bc_taps)
    x_rows = jax.nn.silu(x_pre).astype(bf16)
    bc_rows = jax.nn.silu(bc_pre).astype(bf16)
    b_rows = bc_rows[0]
    c_rows = bc_rows[1]
    gram = jnp.dot(c_rows, b_rows.T, preferred_element_type=f32)
    x_heads = x_rows.reshape(length, head_count, width)

    cumul = jnp.cumsum(decay_rate[:, None] * step_size, axis=1)
    totals = cumul[:, -1]
    trailing = jnp.exp(cumul[:, -1:] - cumul)
    tail_step = trailing * step_size
    weighted_b = (tail_step[:, :, None] * b_rows.astype(f32)[None]).astype(bf16)
    local_state = jnp.einsum("hsn,shp->hnp", weighted_b, x_heads, preferred_element_type=f32)

    state_exact, weight = scan_forward(totals, local_state)
    state_low = state_exact.astype(bf16)

    between = cumul[:, :, None] - cumul[:, None, :]
    decay = jnp.where(causal[None], jnp.exp(jnp.minimum(between, 0.0)), 0.0)
    mixer_low = (gram[None] * decay * step_size[:, None, :]).astype(bf16)
    intra = jnp.einsum("hts,shp->thp", mixer_low, x_heads, preferred_element_type=f32)
    handed = jnp.einsum("tn,hnp->thp", c_rows, state_low, preferred_element_type=f32)
    lifted = jnp.exp(cumul)
    mixed_heads = (
        intra + lifted.T[:, :, None] * handed + d_skip[None, :, None] * x_heads.astype(f32)
    )
    mixed_out = mixed_heads.reshape(length, channels)

    z_rows = z_input.astype(f32)
    gate_value = jax.nn.silu(z_rows)
    gated = mixed_out * gate_value
    scaled = grad_out.astype(f32) * rescale_factor
    sums = lax.psum(
        jnp.stack([jnp.sum(gated * gated, axis=1), jnp.sum(scaled * gated, axis=1)]), "head"
    )
    inv_rms = lax.rsqrt(sums[0] / INNER + EPS)
    normed = gated * inv_rms[:, None]
    mean_dot = inv_rms * sums[1] / INNER
    grad_gated = inv_rms[:, None] * (scaled - normed * mean_dot[:, None])
    grad_z = (grad_gated * mixed_out * silu_grad(z_rows)).astype(bf16)
    grad_mixed = (grad_gated * gate_value).astype(bf16)
    grad_heads = grad_mixed.reshape(length, head_count, width)

    lifted_c = (lifted[:, :, None] * c_rows.astype(f32)[None]).astype(bf16)
    state_grad = jnp.einsum("htn,thp->hnp", lifted_c, grad_heads, preferred_element_type=f32)
    out_exact = scan_backward(weight, state_grad)
    out_low = out_exact.astype(bf16)

    grad_mix = jnp.einsum("thp,shp->hts", grad_heads, x_heads, preferred_element_type=f32)
    decayed = grad_mix * decay
    zterm = decayed * step_size[:, None, :]
    gram_grad = zterm * gram[None]
    reached = jnp.einsum("shp,hnp->hsn", x_heads, out_low, preferred_element_type=f32)
    inner_b = jnp.sum(b_rows.astype(f32)[None] * reached, axis=2)
    state_term = tail_step * inner_b
    grad_cumul = jnp.sum(gram_grad, axis=2) - jnp.sum(gram_grad, axis=1)
    carried_dot = jnp.sum(grad_heads.astype(f32) * handed, axis=2).T
    grad_cumul = grad_cumul + lifted * carried_dot - state_term
    end_grad = jnp.sum(state_term, axis=1) + jnp.exp(totals) * jnp.sum(
        out_exact * state_exact, axis=(1, 2)
    )
    grad_cumul = grad_cumul.at[:, -1].add(end_grad)
    grad_log = jnp.cumsum(grad_cumul[:, ::-1], axis=1)[:, ::-1]
    grad_steps = (
        jnp.sum(decayed * gram[None], axis=1)
        + trailing * inner_b
        + decay_rate[:, None] * grad_log
    )
    grad_x_heads = jnp.einsum("hts,thp->shp", mixer_low, grad_heads, preferred_element_type=f32)
    grad_x_heads = (
        grad_x_heads
        + d_skip[None, :, None] * grad_heads.astype(f32)
        + jnp.einsum("hsn,hnp->shp", weighted_b, out_low, preferred_element_type=f32)
    )
    grad_c_heads = lifted[:, :, None] * jnp.einsum(
        "thp,hnp->htn", grad_heads, state_low, preferred_element_type=f32
    )
    grad_b_heads = tail_step[:, :, None] * reached
    grad_sum = jnp.sum(zterm, axis=0)
    grad_c = jnp.sum(grad_c_heads, axis=0) + jnp.dot(grad_sum, b_rows.astype(f32), precision=HIGH)
    grad_b = jnp.sum(grad_b_heads, axis=0) + jnp.dot(
        grad_sum.T, c_rows.astype(f32), precision=HIGH
    )
    grad_bc_rows = jnp.stack([grad_b, grad_c])
    grad_x_rows = grad_x_heads.reshape(length, channels)

    grad_x_pre = grad_x_rows * silu_grad(x_pre)
    row_share = length // lax.axis_size("head")
    first_row = lax.axis_index("head") * row_share
    grad_bc_all = lax.psum(grad_bc_rows, "head")
    grad_bc_pre = grad_bc_all * silu_grad(bc_pre)
    rows_next = passed_along((grad_x_pre[:3], grad_bc_pre[:, :3]), "seq", -1)
    grad_x = conv_back(jnp.concatenate([grad_x_pre, rows_next[0]], axis=0), conv_x).astype(bf16)
    grad_bc_full = conv_back(
        jnp.concatenate([grad_bc_pre, rows_next[1]], axis=1), convolution_bc_taps
    )
    grad_bc = lax.dynamic_slice_in_dim(grad_bc_full, first_row, row_share, 1).astype(bf16)
    grad_dt = grad_steps * jax.nn.sigmoid(dt_raw + dt_bias[:, None])
    return (grad_x, grad_z, grad_bc, grad_dt)


def solution(mesh):
    return jax.shard_map(
        shards,
        mesh=mesh,
        in_specs=(
            P("seq", "head"),
            P("seq", "head"),
            P(None, "seq", None),
            P("head", "seq"),
            P("head"),
            P("head"),
            P("head"),
            P(None, "head"),
            P(),
            P("head"),
            P("seq", "head"),
        ),
        out_specs=(
            P("seq", "head"),
            P("seq", "head"),
            P(None, ("seq", "head"), None),
            P("head", "seq"),
        ),
        check_vma=False,
    )
```

time: 700 us -> 289 us (0.41)
  waiting for transfers between devices: 373 us -> 154 us
  other arithmetic: 78.7 us -> 12.2 us
  blocking collectives: 108 us -> 51.9 us
  local copies, waits for them, and re-layouts: 50 us -> 14.1 us
  matrix products: 40.3 us -> 6.93 us
  starting transfers between devices: 9.75 us -> 30.7 us
  loops' own time: 18.7 us -> 0 us
    all_gather x2 -> x0, waiting for transfers between devices: 265 us -> none  [entering(): gathered = jax.tree.map(lambda a: lax.all_gather(a, axis), part)]
    unnamed x1 -> x0, blocking collectives: 57.6 us -> none
    all_to_all x0 -> x3, waiting for transfers between devices: none -> 44.9 us  [the longest x1 17.8 us: scan_forward(): got = lax.all_to_all(sent, 'seq', 0, 0, tiled=True)]
    add x39 -> x1, other arithmetic: 37.1 us -> 0.08 us  [shards(): grad_cumul = grad_cumul.at[:, -1].add(end_grad)]
    dot_general x83 -> x13, matrix products: 40.3 us -> 6.71 us  [the longest x1 1.62 us: scan_backward(): scanned = jnp.einsum('hjk,jhx->khx', weight, data, precision=HIGH)]
    dynamic_slice x24 -> x0, local copies, waits for them, and re-layouts: 24.8 us -> none  [block_mix(): lax.map(one_head, (cumul, step_size, x_heads, state_low, skip_gain))]
    all_to_all x0 -> x3, starting transfers between devices: none -> 21.1 us  [the longest x1 8.51 us: scan_forward(): got = lax.all_to_all(sent, 'seq', 0, 0, tiled=True)]
    all_to_all x0 -> x1, blocking collectives: none -> 19 us  [scan_backward(): got = lax.all_to_all(pieces, 'seq', 0, 0, tiled=True)]
  transfers between devices with their start and end apart: 7 -> 8, of which waited for: 5 -> 6; matrix products, arithmetic and copies ran while one was open for 2% -> 3% of each run, Pallas kernels for 0% -> 0%
where the time goes in v1:
time: 289 us; the launch traced here: 285 us
  waiting for transfers between devices  154 us (53%)
  blocking collectives  51.9 us (18%)
  starting transfers between devices  30.7 us (11%)
  between operations  14.7 us (5%)
  local copies, waits for them, and re-layouts  14.1 us (5%)
  other arithmetic  12.2 us (4%)
  matrix products  6.93 us (2%)
    psum x1, waiting for transfers between devices, shards(): grad_bc_all = lax.psum(grad_bc_rows, 'head')  104 us
    psum x1, blocking collectives, shards(): lax.psum(jnp.stack([jnp.sum(gated * gated, axis=1), jnp.sum(scaled * gate...  32.9 us
    all_to_all x1, blocking collectives, scan_backward(): got = lax.all_to_all(pieces, 'seq', 0, 0, tiled=True)  19 us
    all_to_all x1, waiting for transfers between devices, scan_forward(): got = lax.all_to_all(sent, 'seq', 0, 0, tiled=True)  17.8 us
    all_to_all x1, waiting for transfers between devices, scan_forward(): lax.all_to_all(scanned.reshape(count, heads, rows, width), 'seq', 0, 0, t...  14.8 us
    all_to_all x1, waiting for transfers between devices, scan_backward(): lax.all_to_all(scanned.reshape(count, heads, rows, width), 'seq', 0, 0, t...  12.2 us
    ppermute x4, starting transfers between devices, passed_along(): return lax.ppermute(block, axis, route)  9.62 us
    all_to_all x1, starting transfers between devices, scan_forward(): got = lax.all_to_all(sent, 'seq', 0, 0, tiled=True)  8.51 us
  transfers between devices with their start and end apart: 8, of which 6 were waited for; matrix products, arithmetic and copies ran while one was open for 3% of the time, Pallas kernels for 0%

profile of v1, /device:TPU:1, one launch (start us, length us, event | category | flops | bytes accessed | tf_op | source)
XLA Modules:
  0.0 284.7 jit_solution(13604218942189415049)
XLA Ops:
  7.2 0.8 slice.161
  7.9 3.9 %collective-permute-start.1 = (bf16[2,3,128]{2,1,0:T(4,128)(2,1)S(1)}, bf16[2,3,128]{2,1,0:T(4,128)(2,1)S(1)}, u32[]{:S(2)}, u32[]{:S(2)}) collective-permute-start(bf16[2,3,128]{2,1,0:T(4,128)(2,1)S(1)} %slice.161), channel_id=1, source_target_pairs={{0,16},{16,32},{32,48},{48,64},{64,80},{80,96},{96,112},{112,128},... | collective-permute-start | bytes 4616 | tf_op jit(solution)/shard_map/ppermute | solution.py:16
  11.9 0.7 slice.152
  12.6 3.1 %collective-permute-start = (bf16[3,1024]{1,0:T(4,128)(2,1)S(1)}, bf16[3,1024]{1,0:T(4,128)(2,1)S(1)}, u32[]{:S(2)}, u32[]{:S(2)}) collective-permute-start(bf16[3,1024]{1,0:T(4,128)(2,1)S(1)} %slice.152), channel_id=1, source_target_pairs={{0,16},{16,32},{32,48},{48,64},{64,80},{80,96},{96,112},{112,128},... | collective-permute-start | bytes 18440 | tf_op jit(solution)/shard_map/ppermute | solution.py:16
  15.7 0.7 exponential_negate_fusion
  16.4 0.8 broadcast_multiply_fusion
  17.6 0.9 fusion.72
  18.6 0.6 fusion.73
  19.3 0.5 copy-done.25
  19.9 0.7 multiply_convert_fusion.10
  20.6 0.6 fusion.53
  21.7 0.3 multiply_convert_fusion.4
  22.9 0.9 select_maximum_fusion
  23.8 8.5 %all-to-all-start = ((f32[32,8,5,128]{3,1,2,0:T(8,128)}), f32[32,8,5,128]{3,1,2,0:T(8,128)S(1)}, u32[]{:S(2)}, u32[]{:S(2)}) async-start(f32[32,8,5,128]{3,1,2,0:T(8,128)} %select_maximum_fusion), calls=%async_computation | async-start | bytes 1310720 | tf_op jit(solution)/shard_map/all_to_all | solution.py:67
  32.3 17.8 %all-to-all-done = f32[32,8,5,128]{3,1,2,0:T(8,128)S(1)} async-done(((f32[32,8,5,128]{3,1,2,0:T(8,128)}), f32[32,8,5,128]{3,1,2,0:T(8,128)S(1)}, u32[]{:S(2)}, u32[]{:S(2)}) %all-to-all-start) | async-done | bytes 655392 | tf_op jit(solution)/shard_map/all_to_all | solution.py:67
  51.1 0.8 convolution_bitcast_fusion.3
  52.0 1.1 copy.76
  53.1 6.3 %all-to-all-start.1 = ((f32[32,8,4,128]{3,1,2,0:T(8,128)}), f32[32,8,4,128]{3,1,2,0:T(8,128)S(1)}, u32[]{:S(2)}, u32[]{:S(2)}) async-start(f32[32,8,4,128]{3,1,2,0:T(8,128)} %copy.76), calls=%async_computation.1 | async-start | bytes 1048576 | tf_op jit(solution)/shard_map/all_to_all | solution.py:76
  59.6 14.8 %all-to-all-done.1 = f32[32,8,4,128]{3,1,2,0:T(8,128)S(1)} async-done(((f32[32,8,4,128]{3,1,2,0:T(8,128)}), f32[32,8,4,128]{3,1,2,0:T(8,128)S(1)}, u32[]{:S(2)}, u32[]{:S(2)}) %all-to-all-start.1) | async-done | bytes 524320 | tf_op jit(solution)/shard_map/all_to_all | solution.py:76
  75.0 0.6 copy-done.39
  75.6 1.2 fusion.1
  76.8 1.3 copy.78
  78.4 32.9 %psum.14 = f32[2,128]{1,0:T(2,128)S(1)} all-reduce(f32[2,128]{1,0:T(2,128)S(1)} %pad_maximum_fusion.2), channel_id=1, replica_groups=mesh['seq'=32,'head'=16] {'head'}, use_global_device_ids=true, to_apply=%region_4.5 | all-reduce | flops 256 | bytes 2048 | tf_op jit(solution)/shard_map/psum | solution.py:151
  111.4 1.8 fusion.22
  113.4 0.7 copy-done.4
  114.0 0.6 fusion.29
  114.8 19.0 %all_to_all.20 = f32[32,8,4,128]{3,2,1,0:T(4,128)S(1)} all-to-all(f32[32,8,4,128]{3,2,1,0:T(4,128)S(1)} %bitcast.118), channel_id=1, replica_groups=mesh['seq'=32,'head'=16] {'seq'}, dimensions={0} | all-to-all | bytes 1048576 | tf_op jit(solution)/shard_map/all_to_all | solution.py:85
  133.9 1.6 convolution_bitcast_fusion.1
  135.8 1.1 copy.84
  136.9 6.2 %all-to-all-start.3 = ((f32[32,8,4,128]{3,1,2,0:T(8,128)}), f32[32,8,4,128]{3,1,2,0:T(8,128)S(1)}, u32[]{:S(2)}, u32[]{:S(2)}) async-start(f32[32,8,4,128]{3,1,2,0:T(8,128)} %copy.84), calls=%async_computation.3 | async-start | bytes 1048576 | tf_op jit(solution)/shard_map/all_to_all | solution.py:88
  143.2 0.7 copy-done.19
  143.9 0.3 fusion.4
  144.2 0.5 copy-done.7
  144.7 0.5 multiply_reduce_fusion.6
  145.5 12.2 %all-to-all-done.3 = f32[32,8,4,128]{3,1,2,0:T(8,128)S(1)} async-done(((f32[32,8,4,128]{3,1,2,0:T(8,128)}), f32[32,8,4,128]{3,1,2,0:T(8,128)S(1)}, u32[]{:S(2)}, u32[]{:S(2)}) %all-to-all-start.3) | async-done | bytes 524320 | tf_op jit(solution)/shard_map/all_to_all | solution.py:88
  159.8 0.7 pad_maximum_fusion.1
  160.5 0.6 copy-done.40
  161.1 0.4 fusion.3
  161.9 1.3 collective-permute-start.2
  163.3 0.7 divide_multiply_fusion
  164.0 2.4 collective-permute-done.2
  166.5 1.0 fusion.12
  167.4 103.8 %all-reduce.3.cloned.1.call-done = f32[2,128,128]{2,1,0:T(8,128)} async-done(((f32[2,128,128]{2,1,0:T(8,128)}), f32[2,128,128]{2,1,0:T(8,128)}) %all-reduce.3.cloned.1.call-update) | async-done | bytes 131088 | tf_op jit(solution)/shard_map/psum | solution.py:208
  271.2 1.0 multiply_multiply_fusion.1
  272.2 1.3 collective-permute-start.3
  273.5 3.0 %collective-permute-done.3 = f32[2,3,128]{2,1,0:T(4,128)S(1)} collective-permute-done((f32[2,3,128]{2,1,0:T(4,128)S(1)}, f32[2,3,128]{2,1,0:T(4,128)S(1)}, u32[]{:S(2)}, u32[]{:S(2)}) %collective-permute-start.3) | collective-permute-done | bytes 3104 | tf_op jit(solution)/shard_map/ppermute | solution.py:16
  276.6 0.6 copy-done.28
  277.2 0.6 fusion.57
  (134 shorter events, 7.5 us)
Async XLA Ops:
  7.2 12.1 %copy-start.5 = (bf16[2,128,128]{2,1,0:T(8,128)(2,1)S(1)}, bf16[2,128,128]{2,1,0:T(8,128)(2,1)}, u32[]{:S(2)}) copy-start(bf16[2,128,128]{2,1,0:T(8,128)(2,1)} %param.17) | copy-start | bytes 196612
  7.9 11.4 %collective-permute-start.1 = (bf16[2,3,128]{2,1,0:T(4,128)(2,1)S(1)}, bf16[2,3,128]{2,1,0:T(4,128)(2,1)S(1)}, u32[]{:S(2)}, u32[]{:S(2)}) collective-permute-start(bf16[2,3,128]{2,1,0:T(4,128)(2,1)S(1)} %slice.161), channel_id=1, source_target_pairs={{0,16},{16,32},{32,48},{48,64},{64,80},{80,96},{96,112},{112,128},... | collective-permute-start | bytes 4616 | tf_op jit(solution)/shard_map/ppermute | solution.py:16
  12.6 8.7 %collective-permute-start = (bf16[3,1024]{1,0:T(4,128)(2,1)S(1)}, bf16[3,1024]{1,0:T(4,128)(2,1)S(1)}, u32[]{:S(2)}, u32[]{:S(2)}) collective-permute-start(bf16[3,1024]{1,0:T(4,128)(2,1)S(1)} %slice.152), channel_id=1, source_target_pairs={{0,16},{16,32},{32,48},{48,64},{64,80},{80,96},{96,112},{112,128},... | collective-permute-start | bytes 18440 | tf_op jit(solution)/shard_map/ppermute | solution.py:16
  16.4 0.8 copy-start.37
  17.2 57.8 %copy-start.23 = (f32[8,128]{1,0:T(8,128)}, f32[8,128]{1,0:T(8,128)S(1)}, u32[]{:S(2)}) copy-start(f32[8,128]{1,0:T(8,128)S(1)} %get-tuple-element.39) | copy-start | bytes 12292
  17.6 5.2 %copy-start.33 = (f32[8]{0:T(128)}, f32[8]{0:T(128)S(1)}, u32[]{:S(2)}) copy-start(f32[8]{0:T(128)S(1)} %slice_reduce_fusion) | copy-start | bytes 100
  18.5 3.1 %copy-start.9 = (f32[1,1024]{1,0:T(1,128)}, f32[1,1024]{1,0:T(1,128)S(1)}, u32[]{:S(2)}) copy-start(f32[1,1024]{1,0:T(1,128)S(1)} %get-tuple-element.50) | copy-start | bytes 12292
  18.5 3.1 %copy-start.11 = (f32[1,1024]{1,0:T(1,128)}, f32[1,1024]{1,0:T(1,128)S(1)}, u32[]{:S(2)}) copy-start(f32[1,1024]{1,0:T(1,128)S(1)} %get-tuple-element.51) | copy-start | bytes 12292
  18.6 3.1 %copy-start.13 = (f32[1,1024]{1,0:T(1,128)}, f32[1,1024]{1,0:T(1,128)S(1)}, u32[]{:S(2)}) copy-start(f32[1,1024]{1,0:T(1,128)S(1)} %get-tuple-element.52) | copy-start | bytes 12292
  18.6 3.1 %copy-start.15 = (f32[1,1024]{1,0:T(1,128)}, f32[1,1024]{1,0:T(1,128)S(1)}, u32[]{:S(2)}) copy-start(f32[1,1024]{1,0:T(1,128)S(1)} %get-tuple-element.53) | copy-start | bytes 12292
  18.6 0.7 copy-start.35
  19.3 0.6 copy-start.25
  19.3 0.6 copy-start.27
  19.3 0.6 copy-start.31
  20.6 1.0 copy-start.3
  23.8 26.4 %all-to-all-start = ((f32[32,8,5,128]{3,1,2,0:T(8,128)}), f32[32,8,5,128]{3,1,2,0:T(8,128)S(1)}, u32[]{:S(2)}, u32[]{:S(2)}) async-start(f32[32,8,5,128]{3,1,2,0:T(8,128)} %select_maximum_fusion), calls=%async_computation | async-start | bytes 1310720 | tf_op jit(solution)/shard_map/all_to_all | solution.py:67
  32.3 18.7 %copy-start.8 = (pred[32,32]{0,1:T(8,128)(4,1)}, pred[32,32]{0,1:T(8,128)(4,1)S(1)}, u32[]{:S(2)}) copy-start(pred[32,32]{0,1:T(8,128)(4,1)S(1)} %iota_compare_fusion.2) | copy-start | bytes 3076
  53.1 21.3 %all-to-all-start.1 = ((f32[32,8,4,128]{3,1,2,0:T(8,128)}), f32[32,8,4,128]{3,1,2,0:T(8,128)S(1)}, u32[]{:S(2)}, u32[]{:S(2)}) async-start(f32[32,8,4,128]{3,1,2,0:T(8,128)} %copy.76), calls=%async_computation.1 | async-start | bytes 1048576 | tf_op jit(solution)/shard_map/all_to_all | solution.py:76
  59.5 15.5 %copy-start.21 = (pred[128,128]{1,0:T(8,128)(4,1)}, pred[128,128]{1,0:T(8,128)(4,1)S(1)}, u32[]{:S(2)}) copy-start(pred[128,128]{1,0:T(8,128)(4,1)S(1)} %iota_compare_fusion.1) | copy-start | bytes 49156
  59.6 15.4 %copy-start.6 = (f32[128,128]{1,0:T(8,128)}, f32[128,128]{1,0:T(8,128)S(1)}, u32[]{:S(2)}) copy-start(f32[128,128]{1,0:T(8,128)S(1)} %fusion.52) | copy-start | bytes 196612
  74.9 0.7 copy-start.39
  76.8 1.3 copy-start
  76.8 1.3 copy-start.1
  76.8 1.3 copy-start.17
  113.2 0.8 copy-start.4
  113.3 0.7 copy-start.18
  136.9 20.9 %all-to-all-start.3 = ((f32[32,8,4,128]{3,1,2,0:T(8,128)}), f32[32,8,4,128]{3,1,2,0:T(8,128)S(1)}, u32[]{:S(2)}, u32[]{:S(2)}) async-start(f32[32,8,4,128]{3,1,2,0:T(8,128)} %copy.84), calls=%async_computation.3 | async-start | bytes 1048576 | tf_op jit(solution)/shard_map/all_to_all | solution.py:88
  143.1 128.1 %all-reduce.3.cloned.1.call-start = ((), (), s32[]{:S(2)}) async-start(), calls=%async_computation.4 | async-start | bytes 262144 | tf_op jit(solution)/shard_map/psum | solution.py:208
  143.2 0.7 copy-start.19
  143.9 0.8 copy-start.7
  143.9 0.8 copy-start.22
  143.9 0.8 copy-start.24
  160.4 0.7 copy-start.40
  161.9 1.4 copy-start.20
  161.9 1.3 copy-start.34
  161.9 1.3 copy-start.36
  161.9 1.3 copy-start.38
  161.9 4.5 %collective-permute-start.2 = (f32[3,1024]{1,0:T(4,128)S(1)}, f32[3,1024]{1,0:T(4,128)S(1)}, u32[]{:S(2)}, u32[]{:S(2)}) collective-permute-start(f32[3,1024]{1,0:T(4,128)S(1)} %slice.197), channel_id=1, source_target_pairs={{16,0},{32,16},{48,32},{64,48},{80,64},{96,80},{112,96},{128,112},... | collective-permute-start | bytes 36872 | tf_op jit(solution)/shard_map/ppermute | solution.py:16
  163.3 3.1 %copy-start.10 = (f32[1,1024]{1,0:T(1,128)S(1)}, f32[1,1024]{1,0:T(1,128)}, u32[]{:S(2)}) copy-start(f32[1,1024]{1,0:T(1,128)} %copy-done.9) | copy-start | bytes 12292
  163.3 3.1 %copy-start.12 = (f32[1,1024]{1,0:T(1,128)S(1)}, f32[1,1024]{1,0:T(1,128)}, u32[]{:S(2)}) copy-start(f32[1,1024]{1,0:T(1,128)} %copy-done.11) | copy-start | bytes 12292
  163.3 3.1 %copy-start.14 = (f32[1,1024]{1,0:T(1,128)S(1)}, f32[1,1024]{1,0:T(1,128)}, u32[]{:S(2)}) copy-start(f32[1,1024]{1,0:T(1,128)} %copy-done.13) | copy-start | bytes 12292
  163.3 3.1 %copy-start.16 = (f32[1,1024]{1,0:T(1,128)S(1)}, f32[1,1024]{1,0:T(1,128)}, u32[]{:S(2)}) copy-start(f32[1,1024]{1,0:T(1,128)} %copy-done.15) | copy-start | bytes 12292
  164.0 107.2 %copy-start.2 = (f32[2,128,128]{2,1,0:T(8,128)S(1)}, f32[2,128,128]{2,1,0:T(8,128)}, u32[]{:S(2)}) copy-start(f32[2,128,128]{2,1,0:T(8,128)} %get-tuple-element.41) | copy-start | bytes 393220
  272.2 4.4 %collective-permute-start.3 = (f32[2,3,128]{2,1,0:T(4,128)S(1)}, f32[2,3,128]{2,1,0:T(4,128)S(1)}, u32[]{:S(2)}, u32[]{:S(2)}) collective-permute-start(f32[2,3,128]{2,1,0:T(4,128)S(1)} %slice.202), channel_id=1, source_target_pairs={{16,0},{32,16},{48,32},{64,48},{80,64},{96,80},{112,96},{128,112},... | collective-permute-start | bytes 9224 | tf_op jit(solution)/shard_map/ppermute | solution.py:16
  276.5 0.7 copy-start.28
  276.5 0.7 copy-start.30
  276.5 0.7 copy-start.32
  276.6 0.7 copy-start.26
  (1 other events, 0.6 us)
Sparse Core Ops, SparseCore 0:
  160.6 110.5 all-reduce.2

commit v2 on v1

--- a/solution.py
+++ b/solution.py
@@ -1,7 +1,69 @@
 import jax
 import jax.numpy as jnp
 from jax import lax
+from jax.experimental import pallas as pl
+from jax.experimental.pallas import tpu as pltpu
 from jax.sharding import PartitionSpec as P
+import functools
+
+MESH = pl.DeviceIdType.MESH
+AXES = ("seq", "head")
+
+
+def exchange_kernel(axis, n, in_ref, out_ref, land, send_sem, recv_sem):
+    me = lax.axis_index(axis)
+    coords = {a: lax.axis_index(a) for a in AXES}
+
+    def dev(k):
+        return tuple(k if a == axis else coords[a] for a in AXES)
+
+    barrier = pltpu.get_barrier_semaphore()
+    for i in range(1, n):
+        pl.semaphore_signal(barrier, inc=1, device_id=dev(lax.rem(me + i, n)), device_id_type=MESH)
+    pl.semaphore_wait(barrier, n - 1)
+    copies = []
+    for i in range(1, n):
+        peer = lax.rem(me + i, n)
+        copy = pltpu.make_async_remote_copy(
+            src_ref=in_ref.at[peer],
+            dst_ref=land.at[me],
+            send_sem=send_sem.at[i],
+            recv_sem=recv_sem.at[i],
+            device_id=dev(peer),
+            device_id_type=MESH,
+        )
+        copy.start()
+        copies.append(copy)
+    land[me] = in_ref[me]
+    for i in range(1, n):
+        copies[i - 1].wait_send()
+        src = lax.rem(me + (n - i), n)
+        incoming = pltpu.make_async_remote_copy(
+            src_ref=in_ref.at[src],
+            dst_ref=land.at[src],
+            send_sem=send_sem.at[i],
+            recv_sem=recv_sem.at[i],
+            device_id=dev(src),
+            device_id_type=MESH,
+        )
+        incoming.wait_recv()
+    out_ref[...] = land[...]
+
+
+def exchange(x, axis, cid):
+    n = lax.axis_size(axis)
+    return pl.pallas_call(
+        functools.partial(exchange_kernel, axis, n),
+        out_shape=jax.ShapeDtypeStruct(x.shape, x.dtype),
+        in_specs=[pl.BlockSpec(memory_space=pltpu.VMEM)],
+        out_specs=pl.BlockSpec(memory_space=pltpu.VMEM),
+        scratch_shapes=[
+            pltpu.VMEM(x.shape, x.dtype),
+            pltpu.SemaphoreType.DMA((n,)),
+            pltpu.SemaphoreType.DMA((n,)),
+        ],
+        compiler_params=pltpu.CompilerParams(collective_id=cid, has_side_effects=True),
+    )(x)
 
 INNER = 16384
 
@@ -59,34 +121,34 @@
 def scan_forward(totals, local_state):
     count = lax.axis_size("seq")
     heads, nstate, width = local_state.shape
-    pieces = to_pieces(local_state, count)
-    rows = pieces.shape[2]
-    tot_row = jnp.zeros((count, heads, 1, width), jnp.float32)
-    tot_row = tot_row.at[:, :, 0, 0].set(jnp.broadcast_to(totals, (count, heads)))
-    sent = jnp.concatenate([pieces, tot_row], axis=2)
-    got = lax.all_to_all(sent, "seq", 0, 0, tiled=True)
-    block_totals = got[:, :, rows, 0]
+    rows = nstate // count
+    pieces = to_pieces(local_state, count).reshape(count, heads * rows, width)
+    tot_row = jnp.zeros((count, 8, width), jnp.float32)
+    tot_row = tot_row.at[:, 0, :heads].set(jnp.broadcast_to(totals, (count, heads)))
+    sent = jnp.concatenate([pieces, tot_row], axis=1)
+    got = exchange(sent, "seq", 0)
+    block_totals = got[:, heads * rows, :heads]
     running = jnp.cumsum(block_totals, axis=0)
     before = running - block_totals
     later = jnp.arange(count)[:, None] > jnp.arange(count)[None, :]
     gap = before.T[:, :, None] - running.T[:, None, :]
     weight = jnp.where(later[None], jnp.exp(jnp.minimum(gap, 0.0)), 0.0)
-    data = got[:, :, :rows, :].reshape(count, heads, rows * width)
+    data = got[:, : heads * rows, :].reshape(count, heads, rows * width)
     scanned = jnp.einsum("hkj,jhx->khx", weight, data, precision=HIGH)
-    back = lax.all_to_all(scanned.reshape(count, heads, rows, width), "seq", 0, 0, tiled=True)
-    return from_pieces(back), weight
+    back = exchange(scanned.reshape(count, heads * rows, width), "seq", 1)
+    return from_pieces(back.reshape(count, heads, rows, width)), weight
 
 
 def scan_backward(weight, state_grad):
     count = lax.axis_size("seq")
     heads, nstate, width = state_grad.shape
-    pieces = to_pieces(state_grad, count)
-    rows = pieces.shape[2]
-    got = lax.all_to_all(pieces, "seq", 0, 0, tiled=True)
+    rows = nstate // count
+    pieces = to_pieces(state_grad, count).reshape(count, heads * rows, width)
+    got = exchange(pieces, "seq", 1)
     data = got.reshape(count, heads, rows * width)
     scanned = jnp.einsum("hjk,jhx->khx", weight, data, precision=HIGH)
-    back = lax.all_to_all(scanned.reshape(count, heads, rows, width), "seq", 0, 0, tiled=True)
-    return from_pieces(back)
+    back = exchange(scanned.reshape(count, heads * rows, width), "seq", 1)
+    return from_pieces(back.reshape(count, heads, rows, width))
 
 
 def shards(
@@ -148,9 +210,10 @@
     gate_value = jax.nn.silu(z_rows)
     gated = mixed_out * gate_value
     scaled = grad_out.astype(f32) * rescale_factor
-    sums = lax.psum(
-        jnp.stack([jnp.sum(gated * gated, axis=1), jnp.sum(scaled * gated, axis=1)]), "head"
-    )
+    hcount = lax.axis_size("head")
+    own_sums = jnp.stack([jnp.sum(gated * gated, axis=1), jnp.sum(scaled * gated, axis=1)])
+    own_sums = jnp.concatenate([own_sums, jnp.zeros((6, length), f32)], axis=0)
+    sums = jnp.sum(exchange(jnp.broadcast_to(own_sums, (hcount,) + own_sums.shape), "head", 3), axis=0)
     inv_rms = lax.rsqrt(sums[0] / INNER + EPS)
     normed = gated * inv_rms[:, None]
     mean_dot = inv_rms * sums[1] / INNER
@@ -203,16 +266,23 @@
     grad_x_rows = grad_x_heads.reshape(length, channels)
 
     grad_x_pre = grad_x_rows * silu_grad(x_pre)
-    row_share = length // lax.axis_size("head")
+    hcount = lax.axis_size("head")
+    row_share = length // hcount
     first_row = lax.axis_index("head") * row_share
-    grad_bc_all = lax.psum(grad_bc_rows, "head")
-    grad_bc_pre = grad_bc_all * silu_grad(bc_pre)
-    rows_next = passed_along((grad_x_pre[:3], grad_bc_pre[:, :3]), "seq", -1)
-    grad_x = conv_back(jnp.concatenate([grad_x_pre, rows_next[0]], axis=0), conv_x).astype(bf16)
-    grad_bc_full = conv_back(
-        jnp.concatenate([grad_bc_pre, rows_next[1]], axis=1), convolution_bc_taps
-    )
-    grad_bc = lax.dynamic_slice_in_dim(grad_bc_full, first_row, row_share, 1).astype(bf16)
+    bc_pieces = jnp.moveaxis(grad_bc_rows.reshape(2, hcount, row_share, -1), 1, 0)
+    bc_got = exchange(bc_pieces.reshape(hcount, 2 * row_share, -1), "head", 2)
+    grad_bc_mine = jnp.sum(bc_got, axis=0).reshape(2, row_share, -1)
+    bc_pre_mine = lax.dynamic_slice_in_dim(bc_pre, first_row, row_share, 1)
+    grad_bc_pre = grad_bc_mine * silu_grad(bc_pre_mine)
+    total_dev = lax.axis_size("seq") * hcount
+    rim_bc = lax.ppermute(
+        grad_bc_pre[:, :3], ("seq", "head"), [(i + 1, i) for i in range(total_dev - 1)]
+    )
+    rim_x = passed_along(grad_x_pre[:3], "seq", -1)
+    grad_x = conv_back(jnp.concatenate([grad_x_pre, rim_x], axis=0), conv_x).astype(bf16)
+    grad_bc = conv_back(
+        jnp.concatenate([grad_bc_pre, rim_bc], axis=1), convolution_bc_taps
+    ).astype(bf16)
     grad_dt = grad_steps * jax.nn.sigmoid(dt_raw + dt_bias[:, None])
     return (grad_x, grad_z, grad_bc, grad_dt)
 

time: 289 us -> 175 us (0.61)
  the two profiles are of different devices: /device:TPU:1 before, /device:TPU:56 now
where the time goes in v2:
time: 175 us; the launch traced here: 174 us
  Pallas kernels  118 us (67%)
  starting transfers between devices  17.8 us (10%)
  local copies, waits for them, and re-layouts  14.8 us (8%)
  other arithmetic  14 us (8%)
  matrix products  5.72 us (3%)
  waiting for transfers between devices  1.91 us (1%)
    pallas_call x6, Pallas kernels, exchange(): pl.pallas_call(functools.partial(exchange_kernel, axis, n), out_shape=jax...  118 us
    ppermute x3, starting transfers between devices, passed_along(): return lax.ppermute(block, axis, route)  9.08 us
    ppermute x1, starting transfers between devices, shards(): lax.ppermute(grad_bc_pre[:, :3], ('seq', 'head'), [(i + 1, i) for i in ra...  8.77 us
    unnamed x92, local copies, waits for them, and re-layouts  4.17 us
  transfers between devices with their start and end apart: 4, of which 1 were waited for; matrix products, arithmetic and copies ran while one was open for 3% of the time, Pallas kernels for 0%

profile of v2, /device:TPU:56, one launch (start us, length us, event | category | flops | bytes accessed | tf_op | source)
XLA Modules:
  0.0 174.0 jit_solution(4909198416601447772)
XLA Ops:
  0.6 0.7 slice.158
  1.3 3.4 %collective-permute-start.1 = (bf16[2,3,128]{2,1,0:T(4,128)(2,1)S(1)}, bf16[2,3,128]{2,1,0:T(4,128)(2,1)S(1)}, u32[]{:S(2)}, u32[]{:S(2)}) collective-permute-start(bf16[2,3,128]{2,1,0:T(4,128)(2,1)S(1)} %slice.158), channel_id=1, source_target_pairs={{0,16},{16,32},{32,48},{48,64},{64,80},{80,96},{96,112},{112,128},... | collective-permute-start | bytes 4616 | tf_op jit(solution)/shard_map/ppermute | solution.py:78
  4.7 0.7 slice.149
  5.5 3.4 %collective-permute-start = (bf16[3,1024]{1,0:T(4,128)(2,1)S(1)}, bf16[3,1024]{1,0:T(4,128)(2,1)S(1)}, u32[]{:S(2)}, u32[]{:S(2)}) collective-permute-start(bf16[3,1024]{1,0:T(4,128)(2,1)S(1)} %slice.149), channel_id=1, source_target_pairs={{0,16},{16,32},{32,48},{48,64},{64,80},{80,96},{96,112},{112,128},... | collective-permute-start | bytes 18440 | tf_op jit(solution)/shard_map/ppermute | solution.py:78
  9.0 0.6 copy-done.21
  9.6 0.5 copy-done.41
  10.8 0.6 fusion.73
  11.6 0.7 multiply_convert_fusion.10
  12.3 0.6 fusion.51
  13.4 0.3 multiply_convert_fusion.4
  14.4 0.9 pad_maximum_fusion.in_ref
  15.3 24.7 %shard_map.138 = f32[32,40,128]{2,1,0:T(8,128)} custom-call(f32[32,40,128]{2,1,0:T(8,128)} %pad_maximum_fusion.in_ref), custom_call_target="tpu_custom_call" | custom-call | tf_op jit(solution)/shard_map/pallas_call | solution.py:55
  39.9 0.9 slice.170
  41.1 0.8 slice-done
  42.0 1.0 convolution_bitcast_fusion.3
  43.3 0.8 reshape.197.in_ref
  44.2 19.3 %shard_map.139 = f32[32,32,128]{2,1,0:T(8,128)} custom-call(f32[32,32,128]{2,1,0:T(8,128)} %reshape.197.in_ref), custom_call_target="tpu_custom_call" | custom-call | tf_op jit(solution)/shard_map/pallas_call | solution.py:55
  63.5 1.1 convert_element_type.86
  65.2 0.6 copy-done.44
  65.8 0.4 fusion.1
  66.4 0.7 copy-done.1
  67.6 0.6 broadcast_in_dim.25.in_ref
  68.2 16.6 %shard_map.140 = f32[16,8,128]{2,1,0:T(8,128)} custom-call(f32[16,8,128]{2,1,0:T(8,128)} %broadcast_in_dim.25.in_ref), custom_call_target="tpu_custom_call" | custom-call | tf_op jit(solution)/shard_map/pallas_call | solution.py:55
  84.9 0.9 reduce_sum.139
  85.8 1.1 fusion.22
  87.1 0.7 copy-done.7
  87.9 0.5 multiply_reduce_fusion.6
  88.6 0.3 fusion.4
  88.9 0.5 copy-done.4
  89.4 0.6 fusion.30
  90.0 0.9 copy.92
  90.9 23.8 %shard_map.141 = f32[32,32,128]{2,1,0:T(8,128)} custom-call(f32[32,32,128]{2,1,0:T(8,128)} %bitcast.125), custom_call_target="tpu_custom_call" | custom-call | tf_op jit(solution)/shard_map/pallas_call | solution.py:55
  114.7 1.1 reshape.202
  115.9 0.9 convolution_bitcast_fusion.1
  117.2 0.8 reshape.203.in_ref
  118.0 22.3 %shard_map.142 = f32[32,32,128]{2,1,0:T(8,128)} custom-call(f32[32,32,128]{2,1,0:T(8,128)} %reshape.203.in_ref), custom_call_target="tpu_custom_call" | custom-call | tf_op jit(solution)/shard_map/pallas_call | solution.py:55
  140.3 1.4 multiply_reduce_fusion
  144.0 0.7 maximum_bitcast_fusion.in_ref
  144.6 11.5 %shard_map.143 = f32[16,16,128]{2,1,0:T(8,128)} custom-call(f32[16,16,128]{2,1,0:T(8,128)} %maximum_bitcast_fusion.in_ref), custom_call_target="tpu_custom_call" | custom-call | tf_op jit(solution)/shard_map/pallas_call | solution.py:55
  156.1 0.9 reduce_sum.143
  157.0 0.7 bitcast_multiply_fusion
  157.8 8.8 %collective-permute-start.3 = (f32[2,3,128]{2,1,0:T(4,128)S(1)}, f32[2,3,128]{2,1,0:T(4,128)S(1)}, u32[]{:S(2)}, u32[]{:S(2)}) collective-permute-start(f32[2,3,128]{2,1,0:T(4,128)S(1)} %slice.197), channel_id=1, source_target_pairs={{1,0},{2,1},{3,2},{4,3},{5,4},{6,5},{7,6},{8,7},{9,8},{10,9},{11,1... | collective-permute-start | bytes 9224 | tf_op jit(solution)/shard_map/ppermute | solution.py:278
  166.5 0.4 fusion.3
  167.4 2.3 %collective-permute-start.2 = (f32[3,1024]{1,0:T(4,128)S(1)}, f32[3,1024]{1,0:T(4,128)S(1)}, u32[]{:S(2)}, u32[]{:S(2)}) collective-permute-start(f32[3,1024]{1,0:T(4,128)S(1)} %slice.192), channel_id=1, source_target_pairs={{16,0},{32,16},{48,32},{64,48},{80,64},{96,80},{112,96},{128,112},... | collective-permute-start | bytes 36872 | tf_op jit(solution)/shard_map/ppermute | solution.py:78
  169.8 0.7 divide_multiply_fusion
  170.5 0.6 fusion.58
  171.1 1.9 %collective-permute-done.2 = f32[3,1024]{1,0:T(4,128)S(1)} collective-permute-done((f32[3,1024]{1,0:T(4,128)S(1)}, f32[3,1024]{1,0:T(4,128)S(1)}, u32[]{:S(2)}, u32[]{:S(2)}) %collective-permute-start.2) | collective-permute-done | bytes 12320 | tf_op jit(solution)/shard_map/ppermute | solution.py:78
  173.1 1.0 fusion.12
  (146 shorter events, 7.0 us)
Async XLA Ops:
  1.3 10.2 %collective-permute-start.1 = (bf16[2,3,128]{2,1,0:T(4,128)(2,1)S(1)}, bf16[2,3,128]{2,1,0:T(4,128)(2,1)S(1)}, u32[]{:S(2)}, u32[]{:S(2)}) collective-permute-start(bf16[2,3,128]{2,1,0:T(4,128)(2,1)S(1)} %slice.158), channel_id=1, source_target_pairs={{0,16},{16,32},{32,48},{48,64},{64,80},{80,96},{96,112},{112,128},... | collective-permute-start | bytes 4616 | tf_op jit(solution)/shard_map/ppermute | solution.py:78
  4.7 4.3 %copy-start.39 = (f32[8]{0:T(128)S(1)}, f32[8]{0:T(128)}, u32[]{:S(2)}) copy-start(f32[8]{0:T(128)} %param.19) | copy-start | bytes 100
  5.5 3.5 %copy-start.43 = (f32[8]{0:T(128)S(1)}, f32[8]{0:T(128)}, u32[]{:S(2)}) copy-start(f32[8]{0:T(128)} %param.20) | copy-start | bytes 100
  5.5 7.7 %collective-permute-start = (bf16[3,1024]{1,0:T(4,128)(2,1)S(1)}, bf16[3,1024]{1,0:T(4,128)(2,1)S(1)}, u32[]{:S(2)}, u32[]{:S(2)}) collective-permute-start(bf16[3,1024]{1,0:T(4,128)(2,1)S(1)} %slice.149), channel_id=1, source_target_pairs={{0,16},{16,32},{32,48},{48,64},{64,80},{80,96},{96,112},{112,128},... | collective-permute-start | bytes 18440 | tf_op jit(solution)/shard_map/ppermute | solution.py:78
  8.9 0.7 copy-start.21
  8.9 1.7 copy-start.38
  8.9 1.7 %copy-start.23 = (f32[4,1024]{1,0:T(4,128)S(1)}, f32[4,1024]{1,0:T(4,128)}, u32[]{:S(2)}) copy-start(f32[4,1024]{1,0:T(4,128)} %param.22) | copy-start | bytes 49156
  8.9 56.2 %copy-start.24 = (pred[128,128]{1,0:T(8,128)(4,1)}, pred[128,128]{1,0:T(8,128)(4,1)S(1)}, u32[]{:S(2)}) copy-start(pred[128,128]{1,0:T(8,128)(4,1)S(1)} %iota_compare_fusion) | copy-start | bytes 49156
  9.0 2.5 %copy-start.5 = (bf16[2,128,128]{2,1,0:T(8,128)(2,1)S(1)}, bf16[2,128,128]{2,1,0:T(8,128)(2,1)}, u32[]{:S(2)}) copy-start(bf16[2,128,128]{2,1,0:T(8,128)(2,1)} %param.17) | copy-start | bytes 196612
  10.2 55.0 %copy-start.26 = (f32[8,128]{1,0:T(8,128)}, f32[8,128]{1,0:T(8,128)S(1)}, u32[]{:S(2)}) copy-start(f32[8,128]{1,0:T(8,128)S(1)} %get-tuple-element.39) | copy-start | bytes 12292
  10.6 0.8 copy-start.36
  10.7 0.9 copy-start.28
  10.7 0.9 copy-start.30
  10.7 0.9 copy-start.32
  10.7 0.9 copy-start.34
  10.7 2.6 %copy-start.10 = (f32[1,1024]{1,0:T(1,128)}, f32[1,1024]{1,0:T(1,128)S(1)}, u32[]{:S(2)}) copy-start(f32[1,1024]{1,0:T(1,128)S(1)} %get-tuple-element.48) | copy-start | bytes 12292
  10.7 2.6 %copy-start.12 = (f32[1,1024]{1,0:T(1,128)}, f32[1,1024]{1,0:T(1,128)S(1)}, u32[]{:S(2)}) copy-start(f32[1,1024]{1,0:T(1,128)S(1)} %get-tuple-element.49) | copy-start | bytes 12292
  10.7 2.6 %copy-start.14 = (f32[1,1024]{1,0:T(1,128)}, f32[1,1024]{1,0:T(1,128)S(1)}, u32[]{:S(2)}) copy-start(f32[1,1024]{1,0:T(1,128)S(1)} %get-tuple-element.50) | copy-start | bytes 12292
  10.7 2.6 %copy-start.16 = (f32[1,1024]{1,0:T(1,128)}, f32[1,1024]{1,0:T(1,128)S(1)}, u32[]{:S(2)}) copy-start(f32[1,1024]{1,0:T(1,128)S(1)} %get-tuple-element.51) | copy-start | bytes 12292
  11.4 30.6 %copy-start.8 = (pred[32,32]{0,1:T(8,128)(4,1)}, pred[32,32]{0,1:T(8,128)(4,1)S(1)}, u32[]{:S(2)}) copy-start(pred[32,32]{0,1:T(8,128)(4,1)S(1)} %iota_compare_fusion.1) | copy-start | bytes 3076
  12.3 1.0 copy-start.3
  13.1 52.1 %copy-start.6 = (f32[128,128]{1,0:T(8,128)}, f32[128,128]{1,0:T(8,128)S(1)}, u32[]{:S(2)}) copy-start(f32[128,128]{1,0:T(8,128)S(1)} %fusion.50) | copy-start | bytes 196612
  40.9 1.0 slice-start
  66.2 1.0 copy-start.1
  66.2 1.0 copy-start.2
  66.2 1.0 copy-start.18
  84.9 0.9 copy-start.19
  87.0 0.8 copy-start.7
  87.1 0.8 copy-start.25
  87.1 0.8 copy-start.27
  88.6 0.8 copy-start.4
  114.7 1.2 copy-start.9
  118.0 22.3 %copy-start = (f32[32,32,128]{2,1,0:T(8,128)S(1)}, f32[32,32,128]{2,1,0:T(8,128)}, u32[]{:S(2)}) copy-start(f32[32,32,128]{2,1,0:T(8,128)} %shard_map.139) | copy-start | bytes 1572868
  157.7 8.8 %copy-start.45 = (f32[8]{0:T(128)S(1)}, f32[8]{0:T(128)}, u32[]{:S(2)}) copy-start(f32[8]{0:T(128)} %param.21) | copy-start | bytes 100
  157.8 12.7 %collective-permute-start.3 = (f32[2,3,128]{2,1,0:T(4,128)S(1)}, f32[2,3,128]{2,1,0:T(4,128)S(1)}, u32[]{:S(2)}, u32[]{:S(2)}) collective-permute-start(f32[2,3,128]{2,1,0:T(4,128)S(1)} %slice.197), channel_id=1, source_target_pairs={{1,0},{2,1},{3,2},{4,3},{5,4},{6,5},{7,6},{8,7},{9,8},{10,9},{11,1... | collective-permute-start | bytes 9224 | tf_op jit(solution)/shard_map/ppermute | solution.py:278
  167.3 2.4 %copy-start.22 = (f32[8,128]{1,0:T(8,128)S(1)}, f32[8,128]{1,0:T(8,128)}, u32[]{:S(2)}) copy-start(f32[8,128]{1,0:T(8,128)} %param.18) | copy-start | bytes 12292
  167.4 2.3 %copy-start.37 = (f32[8]{0:T(128)S(1)}, f32[8]{0:T(128)}, u32[]{:S(2)}) copy-start(f32[8]{0:T(128)} %copy-done.36) | copy-start | bytes 100
  167.4 2.3 %copy-start.40 = (f32[8]{0:T(128)S(1)}, f32[8]{0:T(128)}, u32[]{:S(2)}) copy-start(f32[8]{0:T(128)} %param.19) | copy-start | bytes 100
  167.4 2.3 %copy-start.42 = (f32[8]{0:T(128)S(1)}, f32[8]{0:T(128)}, u32[]{:S(2)}) copy-start(f32[8]{0:T(128)} %copy-done.41) | copy-start | bytes 100
  167.4 5.6 %collective-permute-start.2 = (f32[3,1024]{1,0:T(4,128)S(1)}, f32[3,1024]{1,0:T(4,128)S(1)}, u32[]{:S(2)}, u32[]{:S(2)}) collective-permute-start(f32[3,1024]{1,0:T(4,128)S(1)} %slice.192), channel_id=1, source_target_pairs={{16,0},{32,16},{48,32},{64,48},{80,64},{96,80},{112,96},{128,112},... | collective-permute-start | bytes 36872 | tf_op jit(solution)/shard_map/ppermute | solution.py:78
  169.7 0.7 copy-start.29
  169.7 0.7 copy-start.31
  169.8 0.7 copy-start.33
  169.8 0.7 copy-start.35
  170.5 2.6 %copy-start.11 = (f32[1,1024]{1,0:T(1,128)S(1)}, f32[1,1024]{1,0:T(1,128)}, u32[]{:S(2)}) copy-start(f32[1,1024]{1,0:T(1,128)} %copy-done.10) | copy-start | bytes 12292
  170.5 2.6 %copy-start.13 = (f32[1,1024]{1,0:T(1,128)S(1)}, f32[1,1024]{1,0:T(1,128)}, u32[]{:S(2)}) copy-start(f32[1,1024]{1,0:T(1,128)} %copy-done.12) | copy-start | bytes 12292
  170.5 2.6 %copy-start.15 = (f32[1,1024]{1,0:T(1,128)S(1)}, f32[1,1024]{1,0:T(1,128)}, u32[]{:S(2)}) copy-start(f32[1,1024]{1,0:T(1,128)} %copy-done.14) | copy-start | bytes 12292
  170.5 2.6 %copy-start.17 = (f32[1,1024]{1,0:T(1,128)S(1)}, f32[1,1024]{1,0:T(1,128)}, u32[]{:S(2)}) copy-start(f32[1,1024]{1,0:T(1,128)} %copy-done.16) | copy-start | bytes 12292
  (3 other events, 1.9 us)

commit v3 on v2

--- a/solution.py
+++ b/solution.py
@@ -173,9 +173,15 @@
     decay_rate = -jnp.exp(a_log)
     step_size = jax.nn.softplus(dt_raw + dt_bias[:, None])
     causal = jnp.tril(jnp.ones((length, length), dtype=bool))
-    rows_prior = passed_along((x_input[length - 3 :], bc_input[:, length - 3 :]), "seq", 1)
-    x_ext = jnp.concatenate([rows_prior[0], x_input], axis=0)
-    bc_ext = jnp.concatenate([rows_prior[1], bc_input], axis=1)
+    nstate = bc_input.shape[2]
+    rows_last = jnp.concatenate(
+        [x_input[length - 3 :], jnp.moveaxis(bc_input[:, length - 3 :], 0, 1).reshape(3, 2 * nstate)],
+        axis=1,
+    )
+    rows_prior = passed_along(rows_last, "seq", 1)
+    x_ext = jnp.concatenate([rows_prior[:, :channels], x_input], axis=0)
+    bc_prior = jnp.moveaxis(rows_prior[:, channels:].reshape(3, 2, nstate), 0, 1)
+    bc_ext = jnp.concatenate([bc_prior, bc_input], axis=1)
     x_pre = conv_rows(x_ext.astype(f32), conv_x)
     bc_pre = conv_rows(bc_ext.astype(f32), convolution_bc_taps)
     x_rows = jax.nn.silu(x_pre).astype(bf16)
@@ -268,21 +274,35 @@
     grad_x_pre = grad_x_rows * silu_grad(x_pre)
     hcount = lax.axis_size("head")
     row_share = length // hcount
-    first_row = lax.axis_index("head") * row_share
-    bc_pieces = jnp.moveaxis(grad_bc_rows.reshape(2, hcount, row_share, -1), 1, 0)
-    bc_got = exchange(bc_pieces.reshape(hcount, 2 * row_share, -1), "head", 2)
-    grad_bc_mine = jnp.sum(bc_got, axis=0).reshape(2, row_share, -1)
-    bc_pre_mine = lax.dynamic_slice_in_dim(bc_pre, first_row, row_share, 1)
-    grad_bc_pre = grad_bc_mine * silu_grad(bc_pre_mine)
-    total_dev = lax.axis_size("seq") * hcount
-    rim_bc = lax.ppermute(
-        grad_bc_pre[:, :3], ("seq", "head"), [(i + 1, i) for i in range(total_dev - 1)]
-    )
-    rim_x = passed_along(grad_x_pre[:3], "seq", -1)
+    hidx = lax.axis_index("head")
+    first_row = hidx * row_share
+    picks = []
+    for h in range(hcount):
+        own = [h * row_share + i for i in range(row_share + 3)]
+        own = [r if r < length else 0 for r in own]
+        picks.append(own + [0, 1, 2] + [0] * (16 - row_share - 6))
+    picks = jnp.array(picks, jnp.int32)
+    piece_rows = picks.shape[1]
+    bc_pieces = jnp.moveaxis(jnp.take(grad_bc_rows, picks.reshape(-1), axis=1).reshape(2, hcount, piece_rows, -1), 1, 0)
+    bc_got = exchange(bc_pieces.reshape(hcount, 2 * piece_rows, -1), "head", 2)
+    grad_bc_mine = jnp.sum(bc_got, axis=0).reshape(2, piece_rows, -1)
+    bc_pre_pad = jnp.concatenate([bc_pre, jnp.zeros((2, 3, nstate), f32)], axis=1)
+    bc_pre_mine = lax.dynamic_slice_in_dim(bc_pre_pad, first_row, row_share + 3, 1)
+    grad_bc_pre = grad_bc_mine[:, : row_share + 3] * silu_grad(bc_pre_mine)
+    grad_bc_top = grad_bc_mine[:, row_share + 3 : row_share + 6] * silu_grad(bc_pre[:, :3])
+    rows_first = jnp.concatenate(
+        [grad_x_pre[:3], jnp.moveaxis(grad_bc_top, 0, 1).reshape(3, 2 * nstate)], axis=1
+    )
+    rows_next = passed_along(rows_first, "seq", -1)
+    rim_x = rows_next[:, :channels]
+    rim_bc = jnp.moveaxis(rows_next[:, channels:].reshape(3, 2, nstate), 0, 1)
+    grad_bc_ext = jnp.where(
+        hidx == hcount - 1,
+        jnp.concatenate([grad_bc_pre[:, :row_share], rim_bc], axis=1),
+        grad_bc_pre,
+    )
     grad_x = conv_back(jnp.concatenate([grad_x_pre, rim_x], axis=0), conv_x).astype(bf16)
-    grad_bc = conv_back(
-        jnp.concatenate([grad_bc_pre, rim_bc], axis=1), convolution_bc_taps
-    ).astype(bf16)
+    grad_bc = conv_back(grad_bc_ext, convolution_bc_taps).astype(bf16)
     grad_dt = grad_steps * jax.nn.sigmoid(dt_raw + dt_bias[:, None])
     return (grad_x, grad_z, grad_bc, grad_dt)
 

time: 175 us -> 173 us (0.989)
  the two profiles are of different devices: /device:TPU:56 before, /device:TPU:1 now
where the time goes in v3:
time: 173 us; the launch traced here: 170 us
  Pallas kernels  126 us (73%)
  local copies, waits for them, and re-layouts  16.3 us (9%)
  other arithmetic  11.7 us (7%)
  matrix products  6.55 us (4%)
  starting transfers between devices  5.24 us (3%)
  waiting for transfers between devices  2.57 us (1%)
    pallas_call x6, Pallas kernels, exchange(): pl.pallas_call(functools.partial(exchange_kernel, axis, n), out_shape=jax...  126 us
    ppermute x2, starting transfers between devices, passed_along(): return lax.ppermute(block, axis, route)  5.24 us
  transfers between devices with their start and end apart: 2, of which 1 were waited for; matrix products, arithmetic and copies ran while one was open for 1% of the time, Pallas kernels for 0%

profile of v3, /device:TPU:1, one launch (start us, length us, event | category | flops | bytes accessed | tf_op | source)
XLA Modules:
  0.0 169.6 jit_solution(1841432479164312659)
XLA Ops:
  0.6 0.7 slice.173
  1.4 0.7 slice_bitcast_fusion.9
  2.1 3.9 %collective-permute-start = (bf16[3,1280]{1,0:T(4,128)(2,1)S(1)}, bf16[3,1280]{1,0:T(4,128)(2,1)S(1)}, u32[]{:S(2)}, u32[]{:S(2)}) collective-permute-start(bf16[3,1280]{1,0:T(4,128)(2,1)S(1)} %pad_maximum_fusion.4), channel_id=1, source_target_pairs={{0,16},{16,32},{32,48},{48,64},{64,80},{80,96},{96,112},{112,128},... | collective-permute-start | bytes 23048 | tf_op jit(solution)/shard_map/ppermute | solution.py:78
  6.1 0.6 copy-done.12
  6.8 0.3 reduce_window_sum.28
  7.4 0.6 copy-done.11
  8.4 0.8 copy-done.3
  9.3 0.3 multiply_convert_fusion.4
  9.8 0.3 fusion.29
  10.3 0.9 pad_maximum_fusion.in_ref
  11.2 25.6 %shard_map.147 = f32[32,40,128]{2,1,0:T(8,128)} custom-call(f32[32,40,128]{2,1,0:T(8,128)} %pad_maximum_fusion.in_ref), custom_call_target="tpu_custom_call" | custom-call | tf_op jit(solution)/shard_map/pallas_call | solution.py:55
  36.8 0.9 slice.196
  38.0 0.7 slice-done
  38.8 1.0 convolution_bitcast_fusion.3
  39.8 0.3 copy.85
  40.1 0.8 reshape.246.in_ref
  41.0 20.6 %shard_map.148 = f32[32,32,128]{2,1,0:T(8,128)} custom-call(f32[32,32,128]{2,1,0:T(8,128)} %reshape.246.in_ref), custom_call_target="tpu_custom_call" | custom-call | tf_op jit(solution)/shard_map/pallas_call | solution.py:55
  61.6 1.1 convert_element_type.86
  63.2 0.6 copy-done.13
  63.9 1.2 fusion.1
  65.1 1.3 copy.88
  66.4 0.3 multiply_reduce_fusion.5
  66.8 0.6 broadcast_in_dim.36.in_ref
  67.4 19.7 %shard_map.149 = f32[16,8,128]{2,1,0:T(8,128)} custom-call(f32[16,8,128]{2,1,0:T(8,128)} %broadcast_in_dim.36.in_ref), custom_call_target="tpu_custom_call" | custom-call | tf_op jit(solution)/shard_map/pallas_call | solution.py:55
  87.2 0.9 reduce_sum.139
  88.1 1.1 fusion.22
  89.4 0.5 multiply_reduce_fusion.6
  89.9 0.3 fusion.4
  90.3 0.6 fusion.30
  90.8 1.0 copy.92
  91.8 21.2 %shard_map.150 = f32[32,32,128]{2,1,0:T(8,128)} custom-call(f32[32,32,128]{2,1,0:T(8,128)} %bitcast.138), custom_call_target="tpu_custom_call" | custom-call | tf_op jit(solution)/shard_map/pallas_call | solution.py:55
  113.0 1.1 reshape.251
  114.2 0.9 convolution_bitcast_fusion.1
  115.1 0.3 copy.94
  115.4 0.9 reshape.252.in_ref
  116.3 20.9 %shard_map.151 = f32[32,32,128]{2,1,0:T(8,128)} custom-call(f32[32,32,128]{2,1,0:T(8,128)} %reshape.252.in_ref), custom_call_target="tpu_custom_call" | custom-call | tf_op jit(solution)/shard_map/pallas_call | solution.py:55
  137.2 1.4 multiply_reduce_fusion
  141.2 1.0 gather_fusion
  142.1 0.7 copy.105
  142.9 18.0 %shard_map.152 = f32[16,32,128]{2,1,0:T(8,128)} custom-call(f32[16,32,128]{2,1,0:T(8,128)} %bitcast.152), custom_call_target="tpu_custom_call" | custom-call | tf_op jit(solution)/shard_map/pallas_call | solution.py:55
  160.9 1.0 reduce_sum.143
  161.9 0.4 fusion.3
  162.7 1.3 collective-permute-start.1
  164.0 0.7 divide_multiply_fusion
  164.7 2.6 %collective-permute-done.1 = f32[3,1280]{1,0:T(4,128)S(1)} collective-permute-done((f32[3,1280]{1,0:T(4,128)S(1)}, f32[3,1280]{1,0:T(4,128)S(1)}, u32[]{:S(2)}, u32[]{:S(2)}) %collective-permute-start.1) | collective-permute-done | bytes 15392 | tf_op jit(solution)/shard_map/ppermute | solution.py:78
  167.3 0.7 maximum_select_fusion
  168.0 0.6 fusion.54
  168.6 0.9 fusion.12
  (91 shorter events, 5.4 us)
Async XLA Ops:
  2.1 6.1 %collective-permute-start = (bf16[3,1280]{1,0:T(4,128)(2,1)S(1)}, bf16[3,1280]{1,0:T(4,128)(2,1)S(1)}, u32[]{:S(2)}, u32[]{:S(2)}) collective-permute-start(bf16[3,1280]{1,0:T(4,128)(2,1)S(1)} %pad_maximum_fusion.4), channel_id=1, source_target_pairs={{0,16},{16,32},{32,48},{48,64},{64,80},{80,96},{96,112},{112,128},... | collective-permute-start | bytes 23048 | tf_op jit(solution)/shard_map/ppermute | solution.py:78
  6.0 0.7 copy-start.12
  6.0 0.7 copy-start.10
  6.1 0.7 copy-start.7
  6.1 1.2 copy-start.9
  6.1 1.2 copy-start.8
  6.7 1.5 copy-start.5
  7.3 0.7 copy-start.11
  8.3 1.0 copy-start.3
  37.7 1.0 slice-start
  63.2 0.7 copy-start.13
  65.1 1.3 copy-start.1
  65.1 1.3 copy-start.2
  65.1 1.3 copy-start.6
  116.3 20.9 %copy-start = (f32[32,32,128]{2,1,0:T(8,128)S(1)}, f32[32,32,128]{2,1,0:T(8,128)}, u32[]{:S(2)}) copy-start(f32[32,32,128]{2,1,0:T(8,128)} %shard_map.148) | copy-start | bytes 1572868
  161.9 2.8 %copy-start.4 = (f32[2,11,128]{2,1,0:T(8,128)}, f32[2,11,128]{2,1,0:T(8,128)S(1)}, u32[]{:S(2)}) copy-start(f32[2,11,128]{2,1,0:T(8,128)S(1)} %slice_multiply_fusion.8) | copy-start | bytes 33796
  162.7 4.6 %collective-permute-start.1 = (f32[3,1280]{1,0:T(4,128)S(1)}, f32[3,1280]{1,0:T(4,128)S(1)}, u32[]{:S(2)}, u32[]{:S(2)}) collective-permute-start(f32[3,1280]{1,0:T(4,128)S(1)} %pad_maximum_fusion.3), channel_id=1, source_target_pairs={{16,0},{32,16},{48,32},{64,48},{80,64},{96,80},{112,96},{128,112},... | collective-permute-start | bytes 46088 | tf_op jit(solution)/shard_map/ppermute | solution.py:78
  164.7 2.6 %slice-start.1 = ((f32[2,11,128]{2,1,0:T(8,128)}), f32[2,8,128]{2,1,0:T(8,128)S(1)}, s32[]{:S(2)}) async-start(f32[2,11,128]{2,1,0:T(8,128)} %copy-done.4), calls=%async_computation.1 | async-start | bytes 16384 | tf_op jit(solution)/shard_map/slice | solution.py:301

commit v4 on v3

--- a/solution.py
+++ b/solution.py
@@ -65,6 +65,132 @@
         compiler_params=pltpu.CompilerParams(collective_id=cid, has_side_effects=True),
     )(x)
 
+def _peer_copies(axis, n, src_of, dst, send_sem, recv_sem):
+    me = lax.axis_index(axis)
+    coords = {a: lax.axis_index(a) for a in AXES}
+
+    def dev(k):
+        return tuple(k if a == axis else coords[a] for a in AXES)
+
+    copies = []
+    for i in range(1, n):
+        peer = lax.rem(me + i, n)
+        copy = pltpu.make_async_remote_copy(
+            src_ref=src_of(peer),
+            dst_ref=dst.at[me],
+            send_sem=send_sem.at[i],
+            recv_sem=recv_sem.at[i],
+            device_id=dev(peer),
+            device_id_type=MESH,
+        )
+        copy.start()
+        copies.append(copy)
+    return copies
+
+
+def _peer_waits(axis, n, copies, src_of, dst, send_sem, recv_sem):
+    me = lax.axis_index(axis)
+    coords = {a: lax.axis_index(a) for a in AXES}
+
+    def dev(k):
+        return tuple(k if a == axis else coords[a] for a in AXES)
+
+    for i in range(1, n):
+        copies[i - 1].wait_send()
+        src = lax.rem(me + (n - i), n)
+        incoming = pltpu.make_async_remote_copy(
+            src_ref=src_of(src),
+            dst_ref=dst.at[src],
+            send_sem=send_sem.at[i],
+            recv_sem=recv_sem.at[i],
+            device_id=dev(src),
+            device_id_type=MESH,
+        )
+        incoming.wait_recv()
+
+
+def _barrier(axis, n):
+    me = lax.axis_index(axis)
+    coords = {a: lax.axis_index(a) for a in AXES}
+    barrier = pltpu.get_barrier_semaphore()
+    for i in range(1, n):
+        peer = lax.rem(me + i, n)
+        dev = tuple(peer if a == axis else coords[a] for a in AXES)
+        pl.semaphore_signal(barrier, inc=1, device_id=dev, device_id_type=MESH)
+    pl.semaphore_wait(barrier, n - 1)
+
+
+def scan_kernel(forward, axis, n, heads, *refs):
+    if forward:
+        in_ref, out_ref, scale_out, land, res, land2, s1, r1, s2, r2 = refs
+    else:
+        in_ref, scale_in, out_ref, land, res, land2, s1, r1, s2, r2 = refs
+    me = lax.axis_index(axis)
+    rows = res.shape[1]
+    _barrier(axis, n)
+    copies = _peer_copies(axis, n, lambda p: in_ref.at[p], land, s1, r1)
+    land[me] = in_ref[me]
+    _peer_waits(axis, n, copies, lambda p: in_ref.at[p], land, s1, r1)
+    if forward:
+        per = rows // heads
+        lane = lax.broadcasted_iota(jnp.int32, (rows, 128), 1)
+        row = lax.broadcasted_iota(jnp.int32, (rows, 128), 0)
+        pick = lane == row // per
+        for k in range(n):
+            grow = jnp.exp(land[k, rows : rows + 1, :])
+            factor = jnp.sum(jnp.where(pick, grow, 0.0), axis=1, keepdims=True)
+            scale_out[k] = jnp.broadcast_to(factor, (rows, 128))
+        acc = jnp.zeros((rows, 128), jnp.float32)
+        for k in range(n):
+            res[k] = acc
+            acc = scale_out[k] * acc + land[k, :rows, :]
+    else:
+        acc = jnp.zeros((rows, 128), jnp.float32)
+        for k in reversed(range(n)):
+            res[k] = acc
+            acc = land[k] + scale_in[k] * acc
+    copies = _peer_copies(axis, n, lambda p: res.at[p], land2, s2, r2)
+    land2[me] = res[me]
+    _peer_waits(axis, n, copies, lambda p: res.at[p], land2, s2, r2)
+    out_ref[...] = land2[...]
+
+
+def scan_pieces(x, axis, heads, cid, scales=None):
+    n = lax.axis_size(axis)
+    forward = scales is None
+    rows = x.shape[1] - 8 if forward else x.shape[1]
+    piece = (n, rows, 128)
+    vm = pl.BlockSpec(memory_space=pltpu.VMEM)
+    scratch = [
+        pltpu.VMEM(x.shape, jnp.float32),
+        pltpu.VMEM(piece, jnp.float32),
+        pltpu.VMEM(piece, jnp.float32),
+        pltpu.SemaphoreType.DMA((n,)),
+        pltpu.SemaphoreType.DMA((n,)),
+        pltpu.SemaphoreType.DMA((n,)),
+        pltpu.SemaphoreType.DMA((n,)),
+    ]
+    params = pltpu.CompilerParams(collective_id=cid, has_side_effects=True)
+    kern = functools.partial(scan_kernel, forward, axis, n, heads)
+    if forward:
+        return pl.pallas_call(
+            kern,
+            out_shape=(jax.ShapeDtypeStruct(piece, jnp.float32), jax.ShapeDtypeStruct(piece, jnp.float32)),
+            in_specs=[vm],
+            out_specs=(vm, vm),
+            scratch_shapes=scratch,
+            compiler_params=params,
+        )(x)
+    return pl.pallas_call(
+        kern,
+        out_shape=jax.ShapeDtypeStruct(piece, jnp.float32),
+        in_specs=[vm, vm],
+        out_specs=vm,
+        scratch_shapes=scratch,
+        compiler_params=params,
+    )(x, scales)
+
+
 INNER = 16384
 
 
@@ -126,28 +252,16 @@
     tot_row = jnp.zeros((count, 8, width), jnp.float32)
     tot_row = tot_row.at[:, 0, :heads].set(jnp.broadcast_to(totals, (count, heads)))
     sent = jnp.concatenate([pieces, tot_row], axis=1)
-    got = exchange(sent, "seq", 0)
-    block_totals = got[:, heads * rows, :heads]
-    running = jnp.cumsum(block_totals, axis=0)
-    before = running - block_totals
-    later = jnp.arange(count)[:, None] > jnp.arange(count)[None, :]
-    gap = before.T[:, :, None] - running.T[:, None, :]
-    weight = jnp.where(later[None], jnp.exp(jnp.minimum(gap, 0.0)), 0.0)
-    data = got[:, : heads * rows, :].reshape(count, heads, rows * width)
-    scanned = jnp.einsum("hkj,jhx->khx", weight, data, precision=HIGH)
-    back = exchange(scanned.reshape(count, heads * rows, width), "seq", 1)
-    return from_pieces(back.reshape(count, heads, rows, width)), weight
-
-
-def scan_backward(weight, state_grad):
+    back, scales = scan_pieces(sent, "seq", heads, 0)
+    return from_pieces(back.reshape(count, heads, rows, width)), scales
+
+
+def scan_backward(scales, state_grad):
     count = lax.axis_size("seq")
     heads, nstate, width = state_grad.shape
     rows = nstate // count
     pieces = to_pieces(state_grad, count).reshape(count, heads * rows, width)
-    got = exchange(pieces, "seq", 1)
-    data = got.reshape(count, heads, rows * width)
-    scanned = jnp.einsum("hjk,jhx->khx", weight, data, precision=HIGH)
-    back = exchange(scanned.reshape(count, heads * rows, width), "seq", 1)
+    back = scan_pieces(pieces, "seq", heads, 1, scales)
     return from_pieces(back.reshape(count, heads, rows, width))
 
 

time: 173 us -> 154 us (0.89)
  Pallas kernels: 126 us -> 111 us
  matrix products: 6.55 us -> 3.76 us
  local copies, waits for them, and re-layouts: 16.3 us -> 13.8 us
    pallas_call x6 -> x2, Pallas kernels: 126 us -> 33.4 us  [exchange(): pl.pallas_call(functools.partial(exchange_kernel, axis, n), out_shape=jax...]
    pallas_call x0 -> x2, Pallas kernels: none -> 77.9 us  [the longest x1 39.5 us: scan_pieces(): pl.pallas_call(kern, out_shape=(jax.ShapeDtypeStruct(piece, jnp.float32),...]
    unnamed x28 -> x82, local copies, waits for them, and re-layouts: 2.74 us -> 6.13 us
    reshape x4 -> x0, local copies, waits for them, and re-layouts: 2.91 us -> none  [the longest x1 1.13 us: scan_backward(): data = got.reshape(count, heads, rows * width)]
    dot_general x2 -> x0, matrix products: 1.95 us -> none  [the longest x1 1.01 us: scan_forward(): scanned = jnp.einsum('hkj,jhx->khx', weight, data, precision=HIGH)]
  transfers between devices with their start and end apart: 2 -> 2, of which waited for: 1 -> 1; matrix products, arithmetic and copies ran while one was open for 1% -> 2% of each run, Pallas kernels for 0% -> 0%
where the time goes in v4:
time: 154 us; the launch traced here: 151 us
  Pallas kernels  111 us (72%)
  local copies, waits for them, and re-layouts  13.8 us (9%)
  other arithmetic  12.7 us (8%)
  starting transfers between devices  5.24 us (3%)
  matrix products  3.76 us (2%)
  waiting for transfers between devices  2.5 us (2%)
    pallas_call x1, Pallas kernels, scan_pieces(): pl.pallas_call(kern, out_shape=(jax.ShapeDtypeStruct(piece, jnp.float32),...  39.5 us
    pallas_call x1, Pallas kernels, scan_pieces(): pl.pallas_call(kern, out_shape=jax.ShapeDtypeStruct(piece, jnp.float32),...  38.4 us
    pallas_call x2, Pallas kernels, exchange(): pl.pallas_call(functools.partial(exchange_kernel, axis, n), out_shape=jax...  33.4 us
    unnamed x82, local copies, waits for them, and re-layouts  6.13 us
    ppermute x2, starting transfers between devices, passed_along(): return lax.ppermute(block, axis, route)  5.24 us
  transfers between devices with their start and end apart: 2, of which 1 were waited for; matrix products, arithmetic and copies ran while one was open for 2% of the time, Pallas kernels for 0%

profile of v4, /device:TPU:1, one launch (start us, length us, event | category | flops | bytes accessed | tf_op | source)
XLA Modules:
  0.0 150.8 jit_solution(15360261235228653077)
XLA Ops:
  0.6 0.7 slice.167
  1.4 0.7 slice_bitcast_fusion.9
  2.1 3.9 %collective-permute-start = (bf16[3,1280]{1,0:T(4,128)(2,1)S(1)}, bf16[3,1280]{1,0:T(4,128)(2,1)S(1)}, u32[]{:S(2)}, u32[]{:S(2)}) collective-permute-start(bf16[3,1280]{1,0:T(4,128)(2,1)S(1)} %pad_maximum_fusion.4), channel_id=1, source_target_pairs={{0,16},{16,32},{32,48},{48,64},{64,80},{80,96},{96,112},{112,128},... | collective-permute-start | bytes 23048 | tf_op jit(solution)/shard_map/ppermute | solution.py:204
  6.1 0.6 copy-done.14
  6.8 0.4 copy-done.34
  7.2 0.3 reduce_window_sum.17
  7.8 0.6 fusion.57
  8.5 0.6 pad_clamp_fusion
  9.1 0.6 pad.18.clone
  10.2 0.7 copy-done.3
  10.9 0.3 multiply_convert_fusion.4
  11.4 0.3 fusion.27
  11.9 0.9 pad_maximum_fusion.refs_0_
  12.8 39.5 %shard_map.147 = (f32[32,32,128]{2,1,0:T(8,128)}, f32[32,32,128]{2,1,0:T(8,128)}) custom-call(f32[32,40,128]{2,1,0:T(8,128)} %pad_maximum_fusion.refs_0_), custom_call_target="tpu_custom_call" | custom-call | tf_op jit(solution)/shard_map/pallas_call | solution.py:176
  52.4 1.1 convert_element_type.86
  54.0 0.6 copy-done.39
  54.6 0.4 fusion.1
  55.2 0.7 copy-done.1
  56.0 0.3 multiply_reduce_fusion.5
  56.3 0.7 copy-done.37
  57.1 0.6 broadcast_in_dim.25.in_ref
  57.7 18.7 %shard_map.148 = f32[16,8,128]{2,1,0:T(8,128)} custom-call(f32[16,8,128]{2,1,0:T(8,128)} %broadcast_in_dim.25.in_ref), custom_call_target="tpu_custom_call" | custom-call | tf_op jit(solution)/shard_map/pallas_call | solution.py:55
  76.5 0.9 reduce_sum.139
  77.3 1.1 fusion.22
  78.7 0.7 copy-done.7
  79.5 0.5 multiply_reduce_fusion.6
  80.1 0.3 fusion.4
  80.5 0.6 fusion.28
  81.0 1.0 copy.73
  82.0 38.4 %shard_map.149 = f32[32,32,128]{2,1,0:T(8,128)} custom-call(f32[32,32,128]{2,1,0:T(8,128)} %bitcast.127, f32[32,32,128]{2,1,0:T(8,128)} %get-tuple-element.31.refs_1_), custom_call_target="tpu_custom_call" | custom-call | tf_op jit(solution)/shard_map/pallas_call | solution.py:184
  120.4 1.4 multiply_reduce_fusion
  121.9 0.2 multiply_reduce_fusion.1
  122.1 0.3 convolution_bitcast_fusion
  123.1 0.3 reduce_window_sum.18
  123.6 0.3 fusion.6
  124.2 1.1 gather_fusion
  125.3 0.7 copy.84
  126.0 14.6 %shard_map.150 = f32[16,32,128]{2,1,0:T(8,128)} custom-call(f32[16,32,128]{2,1,0:T(8,128)} %bitcast.144), custom_call_target="tpu_custom_call" | custom-call | tf_op jit(solution)/shard_map/pallas_call | solution.py:55
  140.7 1.0 reduce_sum.143
  141.7 0.6 copy-done.40
  142.3 0.4 fusion.3
  143.2 1.3 collective-permute-start.1
  144.5 0.7 divide_multiply_fusion
  145.2 2.5 %collective-permute-done.1 = f32[3,1280]{1,0:T(4,128)S(1)} collective-permute-done((f32[3,1280]{1,0:T(4,128)S(1)}, f32[3,1280]{1,0:T(4,128)S(1)}, u32[]{:S(2)}, u32[]{:S(2)}) %collective-permute-start.1) | collective-permute-done | bytes 15392 | tf_op jit(solution)/shard_map/ppermute | solution.py:204
  147.8 0.7 maximum_select_fusion
  148.5 0.6 fusion.44
  149.1 0.7 copy-done.9
  149.8 0.9 fusion.12
  (127 shorter events, 4.3 us)
Async XLA Ops:
  2.0 4.1 %copy-start.32 = (f32[8]{0:T(128)S(1)}, f32[8]{0:T(128)}, u32[]{:S(2)}) copy-start(f32[8]{0:T(128)} %param.20) | copy-start | bytes 100
  2.1 4.0 %copy-start.38 = (f32[8]{0:T(128)S(1)}, f32[8]{0:T(128)}, u32[]{:S(2)}) copy-start(f32[8]{0:T(128)} %param.21) | copy-start | bytes 100
  2.1 7.6 %collective-permute-start = (bf16[3,1280]{1,0:T(4,128)(2,1)S(1)}, bf16[3,1280]{1,0:T(4,128)(2,1)S(1)}, u32[]{:S(2)}, u32[]{:S(2)}) collective-permute-start(bf16[3,1280]{1,0:T(4,128)(2,1)S(1)} %pad_maximum_fusion.4), channel_id=1, source_target_pairs={{0,16},{16,32},{32,48},{48,64},{64,80},{80,96},{96,112},{112,128},... | collective-permute-start | bytes 23048 | tf_op jit(solution)/shard_map/ppermute | solution.py:204
  6.0 0.7 copy-start.14
  6.0 1.7 %copy-start.31 = (f32[2,4,128]{2,1,0:T(4,128)S(1)}, f32[2,4,128]{2,1,0:T(4,128)}, u32[]{:S(2)}) copy-start(f32[2,4,128]{2,1,0:T(4,128)} %param.24) | copy-start | bytes 12292
  6.1 1.7 %copy-start.16 = (f32[4,1024]{1,0:T(4,128)S(1)}, f32[4,1024]{1,0:T(4,128)}, u32[]{:S(2)}) copy-start(f32[4,1024]{1,0:T(4,128)} %param.23) | copy-start | bytes 49156
  6.1 47.9 %copy-start.17 = (pred[128,128]{1,0:T(8,128)(4,1)}, pred[128,128]{1,0:T(8,128)(4,1)S(1)}, u32[]{:S(2)}) copy-start(pred[128,128]{1,0:T(8,128)(4,1)S(1)} %iota_compare_fusion) | copy-start | bytes 49156
  6.1 3.6 %copy-start.5 = (bf16[2,128,128]{2,1,0:T(8,128)(2,1)S(1)}, bf16[2,128,128]{2,1,0:T(8,128)(2,1)}, u32[]{:S(2)}) copy-start(bf16[2,128,128]{2,1,0:T(8,128)(2,1)} %param.18) | copy-start | bytes 196612
  6.7 0.5 copy-start.34
  7.2 46.8 %copy-start.19 = (f32[8,128]{1,0:T(8,128)}, f32[8,128]{1,0:T(8,128)S(1)}, u32[]{:S(2)}) copy-start(f32[8,128]{1,0:T(8,128)S(1)} %get-tuple-element.43) | copy-start | bytes 12292
  7.7 1.4 copy-start.29
  7.7 2.0 %copy-start.21 = (f32[2,1,128]{2,1,0:T(1,128)}, f32[2,1,128]{2,1,0:T(1,128)S(1)}, u32[]{:S(2)}) copy-start(f32[2,1,128]{2,1,0:T(1,128)S(1)} %get-tuple-element.61) | copy-start | bytes 3076
  7.7 2.0 %copy-start.23 = (f32[2,1,128]{2,1,0:T(1,128)}, f32[2,1,128]{2,1,0:T(1,128)S(1)}, u32[]{:S(2)}) copy-start(f32[2,1,128]{2,1,0:T(1,128)S(1)} %get-tuple-element.62) | copy-start | bytes 3076
  7.7 2.0 %copy-start.25 = (f32[2,1,128]{2,1,0:T(1,128)}, f32[2,1,128]{2,1,0:T(1,128)S(1)}, u32[]{:S(2)}) copy-start(f32[2,1,128]{2,1,0:T(1,128)S(1)} %get-tuple-element.63) | copy-start | bytes 3076
  7.8 2.0 %copy-start.27 = (f32[2,1,128]{2,1,0:T(1,128)}, f32[2,1,128]{2,1,0:T(1,128)S(1)}, u32[]{:S(2)}) copy-start(f32[2,1,128]{2,1,0:T(1,128)S(1)} %get-tuple-element.64) | copy-start | bytes 3076
  7.8 3.1 %copy-start.8 = (f32[1,1024]{1,0:T(1,128)}, f32[1,1024]{1,0:T(1,128)S(1)}, u32[]{:S(2)}) copy-start(f32[1,1024]{1,0:T(1,128)S(1)} %get-tuple-element.54) | copy-start | bytes 12292
  7.8 3.1 %copy-start.10 = (f32[1,1024]{1,0:T(1,128)}, f32[1,1024]{1,0:T(1,128)S(1)}, u32[]{:S(2)}) copy-start(f32[1,1024]{1,0:T(1,128)S(1)} %get-tuple-element.55) | copy-start | bytes 12292
  7.8 0.7 copy-start.36
  9.9 1.0 copy-start.3
  10.0 44.0 %copy-start.6 = (f32[128,128]{1,0:T(8,128)}, f32[128,128]{1,0:T(8,128)S(1)}, u32[]{:S(2)}) copy-start(f32[128,128]{1,0:T(8,128)S(1)} %fusion.40) | copy-start | bytes 196612
  54.0 0.7 copy-start.39
  55.0 1.0 copy-start.1
  55.0 1.0 copy-start.2
  55.0 1.0 copy-start.12
  56.3 0.7 copy-start.37
  78.6 0.8 copy-start.7
  78.6 0.8 copy-start.18
  78.6 0.8 copy-start.20
  79.5 0.7 copy-start.13
  82.0 38.4 %copy-start = (f32[32,32,128]{2,1,0:T(8,128)S(1)}, f32[32,32,128]{2,1,0:T(8,128)}, u32[]{:S(2)}) copy-start(f32[32,32,128]{2,1,0:T(8,128)} %get-tuple-element.30) | copy-start | bytes 1572868
  141.7 0.7 copy-start.40
  142.3 2.9 %copy-start.4 = (f32[2,11,128]{2,1,0:T(8,128)}, f32[2,11,128]{2,1,0:T(8,128)S(1)}, u32[]{:S(2)}) copy-start(f32[2,11,128]{2,1,0:T(8,128)S(1)} %slice_multiply_fusion.8) | copy-start | bytes 33796
  143.1 1.4 copy-start.15
  143.2 1.3 copy-start.30
  143.2 1.3 copy-start.33
  143.2 1.3 copy-start.35
  143.2 4.5 %collective-permute-start.1 = (f32[3,1280]{1,0:T(4,128)S(1)}, f32[3,1280]{1,0:T(4,128)S(1)}, u32[]{:S(2)}, u32[]{:S(2)}) collective-permute-start(f32[3,1280]{1,0:T(4,128)S(1)} %pad_maximum_fusion.3), channel_id=1, source_target_pairs={{16,0},{32,16},{48,32},{64,48},{80,64},{96,80},{112,96},{128,112},... | collective-permute-start | bytes 46088 | tf_op jit(solution)/shard_map/ppermute | solution.py:204
  145.2 2.5 %slice-start = ((f32[2,11,128]{2,1,0:T(8,128)}), f32[2,8,128]{2,1,0:T(8,128)S(1)}, s32[]{:S(2)}) async-start(f32[2,11,128]{2,1,0:T(8,128)} %copy-done.4), calls=%async_computation | async-start | bytes 16384 | tf_op jit(solution)/shard_map/slice | solution.py:415
  147.7 0.8 copy-start.22
  147.7 0.8 copy-start.24
  147.7 0.8 copy-start.26
  147.7 0.8 copy-start.28
  149.1 0.7 copy-start.9
  149.1 0.7 copy-start.11

commit v5 on v4

--- a/solution.py
+++ b/solution.py
@@ -137,18 +137,19 @@
         row = lax.broadcasted_iota(jnp.int32, (rows, 128), 0)
         pick = lane == row // per
         for k in range(n):
-            grow = jnp.exp(land[k, rows : rows + 1, :])
+            parts = land[k, rows : rows + 3, :].astype(jnp.float32)
+            grow = jnp.exp(parts[0:1] + parts[1:2] + parts[2:3])
             factor = jnp.sum(jnp.where(pick, grow, 0.0), axis=1, keepdims=True)
             scale_out[k] = jnp.broadcast_to(factor, (rows, 128))
         acc = jnp.zeros((rows, 128), jnp.float32)
         for k in range(n):
-            res[k] = acc
-            acc = scale_out[k] * acc + land[k, :rows, :]
+            res[k] = acc.astype(res.dtype)
+            acc = scale_out[k] * acc + land[k, :rows, :].astype(jnp.float32)
     else:
         acc = jnp.zeros((rows, 128), jnp.float32)
         for k in reversed(range(n)):
-            res[k] = acc
-            acc = land[k] + scale_in[k] * acc
+            res[k] = acc.astype(res.dtype)
+            acc = land[k].astype(jnp.float32) + scale_in[k] * acc
     copies = _peer_copies(axis, n, lambda p: res.at[p], land2, s2, r2)
     land2[me] = res[me]
     _peer_waits(axis, n, copies, lambda p: res.at[p], land2, s2, r2)
@@ -158,13 +159,14 @@
 def scan_pieces(x, axis, heads, cid, scales=None):
     n = lax.axis_size(axis)
     forward = scales is None
-    rows = x.shape[1] - 8 if forward else x.shape[1]
+    rows = x.shape[1] - 16 if forward else x.shape[1]
     piece = (n, rows, 128)
+    low = x.dtype
     vm = pl.BlockSpec(memory_space=pltpu.VMEM)
     scratch = [
-        pltpu.VMEM(x.shape, jnp.float32),
-        pltpu.VMEM(piece, jnp.float32),
-        pltpu.VMEM(piece, jnp.float32),
+        pltpu.VMEM(x.shape, low),
+        pltpu.VMEM(piece, low),
+        pltpu.VMEM(piece, low),
         pltpu.SemaphoreType.DMA((n,)),
         pltpu.SemaphoreType.DMA((n,)),
         pltpu.SemaphoreType.DMA((n,)),
@@ -175,7 +177,7 @@
     if forward:
         return pl.pallas_call(
             kern,
-            out_shape=(jax.ShapeDtypeStruct(piece, jnp.float32), jax.ShapeDtypeStruct(piece, jnp.float32)),
+            out_shape=(jax.ShapeDtypeStruct(piece, low), jax.ShapeDtypeStruct(piece, jnp.float32)),
             in_specs=[vm],
             out_specs=(vm, vm),
             scratch_shapes=scratch,
@@ -183,7 +185,7 @@
         )(x)
     return pl.pallas_call(
         kern,
-        out_shape=jax.ShapeDtypeStruct(piece, jnp.float32),
+        out_shape=jax.ShapeDtypeStruct(piece, low),
         in_specs=[vm, vm],
         out_specs=vm,
         scratch_shapes=scratch,
@@ -249,20 +251,24 @@
     heads, nstate, width = local_state.shape
     rows = nstate // count
     pieces = to_pieces(local_state, count).reshape(count, heads * rows, width)
-    tot_row = jnp.zeros((count, 8, width), jnp.float32)
-    tot_row = tot_row.at[:, 0, :heads].set(jnp.broadcast_to(totals, (count, heads)))
-    sent = jnp.concatenate([pieces, tot_row], axis=1)
+    high = lax.reduce_precision(totals, exponent_bits=8, mantissa_bits=7)
+    rest = totals - high
+    middle = lax.reduce_precision(rest, exponent_bits=8, mantissa_bits=7)
+    parts = jnp.stack([high, middle, rest - middle])
+    tot_row = jnp.zeros((count, 16, width), jnp.float32)
+    tot_row = tot_row.at[:, 0:3, :heads].set(jnp.broadcast_to(parts, (count, 3, heads)))
+    sent = jnp.concatenate([pieces, tot_row], axis=1).astype(jnp.bfloat16)
     back, scales = scan_pieces(sent, "seq", heads, 0)
-    return from_pieces(back.reshape(count, heads, rows, width)), scales
+    return from_pieces(back.reshape(count, heads, rows, width)).astype(jnp.float32), scales
 
 
 def scan_backward(scales, state_grad):
     count = lax.axis_size("seq")
     heads, nstate, width = state_grad.shape
     rows = nstate // count
-    pieces = to_pieces(state_grad, count).reshape(count, heads * rows, width)
+    pieces = to_pieces(state_grad, count).reshape(count, heads * rows, width).astype(jnp.bfloat16)
     back = scan_pieces(pieces, "seq", heads, 1, scales)
-    return from_pieces(back.reshape(count, heads, rows, width))
+    return from_pieces(back.reshape(count, heads, rows, width)).astype(jnp.float32)
 
 
 def shards(

time: 154 us -> 132 us (0.86)
  Pallas kernels: 111 us -> 89.8 us
  local copies, waits for them, and re-layouts: 13.8 us -> 16.6 us
  other arithmetic: 12.7 us -> 11 us
    pallas_call x2, Pallas kernels: 77.9 us -> 54.9 us  [the longest x1 29.2 us: scan_pieces(): pl.pallas_call(kern, out_shape=(jax.ShapeDtypeStruct(piece, low), jax.Sha...]
    transpose x0 -> x2, local copies, waits for them, and re-layouts: none -> 2.14 us  [from_pieces(): return jnp.moveaxis(pieces, 0, 1).reshape(heads, count * rows, width)]
    unnamed x82 -> x80, local copies, waits for them, and re-layouts: 6.13 us -> 7.21 us
where the time goes in v5:
time: 132 us; the launch traced here: 130 us
  Pallas kernels  89.8 us (68%)
  local copies, waits for them, and re-layouts  16.6 us (13%)
  other arithmetic  11 us (8%)
  starting transfers between devices  5.24 us (4%)
  matrix products  3.77 us (3%)
  waiting for transfers between devices  2.5 us (2%)
  between operations  1.38 us (1%)
    pallas_call x2, Pallas kernels, exchange(): pl.pallas_call(functools.partial(exchange_kernel, axis, n), out_shape=jax...  34.9 us
    pallas_call x1, Pallas kernels, scan_pieces(): pl.pallas_call(kern, out_shape=(jax.ShapeDtypeStruct(piece, low), jax.Sha...  29.2 us
    pallas_call x1, Pallas kernels, scan_pieces(): pl.pallas_call(kern, out_shape=jax.ShapeDtypeStruct(piece, low), in_specs...  25.7 us
    unnamed x80, local copies, waits for them, and re-layouts  7.21 us
    ppermute x2, starting transfers between devices, passed_along(): return lax.ppermute(block, axis, route)  5.24 us
  transfers between devices with their start and end apart: 2, of which 1 were waited for; matrix products, arithmetic and copies ran while one was open for 2% of the time, Pallas kernels for 0%

profile of v5, /device:TPU:1, one launch (start us, length us, event | category | flops | bytes accessed | tf_op | source)
XLA Modules:
  0.0 130.2 jit_solution(16981219250163748202)
XLA Ops:
  0.6 0.7 slice.169
  1.4 0.7 slice_bitcast_fusion.9
  2.1 3.9 %collective-permute-start = (bf16[3,1280]{1,0:T(4,128)(2,1)S(1)}, bf16[3,1280]{1,0:T(4,128)(2,1)S(1)}, u32[]{:S(2)}, u32[]{:S(2)}) collective-permute-start(bf16[3,1280]{1,0:T(4,128)(2,1)S(1)} %pad_maximum_fusion.4), channel_id=1, source_target_pairs={{0,16},{16,32},{32,48},{48,64},{64,80},{80,96},{96,112},{112,128},... | collective-permute-start | bytes 23048 | tf_op jit(solution)/shard_map/ppermute | solution.py:206
  6.1 0.6 copy-done.13
  6.8 0.4 copy-done.33
  7.3 0.3 reduce_window_sum.17
  7.7 0.6 copy-done.28
  8.3 0.6 fusion.58
  9.0 0.6 copy-done.35
  9.6 0.6 pad_clamp_fusion
  10.3 0.6 pad.18.clone
  11.3 0.7 copy-done.4
  12.1 0.3 multiply_convert_fusion.4
  12.6 0.3 convolution_convert_fusion.1
  13.0 0.8 pad_maximum_fusion.1.refs_0_
  13.8 29.2 %shard_map.147 = (bf16[32,32,128]{2,1,0:T(8,128)(2,1)}, f32[32,32,128]{2,1,0:T(8,128)}) custom-call(bf16[32,48,128]{2,1,0:T(8,128)(2,1)} %pad_maximum_fusion.1.refs_0_), custom_call_target="tpu_custom_call" | custom-call | tf_op jit(solution)/shard_map/pallas_call | solution.py:178
  43.0 1.0 copy.67
  44.5 0.6 copy-done.38
  45.1 0.4 fusion.1
  45.8 0.7 copy-done.2
  46.6 1.0 multiply_reduce_fusion.5
  47.6 0.7 copy-done.36
  48.3 0.6 broadcast_in_dim.25.in_ref
  48.9 19.6 %shard_map.148 = f32[16,8,128]{2,1,0:T(8,128)} custom-call(f32[16,8,128]{2,1,0:T(8,128)} %broadcast_in_dim.25.in_ref), custom_call_target="tpu_custom_call" | custom-call | tf_op jit(solution)/shard_map/pallas_call | solution.py:55
  68.6 0.9 reduce_sum.132
  69.5 1.1 fusion.22
  70.9 0.6 copy-done.17
  71.5 0.5 multiply_reduce_fusion.6
  72.2 0.6 convolution_convert_fusion
  72.7 0.8 copy.73
  73.5 25.7 %shard_map.149 = bf16[32,32,128]{2,1,0:T(8,128)(2,1)} custom-call(bf16[32,32,128]{2,1,0:T(8,128)(2,1)} %bitcast.158, f32[32,32,128]{2,1,0:T(8,128)} %get-tuple-element.31.refs_1_), custom_call_target="tpu_custom_call" | custom-call | tf_op jit(solution)/shard_map/pallas_call | solution.py:186
  99.3 1.1 copy.74
  100.4 0.3 multiply_reduce_fusion
  100.7 0.3 fusion.4
  102.0 0.3 reduce_window_sum.18
  103.1 1.1 gather_fusion
  104.2 0.7 copy.84
  104.9 15.2 %shard_map.150 = f32[16,32,128]{2,1,0:T(8,128)} custom-call(f32[16,32,128]{2,1,0:T(8,128)} %bitcast.157), custom_call_target="tpu_custom_call" | custom-call | tf_op jit(solution)/shard_map/pallas_call | solution.py:55
  120.1 1.0 reduce_sum.136
  121.2 0.6 copy-done.39
  121.8 0.4 fusion.3
  122.7 1.3 collective-permute-start.1
  124.0 0.7 divide_multiply_fusion
  124.7 2.5 %collective-permute-done.1 = f32[3,1280]{1,0:T(4,128)S(1)} collective-permute-done((f32[3,1280]{1,0:T(4,128)S(1)}, f32[3,1280]{1,0:T(4,128)S(1)}, u32[]{:S(2)}, u32[]{:S(2)}) %collective-permute-start.1) | collective-permute-done | bytes 15392 | tf_op jit(solution)/shard_map/ppermute | solution.py:206
  127.2 0.7 maximum_select_fusion
  128.0 0.6 fusion.42
  128.6 0.7 copy-done.8
  129.3 0.9 fusion.12
  (123 shorter events, 4.6 us)
Async XLA Ops:
  2.1 4.0 %copy-start.37 = (f32[8]{0:T(128)S(1)}, f32[8]{0:T(128)}, u32[]{:S(2)}) copy-start(f32[8]{0:T(128)} %param.21) | copy-start | bytes 100
  2.1 8.8 %collective-permute-start = (bf16[3,1280]{1,0:T(4,128)(2,1)S(1)}, bf16[3,1280]{1,0:T(4,128)(2,1)S(1)}, u32[]{:S(2)}, u32[]{:S(2)}) collective-permute-start(bf16[3,1280]{1,0:T(4,128)(2,1)S(1)} %pad_maximum_fusion.4), channel_id=1, source_target_pairs={{0,16},{16,32},{32,48},{48,64},{64,80},{80,96},{96,112},{112,128},... | collective-permute-start | bytes 23048 | tf_op jit(solution)/shard_map/ppermute | solution.py:206
  6.0 0.7 copy-start.13
  6.0 0.7 copy-start.31
  6.1 38.4 %copy-start.16 = (pred[128,128]{1,0:T(8,128)(4,1)}, pred[128,128]{1,0:T(8,128)(4,1)S(1)}, u32[]{:S(2)}) copy-start(pred[128,128]{1,0:T(8,128)(4,1)S(1)} %iota_compare_fusion) | copy-start | bytes 49156
  6.1 2.8 %copy-start.30 = (f32[2,4,128]{2,1,0:T(4,128)S(1)}, f32[2,4,128]{2,1,0:T(4,128)}, u32[]{:S(2)}) copy-start(f32[2,4,128]{2,1,0:T(4,128)} %param.24) | copy-start | bytes 12292
  6.1 2.8 %copy-start.15 = (f32[4,1024]{1,0:T(4,128)S(1)}, f32[4,1024]{1,0:T(4,128)}, u32[]{:S(2)}) copy-start(f32[4,1024]{1,0:T(4,128)} %param.23) | copy-start | bytes 49156
  6.7 0.5 copy-start.33
  6.7 4.1 %copy-start.6 = (bf16[2,128,128]{2,1,0:T(8,128)(2,1)S(1)}, bf16[2,128,128]{2,1,0:T(8,128)(2,1)}, u32[]{:S(2)}) copy-start(bf16[2,128,128]{2,1,0:T(8,128)(2,1)} %param.18) | copy-start | bytes 196612
  7.2 37.3 %copy-start.18 = (f32[8,128]{1,0:T(8,128)}, f32[8,128]{1,0:T(8,128)S(1)}, u32[]{:S(2)}) copy-start(f32[8,128]{1,0:T(8,128)S(1)} %get-tuple-element.43) | copy-start | bytes 12292
  7.7 0.6 copy-start.28
  8.9 2.0 %copy-start.20 = (f32[2,1,128]{2,1,0:T(1,128)}, f32[2,1,128]{2,1,0:T(1,128)S(1)}, u32[]{:S(2)}) copy-start(f32[2,1,128]{2,1,0:T(1,128)S(1)} %get-tuple-element.59) | copy-start | bytes 3076
  8.9 2.0 %copy-start.22 = (f32[2,1,128]{2,1,0:T(1,128)}, f32[2,1,128]{2,1,0:T(1,128)S(1)}, u32[]{:S(2)}) copy-start(f32[2,1,128]{2,1,0:T(1,128)S(1)} %get-tuple-element.60) | copy-start | bytes 3076
  8.9 2.0 %copy-start.24 = (f32[2,1,128]{2,1,0:T(1,128)}, f32[2,1,128]{2,1,0:T(1,128)S(1)}, u32[]{:S(2)}) copy-start(f32[2,1,128]{2,1,0:T(1,128)S(1)} %get-tuple-element.61) | copy-start | bytes 3076
  8.9 2.0 %copy-start.26 = (f32[2,1,128]{2,1,0:T(1,128)}, f32[2,1,128]{2,1,0:T(1,128)S(1)}, u32[]{:S(2)}) copy-start(f32[2,1,128]{2,1,0:T(1,128)S(1)} %get-tuple-element.62) | copy-start | bytes 3076
  8.9 0.7 copy-start.35
  9.6 2.4 %copy-start.7 = (f32[1,1024]{1,0:T(1,128)}, f32[1,1024]{1,0:T(1,128)S(1)}, u32[]{:S(2)}) copy-start(f32[1,1024]{1,0:T(1,128)S(1)} %get-tuple-element.52) | copy-start | bytes 12292
  9.6 2.4 %copy-start.9 = (f32[1,1024]{1,0:T(1,128)}, f32[1,1024]{1,0:T(1,128)S(1)}, u32[]{:S(2)}) copy-start(f32[1,1024]{1,0:T(1,128)S(1)} %get-tuple-element.53) | copy-start | bytes 12292
  11.0 1.0 copy-start.4
  44.5 0.7 copy-start.38
  45.5 1.0 copy-start.2
  45.6 1.0 copy-start.3
  47.6 0.7 copy-start.36
  68.6 0.9 copy-start.11
  70.8 0.7 copy-start.17
  70.8 0.7 copy-start.19
  71.5 0.7 copy-start.12
  99.2 1.1 copy-start
  99.2 1.1 copy-start.1
  121.1 0.7 copy-start.39
  121.8 2.9 %copy-start.5 = (f32[2,11,128]{2,1,0:T(8,128)}, f32[2,11,128]{2,1,0:T(8,128)S(1)}, u32[]{:S(2)}) copy-start(f32[2,11,128]{2,1,0:T(8,128)S(1)} %slice_multiply_fusion.8) | copy-start | bytes 33796
  122.6 1.4 %copy-start.14 = (f32[8,128]{1,0:T(8,128)S(1)}, f32[8,128]{1,0:T(8,128)}, u32[]{:S(2)}) copy-start(f32[8,128]{1,0:T(8,128)} %param.19) | copy-start | bytes 12292
  122.6 1.3 %copy-start.29 = (f32[8]{0:T(128)S(1)}, f32[8]{0:T(128)}, u32[]{:S(2)}) copy-start(f32[8]{0:T(128)} %copy-done.28) | copy-start | bytes 100
  122.6 1.3 %copy-start.32 = (f32[8]{0:T(128)S(1)}, f32[8]{0:T(128)}, u32[]{:S(2)}) copy-start(f32[8]{0:T(128)} %param.20) | copy-start | bytes 100
  122.6 1.3 %copy-start.34 = (f32[8]{0:T(128)S(1)}, f32[8]{0:T(128)}, u32[]{:S(2)}) copy-start(f32[8]{0:T(128)} %copy-done.33) | copy-start | bytes 100
  122.7 4.5 %collective-permute-start.1 = (f32[3,1280]{1,0:T(4,128)S(1)}, f32[3,1280]{1,0:T(4,128)S(1)}, u32[]{:S(2)}, u32[]{:S(2)}) collective-permute-start(f32[3,1280]{1,0:T(4,128)S(1)} %pad_maximum_fusion.3), channel_id=1, source_target_pairs={{16,0},{32,16},{48,32},{64,48},{80,64},{96,80},{112,96},{128,112},... | collective-permute-start | bytes 46088 | tf_op jit(solution)/shard_map/ppermute | solution.py:206
  124.7 2.5 %slice-start = ((f32[2,11,128]{2,1,0:T(8,128)}), f32[2,8,128]{2,1,0:T(8,128)S(1)}, s32[]{:S(2)}) async-start(f32[2,11,128]{2,1,0:T(8,128)} %copy-done.5), calls=%async_computation | async-start | bytes 16384 | tf_op jit(solution)/shard_map/slice | solution.py:421
  127.2 0.8 copy-start.21
  127.2 0.8 copy-start.23
  127.2 0.8 copy-start.25
  127.2 0.8 copy-start.27
  128.6 0.7 copy-start.8
  128.6 0.7 copy-start.10

commit v6 on v5

--- a/solution.py
+++ b/solution.py
@@ -132,10 +132,8 @@
     land[me] = in_ref[me]
     _peer_waits(axis, n, copies, lambda p: in_ref.at[p], land, s1, r1)
     if forward:
-        per = rows // heads
-        lane = lax.broadcasted_iota(jnp.int32, (rows, 128), 1)
-        row = lax.broadcasted_iota(jnp.int32, (rows, 128), 0)
-        pick = lane == row // per
+        lane = lax.broadcasted_iota(jnp.int32, (1, 128), 1)
+        pick = lane == me // (n // heads)
         for k in range(n):
             parts = land[k, rows : rows + 3, :].astype(jnp.float32)
             grow = jnp.exp(parts[0:1] + parts[1:2] + parts[2:3])
@@ -237,20 +235,18 @@
 
 def to_pieces(state, count):
     heads, nstate, width = state.shape
-    rows = nstate // count
-    return jnp.moveaxis(state.reshape(heads, count, rows, width), 1, 0)
-
-
-def from_pieces(pieces):
-    count, heads, rows, width = pieces.shape
-    return jnp.moveaxis(pieces, 0, 1).reshape(heads, count * rows, width)
+    return state.reshape(count, heads * nstate // count, width)
+
+
+def from_pieces(pieces, heads):
+    count, rows, width = pieces.shape
+    return pieces.reshape(heads, count * rows // heads, width)
 
 
 def scan_forward(totals, local_state):
     count = lax.axis_size("seq")
     heads, nstate, width = local_state.shape
-    rows = nstate // count
-    pieces = to_pieces(local_state, count).reshape(count, heads * rows, width)
+    pieces = to_pieces(local_state, count)
     high = lax.reduce_precision(totals, exponent_bits=8, mantissa_bits=7)
     rest = totals - high
     middle = lax.reduce_precision(rest, exponent_bits=8, mantissa_bits=7)
@@ -259,16 +255,15 @@
     tot_row = tot_row.at[:, 0:3, :heads].set(jnp.broadcast_to(parts, (count, 3, heads)))
     sent = jnp.concatenate([pieces, tot_row], axis=1).astype(jnp.bfloat16)
     back, scales = scan_pieces(sent, "seq", heads, 0)
-    return from_pieces(back.reshape(count, heads, rows, width)).astype(jnp.float32), scales
+    return from_pieces(back, heads).astype(jnp.float32), scales
 
 
 def scan_backward(scales, state_grad):
     count = lax.axis_size("seq")
-    heads, nstate, width = state_grad.shape
-    rows = nstate // count
-    pieces = to_pieces(state_grad, count).reshape(count, heads * rows, width).astype(jnp.bfloat16)
+    heads = state_grad.shape[0]
+    pieces = to_pieces(state_grad, count).astype(jnp.bfloat16)
     back = scan_pieces(pieces, "seq", heads, 1, scales)
-    return from_pieces(back.reshape(count, heads, rows, width)).astype(jnp.float32)
+    return from_pieces(back, heads).astype(jnp.float32)
 
 
 def shards(

time: 132 us -> 126 us (0.955)
  local copies, waits for them, and re-layouts: 16.6 us -> 10.5 us
    pallas_call x2, Pallas kernels: 34.9 us -> 39.2 us  [exchange(): pl.pallas_call(functools.partial(exchange_kernel, axis, n), out_shape=jax...]
    pallas_call x1, Pallas kernels: 25.7 us -> 22 us  [scan_pieces(): pl.pallas_call(kern, out_shape=jax.ShapeDtypeStruct(piece, low), in_specs...]
    unnamed x80 -> x30, local copies, waits for them, and re-layouts: 7.21 us -> 3.82 us
    transpose x2 -> x0, local copies, waits for them, and re-layouts: 2.14 us -> none  [from_pieces(): return jnp.moveaxis(pieces, 0, 1).reshape(heads, count * rows, width)]
  transfers between devices with their start and end apart: 2 -> 2, of which waited for: 1 -> 1; matrix products, arithmetic and copies ran while one was open for 2% -> 1% of each run, Pallas kernels for 0% -> 0%
where the time goes in v6:
time: 126 us; the launch traced here: 124 us
  Pallas kernels  89.5 us (71%)
  local copies, waits for them, and re-layouts  10.5 us (8%)
  other arithmetic  10.3 us (8%)
  starting transfers between devices  5.24 us (4%)
  matrix products  4.48 us (4%)
  waiting for transfers between devices  2.58 us (2%)
    pallas_call x2, Pallas kernels, exchange(): pl.pallas_call(functools.partial(exchange_kernel, axis, n), out_shape=jax...  39.2 us
    pallas_call x1, Pallas kernels, scan_pieces(): pl.pallas_call(kern, out_shape=(jax.ShapeDtypeStruct(piece, low), jax.Sha...  28.3 us
    pallas_call x1, Pallas kernels, scan_pieces(): pl.pallas_call(kern, out_shape=jax.ShapeDtypeStruct(piece, low), in_specs...  22 us
    ppermute x2, starting transfers between devices, passed_along(): return lax.ppermute(block, axis, route)  5.24 us
    unnamed x30, local copies, waits for them, and re-layouts  3.82 us
    ppermute x2, waiting for transfers between devices, passed_along(): return lax.ppermute(block, axis, route)  2.58 us
  transfers between devices with their start and end apart: 2, of which 1 were waited for; matrix products, arithmetic and copies ran while one was open for 1% of the time, Pallas kernels for 0%

profile of v6, /device:TPU:1, one launch (start us, length us, event | category | flops | bytes accessed | tf_op | source)
XLA Modules:
  0.0 123.8 jit_solution(5969488435765890899)
XLA Ops:
  0.6 0.7 slice.169
  1.4 0.7 slice_bitcast_fusion.9
  2.1 3.9 %collective-permute-start = (bf16[3,1280]{1,0:T(4,128)(2,1)S(1)}, bf16[3,1280]{1,0:T(4,128)(2,1)S(1)}, u32[]{:S(2)}, u32[]{:S(2)}) collective-permute-start(bf16[3,1280]{1,0:T(4,128)(2,1)S(1)} %pad_maximum_fusion.4), channel_id=1, source_target_pairs={{0,16},{16,32},{32,48},{48,64},{64,80},{80,96},{96,112},{112,128},... | collective-permute-start | bytes 23048 | tf_op jit(solution)/shard_map/ppermute | solution.py:204
  6.1 0.6 copy-done.8
  6.8 0.3 reduce_window_sum.17
  7.1 0.2 slice_reduce_fusion
  7.4 0.6 copy-done.12
  8.6 0.7 copy-done.4
  9.4 0.3 multiply_convert_fusion.4
  9.7 0.2 copy.55
  9.9 0.3 convolution_convert_fusion.1
  10.2 0.8 pad_maximum_fusion.1.refs_0_
  11.0 28.3 %shard_map.147 = (bf16[32,32,128]{2,1,0:T(8,128)(2,1)}, f32[32,32,128]{2,1,0:T(8,128)}) custom-call(bf16[32,48,128]{2,1,0:T(8,128)(2,1)} %pad_maximum_fusion.1.refs_0_), custom_call_target="tpu_custom_call" | custom-call | tf_op jit(solution)/shard_map/pallas_call | solution.py:176
  39.3 1.1 copy.58
  40.4 0.2 fusion.40
  40.6 0.6 copy-done.14
  41.3 0.4 fusion.1
  41.7 0.2 copy.59
  41.9 0.7 copy-done.2
  42.7 0.3 multiply_reduce_fusion.5
  43.1 0.6 broadcast_in_dim.25.in_ref
  43.7 22.0 %shard_map.148 = f32[16,8,128]{2,1,0:T(8,128)} custom-call(f32[16,8,128]{2,1,0:T(8,128)} %broadcast_in_dim.25.in_ref), custom_call_target="tpu_custom_call" | custom-call | tf_op jit(solution)/shard_map/pallas_call | solution.py:55
  65.8 0.9 reduce_sum.139
  66.7 1.1 fusion.22
  68.0 0.5 multiply_reduce_fusion.6
  68.5 0.4 copy-done.1
  68.9 0.3 fusion.4
  69.3 1.3 %convolution_convert_fusion = bf16[8,128,128]{2,1,0:T(8,128)(2,1)} fusion(bf16[128,8,128]{0,2,1:T(8,128)(2,1)S(1)} %bitcast.125, f32[128,128]{1,0:T(8,128)S(1)} %get-tuple-element.48, f32[8,128]{1,0:T(8,128)S(1)} %get-tuple-element.56), kind=kOutput, calls=%fused_computation.10 | convolution fusion | flops 33947648 | bytes 593920 | tf_op jit(solution)/shard_map/htn,thp->hnp/dot_general | solution.py:347
  70.5 22.0 %shard_map.149 = bf16[32,32,128]{2,1,0:T(8,128)(2,1)} custom-call(bf16[32,32,128]{2,1,0:T(8,128)(2,1)} %bitcast.140, f32[32,32,128]{2,1,0:T(8,128)} %get-tuple-element.31.refs_1_), custom_call_target="tpu_custom_call" | custom-call | tf_op jit(solution)/shard_map/pallas_call | solution.py:184
  92.6 1.3 %multiply_reduce_fusion = f32[32]{0:T(128)S(1)} fusion(bf16[32,32,128]{2,1,0:T(8,128)(2,1)S(1)} %copy-done.1, bf16[32,32,128]{2,1,0:T(8,128)(2,1)} %shard_map.149), kind=kLoop, calls=%fused_computation.51 | loop fusion | flops 524256 | bytes 524416 | tf_op jit(solution)/shard_map/reduce_sum | solution.py:361
  93.9 0.2 multiply_reduce_fusion.1
  94.2 0.3 convolution_bitcast_fusion
  95.2 0.3 reduce_window_sum.18
  95.6 0.3 fusion.6
  95.9 0.2 fusion.5
  96.2 1.0 gather_fusion
  97.2 0.7 copy.72
  97.9 17.1 %shard_map.150 = f32[16,32,128]{2,1,0:T(8,128)} custom-call(f32[16,32,128]{2,1,0:T(8,128)} %bitcast.139), custom_call_target="tpu_custom_call" | custom-call | tf_op jit(solution)/shard_map/pallas_call | solution.py:55
  115.1 1.0 reduce_sum.143
  116.1 0.4 fusion.3
  116.5 0.2 copy.65
  116.7 0.2 multiply_multiply_fusion
  116.9 1.3 %collective-permute-start.1 = (f32[3,1280]{1,0:T(4,128)S(1)}, f32[3,1280]{1,0:T(4,128)S(1)}, u32[]{:S(2)}, u32[]{:S(2)}) collective-permute-start(f32[3,1280]{1,0:T(4,128)S(1)} %pad_maximum_fusion.3), channel_id=1, source_target_pairs={{16,0},{32,16},{48,32},{64,48},{80,64},{96,80},{112,96},{128,112},... | collective-permute-start | bytes 46088 | tf_op jit(solution)/shard_map/ppermute | solution.py:204
  118.2 0.7 divide_multiply_fusion
  118.9 2.6 %collective-permute-done.1 = f32[3,1280]{1,0:T(4,128)S(1)} collective-permute-done((f32[3,1280]{1,0:T(4,128)S(1)}, f32[3,1280]{1,0:T(4,128)S(1)}, u32[]{:S(2)}, u32[]{:S(2)}) %collective-permute-start.1) | collective-permute-done | bytes 15392 | tf_op jit(solution)/shard_map/ppermute | solution.py:204
  121.5 0.7 maximum_select_fusion
  122.2 0.6 fusion.42
  122.8 0.9 fusion.12
  (71 shorter events, 2.3 us)
Async XLA Ops:
  2.1 4.0 %copy-start.13 = (f32[8]{0:T(128)S(1)}, f32[8]{0:T(128)}, u32[]{:S(2)}) copy-start(f32[8]{0:T(128)} %param.21) | copy-start | bytes 100
  2.1 6.1 %collective-permute-start = (bf16[3,1280]{1,0:T(4,128)(2,1)S(1)}, bf16[3,1280]{1,0:T(4,128)(2,1)S(1)}, u32[]{:S(2)}, u32[]{:S(2)}) collective-permute-start(bf16[3,1280]{1,0:T(4,128)(2,1)S(1)} %pad_maximum_fusion.4), channel_id=1, source_target_pairs={{0,16},{16,32},{32,48},{48,64},{64,80},{80,96},{96,112},{112,128},... | collective-permute-start | bytes 23048 | tf_op jit(solution)/shard_map/ppermute | solution.py:204
  6.0 0.7 copy-start.8
  6.0 0.7 copy-start.11
  6.1 1.3 %copy-start.10 = (f32[2,4,128]{2,1,0:T(4,128)S(1)}, f32[2,4,128]{2,1,0:T(4,128)}, u32[]{:S(2)}) copy-start(f32[2,4,128]{2,1,0:T(4,128)} %param.24) | copy-start | bytes 12292
  6.1 1.3 %copy-start.9 = (f32[4,1024]{1,0:T(4,128)S(1)}, f32[4,1024]{1,0:T(4,128)}, u32[]{:S(2)}) copy-start(f32[4,1024]{1,0:T(4,128)} %param.23) | copy-start | bytes 49156
  6.7 1.5 %copy-start.6 = (bf16[2,128,128]{2,1,0:T(8,128)(2,1)S(1)}, bf16[2,128,128]{2,1,0:T(8,128)(2,1)}, u32[]{:S(2)}) copy-start(bf16[2,128,128]{2,1,0:T(8,128)(2,1)} %param.18) | copy-start | bytes 196612
  7.4 0.7 copy-start.12
  8.3 1.0 copy-start.4
  40.6 0.7 copy-start.14
  41.7 1.0 copy-start.2
  41.7 1.0 copy-start.3
  41.7 1.0 copy-start.7
  68.0 1.0 copy-start.1
  92.6 1.4 %copy-start = (bf16[32,32,128]{2,1,0:T(8,128)(2,1)S(1)}, bf16[32,32,128]{2,1,0:T(8,128)(2,1)}, u32[]{:S(2)}) copy-start(bf16[32,32,128]{2,1,0:T(8,128)(2,1)} %shard_map.149) | copy-start | bytes 786436
  116.1 2.8 %copy-start.5 = (f32[2,11,128]{2,1,0:T(8,128)}, f32[2,11,128]{2,1,0:T(8,128)S(1)}, u32[]{:S(2)}) copy-start(f32[2,11,128]{2,1,0:T(8,128)S(1)} %slice_multiply_fusion.8) | copy-start | bytes 33796
  116.9 4.6 %collective-permute-start.1 = (f32[3,1280]{1,0:T(4,128)S(1)}, f32[3,1280]{1,0:T(4,128)S(1)}, u32[]{:S(2)}, u32[]{:S(2)}) collective-permute-start(f32[3,1280]{1,0:T(4,128)S(1)} %pad_maximum_fusion.3), channel_id=1, source_target_pairs={{16,0},{32,16},{48,32},{64,48},{80,64},{96,80},{112,96},{128,112},... | collective-permute-start | bytes 46088 | tf_op jit(solution)/shard_map/ppermute | solution.py:204
  118.9 2.6 %slice-start = ((f32[2,11,128]{2,1,0:T(8,128)}), f32[2,8,128]{2,1,0:T(8,128)S(1)}, s32[]{:S(2)}) async-start(f32[2,11,128]{2,1,0:T(8,128)} %copy-done.5), calls=%async_computation | async-start | bytes 16384 | tf_op jit(solution)/shard_map/slice | solution.py:416

commit v7 on v6

--- a/solution.py
+++ b/solution.py
@@ -191,6 +191,123 @@
     )(x, scales)
 
 
+def forward_kernel(n, hn, heads, *refs):
+    (in_ref, c_ref, base_ref, lift_ref, gate_ref, scaled_ref,
+     out_ref, scale_out, mixed_out, handed_out, sums_out,
+     land, res, land2, gath, s1, r1, s2, r2, s3, r3) = refs
+    me = lax.axis_index("seq")
+    hme = lax.axis_index("head")
+    rows = res.shape[1]
+    width = 128
+    barrier = pltpu.get_barrier_semaphore()
+    for i in range(1, n):
+        pl.semaphore_signal(barrier, inc=1, device_id=(lax.rem(me + i, n), hme), device_id_type=MESH)
+    for i in range(1, hn):
+        pl.semaphore_signal(barrier, inc=1, device_id=(me, lax.rem(hme + i, hn)), device_id_type=MESH)
+    pl.semaphore_wait(barrier, n - 1 + hn - 1)
+    copies = _peer_copies("seq", n, lambda p: in_ref.at[p], land, s1, r1)
+    land[me] = in_ref[me]
+    _peer_waits("seq", n, copies, lambda p: in_ref.at[p], land, s1, r1)
+    lane = lax.broadcasted_iota(jnp.int32, (1, width), 1)
+    pick = lane == me // (n // heads)
+    for k in range(n):
+        parts = land[k, rows : rows + 3, :].astype(jnp.float32)
+        grow = jnp.exp(parts[0:1] + parts[1:2] + parts[2:3])
+        factor = jnp.sum(jnp.where(pick, grow, 0.0), axis=1, keepdims=True)
+        scale_out[k] = jnp.broadcast_to(factor, (rows, width))
+    acc = jnp.zeros((rows, width), jnp.float32)
+    for k in range(n):
+        res[k] = acc.astype(res.dtype)
+        acc = scale_out[k] * acc + land[k, :rows, :].astype(jnp.float32)
+    copies = _peer_copies("seq", n, lambda p: res.at[p], land2, s2, r2)
+    land2[me] = res[me]
+    _peer_waits("seq", n, copies, lambda p: res.at[p], land2, s2, r2)
+    out_ref[...] = land2[...]
+    per = n // heads
+    length = c_ref.shape[0]
+    sq = jnp.zeros((length, 1), jnp.float32)
+    sd = jnp.zeros((length, 1), jnp.float32)
+    for h in range(heads):
+        state = land2[h * per : (h + 1) * per].reshape(per * rows, width)
+        hand = jnp.dot(c_ref[...], state, preferred_element_type=jnp.float32)
+        cols = slice(h * width, (h + 1) * width)
+        handed_out[:, cols] = hand
+        mix = base_ref[:, cols] + lift_ref[:, cols] * hand
+        mixed_out[:, cols] = mix
+        gated = mix * gate_ref[:, cols]
+        sq = sq + jnp.sum(gated * gated, axis=1, keepdims=True)
+        sd = sd + jnp.sum(scaled_ref[:, cols] * gated, axis=1, keepdims=True)
+    sq_row = jnp.broadcast_to(sq, (length, length)).T[0:8]
+    sd_row = jnp.broadcast_to(sd, (length, length)).T[0:8]
+    row = lax.broadcasted_iota(jnp.int32, (8, length), 0)
+    mine = jnp.where(row == 0, sq_row, jnp.where(row == 1, sd_row, 0.0))
+    gath[hme] = mine
+    copies = []
+    for i in range(1, hn):
+        peer = lax.rem(hme + i, hn)
+        copy = pltpu.make_async_remote_copy(
+            src_ref=gath.at[hme],
+            dst_ref=gath.at[hme],
+            send_sem=s3.at[i],
+            recv_sem=r3.at[i],
+            device_id=(me, peer),
+            device_id_type=MESH,
+        )
+        copy.start()
+        copies.append(copy)
+    for i in range(1, hn):
+        copies[i - 1].wait_send()
+        src = lax.rem(hme + (hn - i), hn)
+        incoming = pltpu.make_async_remote_copy(
+            src_ref=gath.at[src],
+            dst_ref=gath.at[src],
+            send_sem=s3.at[i],
+            recv_sem=r3.at[i],
+            device_id=(me, src),
+            device_id_type=MESH,
+        )
+        incoming.wait_recv()
+    total = gath[0]
+    for j in range(1, hn):
+        total = total + gath[j]
+    sums_out[...] = total
+
+
+def forward_scan_mix(x, c_rows, base, lift, gate, scaled, heads, cid):
+    n = lax.axis_size("seq")
+    hn = lax.axis_size("head")
+    rows = x.shape[1] - 16
+    piece = (n, rows, 128)
+    length, channels = base.shape
+    vm = pl.BlockSpec(memory_space=pltpu.VMEM)
+    f32 = jnp.float32
+    return pl.pallas_call(
+        functools.partial(forward_kernel, n, hn, heads),
+        out_shape=(
+            jax.ShapeDtypeStruct(piece, x.dtype),
+            jax.ShapeDtypeStruct(piece, f32),
+            jax.ShapeDtypeStruct((length, channels), f32),
+            jax.ShapeDtypeStruct((length, channels), f32),
+            jax.ShapeDtypeStruct((8, length), f32),
+        ),
+        in_specs=[vm] * 6,
+        out_specs=(vm,) * 5,
+        scratch_shapes=[
+            pltpu.VMEM(x.shape, x.dtype),
+            pltpu.VMEM(piece, x.dtype),
+            pltpu.VMEM(piece, x.dtype),
+            pltpu.VMEM((hn, 8, length), f32),
+            pltpu.SemaphoreType.DMA((n,)),
+            pltpu.SemaphoreType.DMA((n,)),
+            pltpu.SemaphoreType.DMA((n,)),
+            pltpu.SemaphoreType.DMA((n,)),
+            pltpu.SemaphoreType.DMA((hn,)),
+            pltpu.SemaphoreType.DMA((hn,)),
+        ],
+        compiler_params=pltpu.CompilerParams(collective_id=cid, has_side_effects=True),
+    )(x, c_rows, base, lift, gate, scaled)
+
+
 INNER = 16384
 
 
@@ -243,7 +360,7 @@
     return pieces.reshape(heads, count * rows // heads, width)
 
 
-def scan_forward(totals, local_state):
+def scan_forward(totals, local_state, c_rows, base, lift, gate, scaled):
     count = lax.axis_size("seq")
     heads, nstate, width = local_state.shape
     pieces = to_pieces(local_state, count)
@@ -254,8 +371,8 @@
     tot_row = jnp.zeros((count, 16, width), jnp.float32)
     tot_row = tot_row.at[:, 0:3, :heads].set(jnp.broadcast_to(parts, (count, 3, heads)))
     sent = jnp.concatenate([pieces, tot_row], axis=1).astype(jnp.bfloat16)
-    back, scales = scan_pieces(sent, "seq", heads, 0)
-    return from_pieces(back, heads).astype(jnp.float32), scales
+    back, scales, mixed, handed, sums = forward_scan_mix(sent, c_rows, base, lift, gate, scaled, heads, 0)
+    return from_pieces(back, heads).astype(jnp.float32), scales, mixed, handed, sums
 
 
 def scan_backward(scales, state_grad):
@@ -313,28 +430,23 @@
     weighted_b = (tail_step[:, :, None] * b_rows.astype(f32)[None]).astype(bf16)
     local_state = jnp.einsum("hsn,shp->hnp", weighted_b, x_heads, preferred_element_type=f32)
 
-    state_exact, weight = scan_forward(totals, local_state)
-    state_low = state_exact.astype(bf16)
-
     between = cumul[:, :, None] - cumul[:, None, :]
     decay = jnp.where(causal[None], jnp.exp(jnp.minimum(between, 0.0)), 0.0)
     mixer_low = (gram[None] * decay * step_size[:, None, :]).astype(bf16)
     intra = jnp.einsum("hts,shp->thp", mixer_low, x_heads, preferred_element_type=f32)
-    handed = jnp.einsum("tn,hnp->thp", c_rows, state_low, preferred_element_type=f32)
     lifted = jnp.exp(cumul)
-    mixed_heads = (
-        intra + lifted.T[:, :, None] * handed + d_skip[None, :, None] * x_heads.astype(f32)
-    )
-    mixed_out = mixed_heads.reshape(length, channels)
-
+    base = (intra + d_skip[None, :, None] * x_heads.astype(f32)).reshape(length, channels)
+    lift_full = jnp.broadcast_to(lifted.T[:, :, None], (length, head_count, width)).reshape(length, channels)
     z_rows = z_input.astype(f32)
     gate_value = jax.nn.silu(z_rows)
+    scaled = grad_out.astype(f32) * rescale_factor
+
+    state_exact, weight, mixed_out, handed_flat, sums = scan_forward(
+        totals, local_state, c_rows, base, lift_full, gate_value, scaled
+    )
+    state_low = state_exact.astype(bf16)
+    handed = handed_flat.reshape(length, head_count, width)
     gated = mixed_out * gate_value
-    scaled = grad_out.astype(f32) * rescale_factor
-    hcount = lax.axis_size("head")
-    own_sums = jnp.stack([jnp.sum(gated * gated, axis=1), jnp.sum(scaled * gated, axis=1)])
-    own_sums = jnp.concatenate([own_sums, jnp.zeros((6, length), f32)], axis=0)
-    sums = jnp.sum(exchange(jnp.broadcast_to(own_sums, (hcount,) + own_sums.shape), "head", 3), axis=0)
     inv_rms = lax.rsqrt(sums[0] / INNER + EPS)
     normed = gated * inv_rms[:, None]
     mean_dot = inv_rms * sums[1] / INNER

time: 126 us -> 127 us (level)
  the two profiles are of different devices: /device:TPU:1 before, /device:TPU:22 now
where the time goes in v7:
time: 127 us; the launch traced here: 126 us
  Pallas kernels  85.3 us (67%)
  other arithmetic  13.3 us (10%)
  local copies, waits for them, and re-layouts  11 us (9%)
  starting transfers between devices  5.83 us (5%)
  matrix products  5.3 us (4%)
  waiting for transfers between devices  4.66 us (4%)
    pallas_call x1, Pallas kernels, forward_scan_mix(): pl.pallas_call(functools.partial(forward_kernel, n, hn, heads), out_shape...  43.6 us
    pallas_call x1, Pallas kernels, scan_pieces(): pl.pallas_call(kern, out_shape=jax.ShapeDtypeStruct(piece, low), in_specs...  27.2 us
    pallas_call x1, Pallas kernels, exchange(): pl.pallas_call(functools.partial(exchange_kernel, axis, n), out_shape=jax...  14.6 us
    ppermute x2, starting transfers between devices, passed_along(): return lax.ppermute(block, axis, route)  5.83 us
    unnamed x34, local copies, waits for them, and re-layouts  4.72 us
    ppermute x2, waiting for transfers between devices, passed_along(): return lax.ppermute(block, axis, route)  4.66 us
  transfers between devices with their start and end apart: 2, of which 1 were waited for; matrix products, arithmetic and copies ran while one was open for 4% of the time, Pallas kernels for 0%

profile of v7, /device:TPU:22, one launch (start us, length us, event | category | flops | bytes accessed | tf_op | source)
XLA Modules:
  0.0 126.4 jit_solution(2728831602773842167)
XLA Ops:
  0.6 0.7 slice.171
  1.4 0.7 slice_bitcast_fusion.6
  2.1 3.4 %collective-permute-start = (bf16[3,1280]{1,0:T(4,128)(2,1)S(1)}, bf16[3,1280]{1,0:T(4,128)(2,1)S(1)}, u32[]{:S(2)}, u32[]{:S(2)}) collective-permute-start(bf16[3,1280]{1,0:T(4,128)(2,1)S(1)} %pad_maximum_fusion.4), channel_id=1, source_target_pairs={{0,16},{16,32},{32,48},{48,64},{64,80},{80,96},{96,112},{112,128},... | collective-permute-start | bytes 23048 | tf_op jit(solution)/shard_map/ppermute | solution.py:321
  5.5 0.6 copy-done.9
  6.3 0.3 reduce_window_sum.17
  6.5 0.2 slice_reduce_fusion
  6.8 0.6 copy-done.11
  7.5 0.7 copy-done.13
  8.1 0.7 copy-done.8
  8.8 2.2 %convert_multiply_fusion.1 = (f32[128,1024]{1,0:T(8,128)}, f32[128,1024]{1,0:T(8,128)}) fusion(bf16[128,1024]{1,0:T(8,128)(2,1)} %param.17, f32[1024]{0:T(1024)S(1)} %copy-done.8, bf16[128,1024]{1,0:T(8,128)(2,1)} %param.26), kind=kLoop, calls=%fused_computation.19 | loop fusion | flops 917504 | bytes 1576960 | tf_op jit(solution)/shard_map/jit(silu)/mul | solution.py:441
  11.1 0.2 broadcast_in_dim.22
  11.3 0.9 copy.115
  12.4 0.6 fusion.58
  13.4 0.3 multiply_convert_fusion.3
  13.8 0.2 copy.66
  14.0 0.4 copy-done.15
  14.5 0.4 fusion
  14.8 1.0 copy.91.refs_2_
  15.9 0.2 convolution_convert_fusion.1
  16.1 0.8 pad_maximum_fusion.1.refs_0_
  16.9 43.6 %shard_map.147 = (bf16[32,32,128]{2,1,0:T(8,128)(2,1)}, f32[32,32,128]{2,1,0:T(8,128)}, f32[128,1024]{1,0:T(8,128)}, f32[128,1024]{1,0:T(8,128)}, f32[8,128]{1,0:T(8,128)}) custom-call(bf16[32,48,128]{2,1,0:T(8,128)(2,1)} %pad_maximum_fusion.1.refs_0_, bf16[128,128]{1,0:T(8,128)(2,1)} %get-tuple-element.53.refs_1_, f32[128,1024]{1,0:T(8,128)} %copy.91.refs_2_, ...), custom_call_target="tpu_custom_call" | custom-call | tf_op jit(solution)/shard_map/pallas_call | solution.py:284
  60.5 0.8 fusion.53
  61.2 0.7 rsqrt_bitcast_fusion
  61.9 2.1 %fusion.21 = (bf16[128,1024]{1,0:T(8,128)(2,1)}, bf16[128,1024]{1,0:T(8,128)(2,1)S(1)}) fusion(bf16[128,1024]{1,0:T(8,128)(2,1)S(1)} %copy-done.1, f32[128,1024]{1,0:T(8,128)} %get-tuple-element.34, f32[128]{0:T(128)S(1)} %fusion.53, f32[128]{0:T(128)S(1)} %rsqrt_bitcast_fusion, f32[1024]{0:T(1024)S(1)} %copy-done.8, bf16[128,1024]{1,0:T(8,128)(2,1)S(1)} %copy-done.2), kind=kLoop, calls=%fused_computation.40 | loop fusion | flops 2752512 | bytes 1577984 | tf_op jit(solution)/shard_map/convert_element_type | solution.py:454
  64.2 0.6 multiply_reduce_fusion.4
  64.8 1.3 %convolution_convert_fusion = bf16[8,128,128]{2,1,0:T(8,128)(2,1)} fusion(bf16[128,8,128]{0,2,1:T(8,128)(2,1)S(1)} %bitcast.138, f32[128,128]{1,0:T(8,128)S(1)} %get-tuple-element.52, f32[8,128]{1,0:T(8,128)S(1)} %get-tuple-element.61), kind=kOutput, calls=%fused_computation.9 | convolution fusion | flops 33947648 | bytes 593920 | tf_op jit(solution)/shard_map/htn,thp->hnp/dot_general | solution.py:459
  66.0 27.2 %shard_map.148 = bf16[32,32,128]{2,1,0:T(8,128)(2,1)} custom-call(bf16[32,32,128]{2,1,0:T(8,128)(2,1)} %bitcast.148, f32[32,32,128]{2,1,0:T(8,128)} %get-tuple-element.35.refs_1_), custom_call_target="tpu_custom_call" | custom-call | tf_op jit(solution)/shard_map/pallas_call | solution.py:184
  93.2 1.3 %multiply_reduce_fusion.1 = (f32[8,128]{1,0:T(8,128)S(1)}, f32[128,128]{0,1:T(8,128)S(1)}) fusion(f32[128,128]{0,1:T(8,128)S(1)} %copy.64, f32[8,128]{1,0:T(8,128)S(1)} %get-tuple-element.63, bf16[8,128,128]{2,1,0:T(8,128)(2,1)} %bitcast.141, bf16[128,1024]{1,0:T(8,128)(2,1)S(1)} %get-tuple-element.44), kind=kOutput, calls=%fused_computation.52 | convolution fusion | flops 34061312 | bytes 663552 | tf_op jit(solution)/shard_map/shp,hnp->hsn/dot_general | solution.py:467
  94.6 0.3 convolution_bitcast_fusion
  94.9 0.6 copy-done.5
  95.5 0.3 multiply_reduce_fusion
  96.1 0.2 copy.93
  96.8 0.3 reduce_window_sum.18
  97.3 0.3 fusion.3
  97.6 0.2 fusion.5
  98.2 1.0 gather_fusion
  99.2 0.7 copy.83
  99.9 14.6 %shard_map.149 = f32[16,32,128]{2,1,0:T(8,128)} custom-call(f32[16,32,128]{2,1,0:T(8,128)} %bitcast.146), custom_call_target="tpu_custom_call" | custom-call | tf_op jit(solution)/shard_map/pallas_call | solution.py:55
  114.5 1.0 reduce_sum.113
  115.5 0.4 fusion.2
  115.9 0.2 copy.92
  116.1 0.2 multiply_multiply_fusion
  116.4 2.4 %collective-permute-start.1 = (f32[3,1280]{1,0:T(4,128)S(1)}, f32[3,1280]{1,0:T(4,128)S(1)}, u32[]{:S(2)}, u32[]{:S(2)}) collective-permute-start(f32[3,1280]{1,0:T(4,128)S(1)} %pad_maximum_fusion.3), channel_id=1, source_target_pairs={{16,0},{32,16},{48,32},{64,48},{80,64},{96,80},{112,96},{128,112},... | collective-permute-start | bytes 46088 | tf_op jit(solution)/shard_map/ppermute | solution.py:321
  118.8 0.7 divide_multiply_fusion
  119.5 4.7 %collective-permute-done.1 = f32[3,1280]{1,0:T(4,128)S(1)} collective-permute-done((f32[3,1280]{1,0:T(4,128)S(1)}, f32[3,1280]{1,0:T(4,128)S(1)}, u32[]{:S(2)}, u32[]{:S(2)}) %collective-permute-start.1) | collective-permute-done | bytes 15392 | tf_op jit(solution)/shard_map/ppermute | solution.py:321
  124.2 0.7 maximum_select_fusion
  124.9 0.6 fusion.45
  125.5 0.9 fusion.11
  (70 shorter events, 2.4 us)
Async XLA Ops:
  2.1 3.5 %copy-start.14 = (f32[8]{0:T(128)S(1)}, f32[8]{0:T(128)}, u32[]{:S(2)}) copy-start(f32[8]{0:T(128)} %param.21) | copy-start | bytes 100
  2.1 10.2 %collective-permute-start = (bf16[3,1280]{1,0:T(4,128)(2,1)S(1)}, bf16[3,1280]{1,0:T(4,128)(2,1)S(1)}, u32[]{:S(2)}, u32[]{:S(2)}) collective-permute-start(bf16[3,1280]{1,0:T(4,128)(2,1)S(1)} %pad_maximum_fusion.4), channel_id=1, source_target_pairs={{0,16},{16,32},{32,48},{48,64},{64,80},{80,96},{96,112},{112,128},... | collective-permute-start | bytes 23048 | tf_op jit(solution)/shard_map/ppermute | solution.py:321
  5.5 0.7 copy-start.9
  5.5 0.7 copy-start.12
  6.7 0.7 copy-start.10
  6.8 0.7 copy-start.11
  7.5 0.7 copy-start.13
  8.1 0.7 copy-start.8
  11.3 0.9 copy-start.7
  12.4 1.0 copy-start.4
  13.8 0.7 copy-start.15
  16.9 45.0 %copy-start.1 = (bf16[128,1024]{1,0:T(8,128)(2,1)S(1)}, bf16[128,1024]{1,0:T(8,128)(2,1)}, u32[]{:S(2)}) copy-start(bf16[128,1024]{1,0:T(8,128)(2,1)} %param.17) | copy-start | bytes 786436
  16.9 45.0 %copy-start.2 = (bf16[128,1024]{1,0:T(8,128)(2,1)S(1)}, bf16[128,1024]{1,0:T(8,128)(2,1)}, u32[]{:S(2)}) copy-start(bf16[128,1024]{1,0:T(8,128)(2,1)} %param.26) | copy-start | bytes 786436
  93.2 1.3 %copy-start = (bf16[32,32,128]{2,1,0:T(8,128)(2,1)S(1)}, bf16[32,32,128]{2,1,0:T(8,128)(2,1)}, u32[]{:S(2)}) copy-start(bf16[32,32,128]{2,1,0:T(8,128)(2,1)} %shard_map.148) | copy-start | bytes 786436
  94.6 1.0 copy-start.5
  94.6 1.6 %copy-start.3 = (f32[128,1024]{1,0:T(8,128)S(1)}, f32[128,1024]{1,0:T(8,128)}, u32[]{:S(2)}) copy-start(f32[128,1024]{1,0:T(8,128)} %get-tuple-element.37) | copy-start | bytes 1572868
  115.5 4.0 %copy-start.6 = (f32[2,11,128]{2,1,0:T(8,128)}, f32[2,11,128]{2,1,0:T(8,128)S(1)}, u32[]{:S(2)}) copy-start(f32[2,11,128]{2,1,0:T(8,128)S(1)} %slice_multiply_fusion.8) | copy-start | bytes 33796
  116.4 7.8 %collective-permute-start.1 = (f32[3,1280]{1,0:T(4,128)S(1)}, f32[3,1280]{1,0:T(4,128)S(1)}, u32[]{:S(2)}, u32[]{:S(2)}) collective-permute-start(f32[3,1280]{1,0:T(4,128)S(1)} %pad_maximum_fusion.3), channel_id=1, source_target_pairs={{16,0},{32,16},{48,32},{64,48},{80,64},{96,80},{112,96},{128,112},... | collective-permute-start | bytes 46088 | tf_op jit(solution)/shard_map/ppermute | solution.py:321
  119.5 4.7 %slice-start = ((f32[2,11,128]{2,1,0:T(8,128)}), f32[2,8,128]{2,1,0:T(8,128)S(1)}, s32[]{:S(2)}) async-start(f32[2,11,128]{2,1,0:T(8,128)} %copy-done.6), calls=%async_computation | async-start | bytes 16384 | tf_op jit(solution)/shard_map/slice | solution.py:528

commit v8 on v6

--- a/solution.py
+++ b/solution.py
@@ -191,6 +191,85 @@
     )(x, scales)
 
 
+def tail_kernel(n, hn, in_ref, rim_ref, out_ref, rim_out, land, send, rim_land, s1, r1, s2, r2):
+    me = lax.axis_index("seq")
+    hme = lax.axis_index("head")
+    prev = lax.rem(me + n - 1, n)
+    nxt = lax.rem(me + 1, n)
+    barrier = pltpu.get_barrier_semaphore()
+    for i in range(1, hn):
+        pl.semaphore_signal(barrier, inc=1, device_id=(me, lax.rem(hme + i, hn)), device_id_type=MESH)
+    pl.semaphore_signal(barrier, inc=1, device_id=(prev, hme), device_id_type=MESH)
+    pl.semaphore_signal(barrier, inc=1, device_id=(nxt, hme), device_id_type=MESH)
+    pl.semaphore_wait(barrier, hn + 1)
+    rim_copy = pltpu.make_async_remote_copy(
+        src_ref=rim_ref, dst_ref=rim_land, send_sem=s2.at[0], recv_sem=r2.at[0],
+        device_id=(prev, hme), device_id_type=MESH,
+    )
+    rim_copy.start()
+    send[...] = in_ref[...]
+    rim_copy.wait_send()
+    rim_copy.wait_recv()
+    keep = (1 - me // (n - 1)).astype(jnp.float32)
+    rows = in_ref.shape[1] // 2
+    nst = in_ref.shape[2]
+    width = rim_ref.shape[1] - nst
+    rim_bc = rim_land[0:8, width:] * keep
+    last = hn - 1
+    send[last, 8:11, :] = send[last, 8:11, :] + rim_bc[0:3]
+    send[last, rows + 8 : rows + 11, :] = send[last, rows + 8 : rows + 11, :] + rim_bc[3:6]
+    rim_out[...] = rim_land[0:8, 0:width] * keep
+    src_of = lambda p: send.at[p]
+    copies = []
+    for i in range(1, hn):
+        peer = lax.rem(hme + i, hn)
+        copy = pltpu.make_async_remote_copy(
+            src_ref=send.at[peer], dst_ref=land.at[hme], send_sem=s1.at[i], recv_sem=r1.at[i],
+            device_id=(me, peer), device_id_type=MESH,
+        )
+        copy.start()
+        copies.append(copy)
+    land[hme] = send[hme]
+    for i in range(1, hn):
+        copies[i - 1].wait_send()
+        src = lax.rem(hme + (hn - i), hn)
+        incoming = pltpu.make_async_remote_copy(
+            src_ref=send.at[src], dst_ref=land.at[src], send_sem=s1.at[i], recv_sem=r1.at[i],
+            device_id=(me, src), device_id_type=MESH,
+        )
+        incoming.wait_recv()
+    total = land[0]
+    for j in range(1, hn):
+        total = total + land[j]
+    out_ref[...] = total
+
+
+def tail_exchange(pieces, rim, cid):
+    n = lax.axis_size("seq")
+    hn = lax.axis_size("head")
+    vm = pl.BlockSpec(memory_space=pltpu.VMEM)
+    width = rim.shape[1] - pieces.shape[2]
+    return pl.pallas_call(
+        functools.partial(tail_kernel, n, hn),
+        out_shape=(
+            jax.ShapeDtypeStruct(pieces.shape[1:], jnp.float32),
+            jax.ShapeDtypeStruct((8, width), jnp.float32),
+        ),
+        in_specs=[vm, vm],
+        out_specs=(vm, vm),
+        scratch_shapes=[
+            pltpu.VMEM(pieces.shape, jnp.float32),
+            pltpu.VMEM(pieces.shape, jnp.float32),
+            pltpu.VMEM(rim.shape, jnp.float32),
+            pltpu.SemaphoreType.DMA((hn,)),
+            pltpu.SemaphoreType.DMA((hn,)),
+            pltpu.SemaphoreType.DMA((1,)),
+            pltpu.SemaphoreType.DMA((1,)),
+        ],
+        compiler_params=pltpu.CompilerParams(collective_id=cid, has_side_effects=True),
+    )(pieces, rim)
+
+
 INNER = 16384
 
 
@@ -394,28 +473,22 @@
     picks = []
     for h in range(hcount):
         own = [h * row_share + i for i in range(row_share + 3)]
-        own = [r if r < length else 0 for r in own]
-        picks.append(own + [0, 1, 2] + [0] * (16 - row_share - 6))
+        own = [r if r < length else length for r in own]
+        picks.append(own + [length] * (16 - row_share - 3))
     picks = jnp.array(picks, jnp.int32)
     piece_rows = picks.shape[1]
-    bc_pieces = jnp.moveaxis(jnp.take(grad_bc_rows, picks.reshape(-1), axis=1).reshape(2, hcount, piece_rows, -1), 1, 0)
-    bc_got = exchange(bc_pieces.reshape(hcount, 2 * piece_rows, -1), "head", 2)
-    grad_bc_mine = jnp.sum(bc_got, axis=0).reshape(2, piece_rows, -1)
+    bc_rows_z = jnp.concatenate([grad_bc_rows, jnp.zeros((2, 1, nstate), f32)], axis=1)
+    bc_pieces = jnp.moveaxis(jnp.take(bc_rows_z, picks.reshape(-1), axis=1).reshape(2, hcount, piece_rows, -1), 1, 0)
+    top = (grad_bc_rows[:, :3] * silu_grad(bc_pre[:, :3])).reshape(6, nstate)
+    rim_send = jnp.zeros((8, channels + nstate), f32)
+    rim_send = rim_send.at[0:3, :channels].set(grad_x_pre[:3]).at[0:6, channels:].set(top)
+    summed, rim_got = tail_exchange(bc_pieces.reshape(hcount, 2 * piece_rows, -1), rim_send, 2)
+    grad_bc_mine = summed.reshape(2, piece_rows, -1)[:, : row_share + 3]
     bc_pre_pad = jnp.concatenate([bc_pre, jnp.zeros((2, 3, nstate), f32)], axis=1)
     bc_pre_mine = lax.dynamic_slice_in_dim(bc_pre_pad, first_row, row_share + 3, 1)
-    grad_bc_pre = grad_bc_mine[:, : row_share + 3] * silu_grad(bc_pre_mine)
-    grad_bc_top = grad_bc_mine[:, row_share + 3 : row_share + 6] * silu_grad(bc_pre[:, :3])
-    rows_first = jnp.concatenate(
-        [grad_x_pre[:3], jnp.moveaxis(grad_bc_top, 0, 1).reshape(3, 2 * nstate)], axis=1
-    )
-    rows_next = passed_along(rows_first, "seq", -1)
-    rim_x = rows_next[:, :channels]
-    rim_bc = jnp.moveaxis(rows_next[:, channels:].reshape(3, 2, nstate), 0, 1)
-    grad_bc_ext = jnp.where(
-        hidx == hcount - 1,
-        jnp.concatenate([grad_bc_pre[:, :row_share], rim_bc], axis=1),
-        grad_bc_pre,
-    )
+    in_rim = (hidx == hcount - 1) & (jnp.arange(row_share + 3) >= row_share)
+    grad_bc_ext = grad_bc_mine * jnp.where(in_rim[None, :, None], 1.0, silu_grad(bc_pre_mine))
+    rim_x = rim_got[:3]
     grad_x = conv_back(jnp.concatenate([grad_x_pre, rim_x], axis=0), conv_x).astype(bf16)
     grad_bc = conv_back(grad_bc_ext, convolution_bc_taps).astype(bf16)
     grad_dt = grad_steps * jax.nn.sigmoid(dt_raw + dt_bias[:, None])

time: 126 us -> 128 us (1.016)
  local copies, waits for them, and re-layouts: 10.5 us -> 13.8 us
  waiting for transfers between devices: 2.58 us -> 0.01 us
  Pallas kernels: 89.5 us -> 91.4 us
  other arithmetic: 10.3 us -> 12.1 us
  starting transfers between devices: 5.24 us -> 3.95 us
    pallas_call x2 -> x1, Pallas kernels: 39.2 us -> 20.2 us  [exchange(): pl.pallas_call(functools.partial(exchange_kernel, axis, n), out_shape=jax...]
    pallas_call x0 -> x1, Pallas kernels: none -> 17.1 us  [tail_exchange(): pl.pallas_call(functools.partial(tail_kernel, n, hn), out_shape=(jax.Shap...]
    pallas_call x1, Pallas kernels: 22 us -> 25.5 us  [scan_pieces(): pl.pallas_call(kern, out_shape=jax.ShapeDtypeStruct(piece, low), in_specs...]
    another operation x1 -> x4, other arithmetic: 0.01 us -> 2.7 us
    ppermute x2 -> x1, waiting for transfers between devices: 2.58 us -> 0.01 us  [passed_along(): return lax.ppermute(block, axis, route)]
    scatter x0 -> x2, local copies, waits for them, and re-layouts: none -> 1.69 us  [shards(): rim_send.at[0:3, :channels].set(grad_x_pre[:3]).at[0:6, channels:].set(top)]
    ppermute x2 -> x1, starting transfers between devices: 5.24 us -> 3.95 us  [passed_along(): return lax.ppermute(block, axis, route)]
    unnamed x30 -> x35, local copies, waits for them, and re-layouts: 3.82 us -> 4.81 us
  transfers between devices with their start and end apart: 2 -> 1, of which waited for: 1 -> 0; matrix products, arithmetic and copies ran while one was open for 1% -> 2% of each run, Pallas kernels for 0% -> 0%
where the time goes in v8:
time: 128 us; the launch traced here: 127 us
  Pallas kernels  91.4 us (71%)
  local copies, waits for them, and re-layouts  13.8 us (11%)
  other arithmetic  12.1 us (9%)
  matrix products  4.48 us (4%)
  starting transfers between devices  3.95 us (3%)
    pallas_call x1, Pallas kernels, scan_pieces(): pl.pallas_call(kern, out_shape=(jax.ShapeDtypeStruct(piece, low), jax.Sha...  28.6 us
    pallas_call x1, Pallas kernels, scan_pieces(): pl.pallas_call(kern, out_shape=jax.ShapeDtypeStruct(piece, low), in_specs...  25.5 us
    pallas_call x1, Pallas kernels, exchange(): pl.pallas_call(functools.partial(exchange_kernel, axis, n), out_shape=jax...  20.2 us
    pallas_call x1, Pallas kernels, tail_exchange(): pl.pallas_call(functools.partial(tail_kernel, n, hn), out_shape=(jax.Shap...  17.1 us
    unnamed x35, local copies, waits for them, and re-layouts  4.81 us
    ppermute x1, starting transfers between devices, passed_along(): return lax.ppermute(block, axis, route)  3.95 us
    another operation x4, other arithmetic  2.7 us
  transfers between devices with their start and end apart: 1, of which 0 were waited for; matrix products, arithmetic and copies ran while one was open for 2% of the time, Pallas kernels for 0%

profile of v8, /device:TPU:1, one launch (start us, length us, event | category | flops | bytes accessed | tf_op | source)
XLA Modules:
  0.0 126.8 jit_solution(11970144445062833615)
XLA Ops:
  0.6 0.7 slice.209
  1.4 0.7 slice_bitcast_fusion.8
  2.1 3.9 %collective-permute-start = (bf16[3,1280]{1,0:T(4,128)(2,1)S(1)}, bf16[3,1280]{1,0:T(4,128)(2,1)S(1)}, u32[]{:S(2)}, u32[]{:S(2)}) collective-permute-start(bf16[3,1280]{1,0:T(4,128)(2,1)S(1)} %pad_maximum_fusion.3), channel_id=1, source_target_pairs={{0,16},{16,32},{32,48},{48,64},{64,80},{80,96},{96,112},{112,128},... | collective-permute-start | bytes 23048 | tf_op jit(solution)/shard_map/ppermute | solution.py:283
  6.1 0.6 copy-done.14
  6.7 0.6 copy-done.12
  7.4 0.3 reduce_window_sum.17
  7.7 0.2 slice_reduce_fusion
  8.1 0.6 fusion.62
  8.7 0.7 and_reduce_fusion
  10.0 0.7 copy-done.4
  10.7 0.3 multiply_convert_fusion.4
  11.2 0.3 convolution_convert_fusion.1
  11.6 0.8 pad_maximum_fusion.1.refs_0_
  12.4 28.6 %shard_map.147 = (bf16[32,32,128]{2,1,0:T(8,128)(2,1)}, f32[32,32,128]{2,1,0:T(8,128)}) custom-call(bf16[32,48,128]{2,1,0:T(8,128)(2,1)} %pad_maximum_fusion.1.refs_0_), custom_call_target="tpu_custom_call" | custom-call | tf_op jit(solution)/shard_map/pallas_call | solution.py:176
  41.0 1.1 copy.63
  42.1 0.2 fusion.40
  42.4 0.6 copy-done.15
  43.0 0.4 fusion.1
  43.4 0.2 copy.85
  43.6 0.7 copy-done.2
  44.4 0.3 multiply_reduce_fusion.5
  44.8 0.6 broadcast_in_dim.33.in_ref
  45.5 20.2 %shard_map.148 = f32[16,8,128]{2,1,0:T(8,128)} custom-call(f32[16,8,128]{2,1,0:T(8,128)} %broadcast_in_dim.33.in_ref), custom_call_target="tpu_custom_call" | custom-call | tf_op jit(solution)/shard_map/pallas_call | solution.py:55
  65.7 0.9 reduce_sum.130
  66.5 1.1 fusion.22
  67.9 0.5 multiply_reduce_fusion.6
  68.4 0.4 copy-done.1
  68.8 0.3 fusion.4
  69.2 1.3 %convolution_convert_fusion = bf16[8,128,128]{2,1,0:T(8,128)(2,1)} fusion(bf16[128,8,128]{0,2,1:T(8,128)(2,1)S(1)} %bitcast.119, f32[128,128]{1,0:T(8,128)S(1)} %get-tuple-element.76, f32[8,128]{1,0:T(8,128)S(1)} %get-tuple-element.84), kind=kOutput, calls=%fused_computation.10 | convolution fusion | flops 33947648 | bytes 593920 | tf_op jit(solution)/shard_map/htn,thp->hnp/dot_general | solution.py:426
  70.4 25.5 %shard_map.149 = bf16[32,32,128]{2,1,0:T(8,128)(2,1)} custom-call(bf16[32,32,128]{2,1,0:T(8,128)(2,1)} %bitcast.134, f32[32,32,128]{2,1,0:T(8,128)} %get-tuple-element.57.refs_1_), custom_call_target="tpu_custom_call" | custom-call | tf_op jit(solution)/shard_map/pallas_call | solution.py:184
  95.9 1.3 %multiply_reduce_fusion = f32[32]{0:T(128)S(1)} fusion(bf16[32,32,128]{2,1,0:T(8,128)(2,1)S(1)} %copy-done.1, bf16[32,32,128]{2,1,0:T(8,128)(2,1)} %shard_map.149), kind=kLoop, calls=%fused_computation.51 | loop fusion | flops 524256 | bytes 524416 | tf_op jit(solution)/shard_map/reduce_sum | solution.py:440
  97.3 0.2 multiply_reduce_fusion.1
  97.5 0.3 convolution_bitcast_fusion
  98.5 0.3 reduce_window_sum.18
  99.0 0.3 fusion.6
  99.5 0.4 fusion.3
  99.9 0.2 copy.86
  100.1 0.2 multiply_multiply_fusion
  100.5 1.0 gather_fusion
  101.4 0.7 copy.79
  102.2 2.0 %fusion.48 = f32[6,128]{1,0:T(8,128)S(1)} fusion(f32[6,128]{1,0:T(8,128)S(1)} %reshape.303, s32[]{:T(128)} %bitcast.37, s32[]{:T(128)} %bitcast.38, f32[3,1024]{1,0:T(4,128)S(1)} %slice.262, pred[]{:T(512)} %and_reduce_fusion), kind=kLoop, calls=%fused_computation.118 | loop fusion | flops 768 | bytes 18441 | tf_op jit(solution)/shard_map/select.6
  104.2 1.7 %scatter.20.rim_ref = f32[8,1152]{1,0:T(8,128)S(1)} dynamic-update-slice(f32[8,1152]{1,0:T(8,128)S(1)} %scatter.19, f32[6,128]{1,0:T(8,128)S(1)} %fusion.48, s32[]{:T(128)} %bitcast.37, s32[]{:T(128)} %bitcast.38) | dynamic-update-slice | bytes 6148 | tf_op jit(solution)/shard_map/scatter | solution.py:484
  105.9 0.6 copy-done.5
  106.4 17.1 %shard_map.150 = (f32[32,128]{1,0:T(8,128)}, f32[8,1024]{1,0:T(8,128)}) custom-call(f32[16,32,128]{2,1,0:T(8,128)} %bitcast.132, f32[8,1152]{1,0:T(8,128)} %copy-done.5), custom_call_target="tpu_custom_call" | custom-call | tf_op jit(solution)/shard_map/pallas_call | solution.py:252
  123.6 0.8 slice_multiply_fusion.8
  124.4 0.6 fusion.42
  125.2 0.9 fusion.12
  126.1 0.7 divide_multiply_fusion
  (76 shorter events, 3.0 us)
Async XLA Ops:
  2.1 7.5 %collective-permute-start = (bf16[3,1280]{1,0:T(4,128)(2,1)S(1)}, bf16[3,1280]{1,0:T(4,128)(2,1)S(1)}, u32[]{:S(2)}, u32[]{:S(2)}) collective-permute-start(bf16[3,1280]{1,0:T(4,128)(2,1)S(1)} %pad_maximum_fusion.3), channel_id=1, source_target_pairs={{0,16},{16,32},{32,48},{48,64},{64,80},{80,96},{96,112},{112,128},... | collective-permute-start | bytes 23048 | tf_op jit(solution)/shard_map/ppermute | solution.py:283
  6.0 0.7 copy-start.14
  6.0 0.7 copy-start.8
  6.7 0.7 copy-start.12
  7.3 0.7 copy-start.11
  7.3 0.7 copy-start.9
  7.4 2.2 %copy-start.6 = (bf16[2,128,128]{2,1,0:T(8,128)(2,1)S(1)}, bf16[2,128,128]{2,1,0:T(8,128)(2,1)}, u32[]{:S(2)}) copy-start(bf16[2,128,128]{2,1,0:T(8,128)(2,1)} %param.22) | copy-start | bytes 196612
  8.1 0.7 copy-start.16
  8.7 0.7 copy-start.13
  9.7 1.0 copy-start.4
  42.3 0.7 copy-start.15
  43.4 1.0 copy-start.2
  43.4 1.0 copy-start.3
  43.4 1.0 copy-start.7
  67.9 1.0 copy-start.1
  95.9 1.4 %copy-start = (bf16[32,32,128]{2,1,0:T(8,128)(2,1)S(1)}, bf16[32,32,128]{2,1,0:T(8,128)(2,1)}, u32[]{:S(2)}) copy-start(bf16[32,32,128]{2,1,0:T(8,128)(2,1)} %shard_map.149) | copy-start | bytes 786436
  105.8 0.6 copy-start.5
  124.4 0.8 copy-start.10

commit v9 on v8

--- a/solution.py
+++ b/solution.py
@@ -330,8 +330,8 @@
     rest = totals - high
     middle = lax.reduce_precision(rest, exponent_bits=8, mantissa_bits=7)
     parts = jnp.stack([high, middle, rest - middle])
-    tot_row = jnp.zeros((count, 16, width), jnp.float32)
-    tot_row = tot_row.at[:, 0:3, :heads].set(jnp.broadcast_to(parts, (count, 3, heads)))
+    tot_row = jnp.pad(parts, ((0, 13), (0, width - heads)))
+    tot_row = jnp.broadcast_to(tot_row, (count, 16, width))
     sent = jnp.concatenate([pieces, tot_row], axis=1).astype(jnp.bfloat16)
     back, scales = scan_pieces(sent, "seq", heads, 0)
     return from_pieces(back, heads).astype(jnp.float32), scales
@@ -480,8 +480,9 @@
     bc_rows_z = jnp.concatenate([grad_bc_rows, jnp.zeros((2, 1, nstate), f32)], axis=1)
     bc_pieces = jnp.moveaxis(jnp.take(bc_rows_z, picks.reshape(-1), axis=1).reshape(2, hcount, piece_rows, -1), 1, 0)
     top = (grad_bc_rows[:, :3] * silu_grad(bc_pre[:, :3])).reshape(6, nstate)
-    rim_send = jnp.zeros((8, channels + nstate), f32)
-    rim_send = rim_send.at[0:3, :channels].set(grad_x_pre[:3]).at[0:6, channels:].set(top)
+    rim_send = jnp.concatenate(
+        [jnp.pad(grad_x_pre[:3], ((0, 5), (0, 0))), jnp.pad(top, ((0, 2), (0, 0)))], axis=1
+    )
     summed, rim_got = tail_exchange(bc_pieces.reshape(hcount, 2 * piece_rows, -1), rim_send, 2)
     grad_bc_mine = summed.reshape(2, piece_rows, -1)[:, : row_share + 3]
     bc_pre_pad = jnp.concatenate([bc_pre, jnp.zeros((2, 3, nstate), f32)], axis=1)

time: 128 us -> 123 us (0.961)
  local copies, waits for them, and re-layouts: 13.8 us -> 11.3 us
  other arithmetic: 12.1 us -> 10.1 us
    pallas_call x1, Pallas kernels: 25.5 us -> 22.1 us  [scan_pieces(): pl.pallas_call(kern, out_shape=jax.ShapeDtypeStruct(piece, low), in_specs...]
    another operation x4 -> x1, other arithmetic: 2.7 us -> 0.01 us
    pallas_call x1, Pallas kernels: 17.1 us -> 19 us  [tail_exchange(): pl.pallas_call(functools.partial(tail_kernel, n, hn), out_shape=(jax.Shap...]
    pallas_call x1, Pallas kernels: 20.2 us -> 22 us  [exchange(): pl.pallas_call(functools.partial(exchange_kernel, axis, n), out_shape=jax...]
    scatter x3 -> x0, local copies, waits for them, and re-layouts: 1.71 us -> none  [the longest x2 1.69 us: shards(): rim_send.at[0:3, :channels].set(grad_x_pre[:3]).at[0:6, channels:].set(top)]
    unnamed x35 -> x33, local copies, waits for them, and re-layouts: 4.81 us -> 4.61 us
  transfers between devices with their start and end apart: 1 -> 1, of which waited for: 0 -> 0; matrix products, arithmetic and copies ran while one was open for 2% -> 1% of each run, Pallas kernels for 0% -> 0%
where the time goes in v9:
time: 123 us; the launch traced here: 122 us
  Pallas kernels  91.3 us (74%)
  local copies, waits for them, and re-layouts  11.3 us (9%)
  other arithmetic  10.1 us (8%)
  matrix products  4.49 us (4%)
  starting transfers between devices  3.95 us (3%)
    pallas_call x1, Pallas kernels, scan_pieces(): pl.pallas_call(kern, out_shape=(jax.ShapeDtypeStruct(piece, low), jax.Sha...  28.2 us
    pallas_call x1, Pallas kernels, scan_pieces(): pl.pallas_call(kern, out_shape=jax.ShapeDtypeStruct(piece, low), in_specs...  22.1 us
    pallas_call x1, Pallas kernels, exchange(): pl.pallas_call(functools.partial(exchange_kernel, axis, n), out_shape=jax...  22 us
    pallas_call x1, Pallas kernels, tail_exchange(): pl.pallas_call(functools.partial(tail_kernel, n, hn), out_shape=(jax.Shap...  19 us
    unnamed x33, local copies, waits for them, and re-layouts  4.61 us
    ppermute x1, starting transfers between devices, passed_along(): return lax.ppermute(block, axis, route)  3.95 us
  transfers between devices with their start and end apart: 1, of which 0 were waited for; matrix products, arithmetic and copies ran while one was open for 1% of the time, Pallas kernels for 0%

profile of v9, /device:TPU:1, one launch (start us, length us, event | category | flops | bytes accessed | tf_op | source)
XLA Modules:
  0.0 122.2 jit_solution(11917442876681465895)
XLA Ops:
  0.6 0.7 slice.139
  1.4 0.7 slice_bitcast_fusion.8
  2.1 3.9 %collective-permute-start = (bf16[3,1280]{1,0:T(4,128)(2,1)S(1)}, bf16[3,1280]{1,0:T(4,128)(2,1)S(1)}, u32[]{:S(2)}, u32[]{:S(2)}) collective-permute-start(bf16[3,1280]{1,0:T(4,128)(2,1)S(1)} %pad_maximum_fusion.3), channel_id=1, source_target_pairs={{0,16},{16,32},{32,48},{48,64},{64,80},{80,96},{96,112},{112,128},... | collective-permute-start | bytes 23048 | tf_op jit(solution)/shard_map/ppermute | solution.py:283
  6.1 0.6 copy-done.14
  6.8 0.3 reduce_window_sum.17
  7.1 0.2 slice_reduce_fusion
  7.5 0.7 copy-done.12
  8.7 0.7 copy-done.4
  9.4 0.3 multiply_convert_fusion.4
  9.8 0.2 copy.88
  9.9 0.3 convolution_convert_fusion.1
  10.3 0.8 pad_maximum_fusion.1.refs_0_
  11.0 28.2 %shard_map.147 = (bf16[32,32,128]{2,1,0:T(8,128)(2,1)}, f32[32,32,128]{2,1,0:T(8,128)}) custom-call(bf16[32,48,128]{2,1,0:T(8,128)(2,1)} %pad_maximum_fusion.1.refs_0_), custom_call_target="tpu_custom_call" | custom-call | tf_op jit(solution)/shard_map/pallas_call | solution.py:176
  39.3 1.1 copy.63
  40.4 0.2 fusion.40
  40.7 0.6 copy-done.15
  41.3 0.4 fusion.1
  41.7 0.2 copy.85
  41.9 0.7 copy-done.2
  42.7 0.3 multiply_reduce_fusion.5
  43.1 0.6 broadcast_in_dim.36.in_ref
  43.8 22.0 %shard_map.148 = f32[16,8,128]{2,1,0:T(8,128)} custom-call(f32[16,8,128]{2,1,0:T(8,128)} %broadcast_in_dim.36.in_ref), custom_call_target="tpu_custom_call" | custom-call | tf_op jit(solution)/shard_map/pallas_call | solution.py:55
  65.8 0.9 reduce_sum.130
  66.6 1.1 fusion.22
  67.7 0.2 copy.89
  68.0 0.5 multiply_reduce_fusion.6
  68.5 0.4 copy-done.1
  68.9 0.3 fusion.4
  69.3 1.3 %convolution_convert_fusion = bf16[8,128,128]{2,1,0:T(8,128)(2,1)} fusion(bf16[128,8,128]{0,2,1:T(8,128)(2,1)S(1)} %bitcast.117, f32[128,128]{1,0:T(8,128)S(1)} %get-tuple-element.40, f32[8,128]{1,0:T(8,128)S(1)} %get-tuple-element.48), kind=kOutput, calls=%fused_computation.10 | convolution fusion | flops 33947648 | bytes 593920 | tf_op jit(solution)/shard_map/htn,thp->hnp/dot_general | solution.py:426
  70.5 22.1 %shard_map.149 = bf16[32,32,128]{2,1,0:T(8,128)(2,1)} custom-call(bf16[32,32,128]{2,1,0:T(8,128)(2,1)} %bitcast.132, f32[32,32,128]{2,1,0:T(8,128)} %get-tuple-element.21.refs_1_), custom_call_target="tpu_custom_call" | custom-call | tf_op jit(solution)/shard_map/pallas_call | solution.py:184
  92.6 1.3 %multiply_reduce_fusion = f32[32]{0:T(128)S(1)} fusion(bf16[32,32,128]{2,1,0:T(8,128)(2,1)S(1)} %copy-done.1, bf16[32,32,128]{2,1,0:T(8,128)(2,1)} %shard_map.149), kind=kLoop, calls=%fused_computation.51 | loop fusion | flops 524256 | bytes 524416 | tf_op jit(solution)/shard_map/reduce_sum | solution.py:440
  94.0 0.2 multiply_reduce_fusion.1
  94.2 0.3 convolution_bitcast_fusion
  95.2 0.3 reduce_window_sum.18
  95.7 0.3 fusion.6
  96.0 0.2 fusion.5
  96.2 0.4 fusion.3
  96.6 0.2 copy.86
  97.0 1.0 gather_fusion
  97.9 0.7 copy.79
  98.7 0.2 multiply_multiply_fusion
  98.9 0.5 copy-done.13
  99.4 0.6 select_maximum_fusion.rim_ref
  100.0 19.0 %shard_map.150 = (f32[32,128]{1,0:T(8,128)}, f32[8,1024]{1,0:T(8,128)}) custom-call(f32[16,32,128]{2,1,0:T(8,128)} %bitcast.130, f32[8,1152]{1,0:T(8,128)} %select_maximum_fusion.rim_ref), custom_call_target="tpu_custom_call" | custom-call | tf_op jit(solution)/shard_map/pallas_call | solution.py:252
  119.0 0.8 slice_multiply_fusion.8
  119.8 0.6 fusion.42
  120.6 0.9 fusion.12
  121.5 0.7 divide_multiply_fusion
  (69 shorter events, 2.4 us)
Async XLA Ops:
  2.1 6.2 %collective-permute-start = (bf16[3,1280]{1,0:T(4,128)(2,1)S(1)}, bf16[3,1280]{1,0:T(4,128)(2,1)S(1)}, u32[]{:S(2)}, u32[]{:S(2)}) collective-permute-start(bf16[3,1280]{1,0:T(4,128)(2,1)S(1)} %pad_maximum_fusion.3), channel_id=1, source_target_pairs={{0,16},{16,32},{32,48},{48,64},{64,80},{80,96},{96,112},{112,128},... | collective-permute-start | bytes 23048 | tf_op jit(solution)/shard_map/ppermute | solution.py:283
  6.0 0.7 copy-start.7
  6.0 0.7 copy-start.14
  6.1 0.7 copy-start.11
  6.7 0.7 copy-start.10
  6.7 0.7 copy-start.8
  6.7 1.5 %copy-start.5 = (bf16[2,128,128]{2,1,0:T(8,128)(2,1)S(1)}, bf16[2,128,128]{2,1,0:T(8,128)(2,1)}, u32[]{:S(2)}) copy-start(bf16[2,128,128]{2,1,0:T(8,128)(2,1)} %param.16) | copy-start | bytes 196612
  7.4 0.7 copy-start.12
  8.4 1.0 copy-start.4
  40.6 0.7 copy-start.15
  41.7 1.0 copy-start.2
  41.7 1.0 copy-start.3
  41.7 1.0 copy-start.6
  68.0 1.0 copy-start.1
  92.6 1.4 %copy-start = (bf16[32,32,128]{2,1,0:T(8,128)(2,1)S(1)}, bf16[32,32,128]{2,1,0:T(8,128)(2,1)}, u32[]{:S(2)}) copy-start(bf16[32,32,128]{2,1,0:T(8,128)(2,1)} %shard_map.149) | copy-start | bytes 786436
  98.7 0.7 copy-start.13
  119.8 0.8 copy-start.9

commit v10 on v9

--- a/solution.py
+++ b/solution.py
@@ -373,13 +373,23 @@
         axis=1,
     )
     rows_prior = passed_along(rows_last, "seq", 1)
-    x_ext = jnp.concatenate([rows_prior[:, :channels], x_input], axis=0)
     bc_prior = jnp.moveaxis(rows_prior[:, channels:].reshape(3, 2, nstate), 0, 1)
-    bc_ext = jnp.concatenate([bc_prior, bc_input], axis=1)
-    x_pre = conv_rows(x_ext.astype(f32), conv_x)
-    bc_pre = conv_rows(bc_ext.astype(f32), convolution_bc_taps)
-    x_rows = jax.nn.silu(x_pre).astype(bf16)
-    bc_rows = jax.nn.silu(bc_pre).astype(bf16)
+    x_in = x_input.astype(f32)
+    bc_in = bc_input.astype(f32)
+    x_pre_body = conv_rows(x_in, conv_x)
+    bc_pre_body = conv_rows(bc_in, convolution_bc_taps)
+    x_pre_head = conv_rows(jnp.concatenate([rows_prior[:, :channels].astype(f32), x_in[:3]], axis=0), conv_x)
+    bc_pre_head = conv_rows(
+        jnp.concatenate([bc_prior.astype(f32), bc_in[:, :3]], axis=1), convolution_bc_taps
+    )
+    x_body = jax.nn.silu(x_pre_body).astype(bf16)
+    x_head = jax.nn.silu(x_pre_head).astype(bf16)
+    bc_body = jax.nn.silu(bc_pre_body).astype(bf16)
+    bc_head = jax.nn.silu(bc_pre_head).astype(bf16)
+    x_pre = jnp.concatenate([x_pre_head, x_pre_body], axis=0)
+    bc_pre = jnp.concatenate([bc_pre_head, bc_pre_body], axis=1)
+    x_rows = jnp.concatenate([x_head, x_body], axis=0)
+    bc_rows = jnp.concatenate([bc_head, bc_body], axis=1)
     b_rows = bc_rows[0]
     c_rows = bc_rows[1]
     gram = jnp.dot(c_rows, b_rows.T, preferred_element_type=f32)
@@ -390,7 +400,13 @@
     trailing = jnp.exp(cumul[:, -1:] - cumul)
     tail_step = trailing * step_size
     weighted_b = (tail_step[:, :, None] * b_rows.astype(f32)[None]).astype(bf16)
-    local_state = jnp.einsum("hsn,shp->hnp", weighted_b, x_heads, preferred_element_type=f32)
+    wb_body = (tail_step[:, 3:, None] * bc_body[0].astype(f32)[None]).astype(bf16)
+    wb_head = (tail_step[:, :3, None] * bc_head[0].astype(f32)[None]).astype(bf16)
+    local_state = jnp.einsum(
+        "hsn,shp->hnp", wb_body, x_body.reshape(length - 3, head_count, width), preferred_element_type=f32
+    ) + jnp.einsum(
+        "hsn,shp->hnp", wb_head, x_head.reshape(3, head_count, width), preferred_element_type=f32
+    )
 
     state_exact, weight = scan_forward(totals, local_state)
     state_low = state_exact.astype(bf16)

time: 123 us -> 128 us (1.041)
  local copies, waits for them, and re-layouts: 11.3 us -> 13.4 us
    pallas_call x1, Pallas kernels: 22.1 us -> 26.1 us  [scan_pieces(): pl.pallas_call(kern, out_shape=jax.ShapeDtypeStruct(piece, low), in_specs...]
    pallas_call x1, Pallas kernels: 22 us -> 19.7 us  [exchange(): pl.pallas_call(functools.partial(exchange_kernel, axis, n), out_shape=jax...]
    pallas_call x1, Pallas kernels: 19 us -> 17.1 us  [tail_exchange(): pl.pallas_call(functools.partial(tail_kernel, n, hn), out_shape=(jax.Shap...]
    unnamed x33 -> x32, local copies, waits for them, and re-layouts: 4.61 us -> 5.73 us
  transfers between devices with their start and end apart: 1 -> 1, of which waited for: 0 -> 0; matrix products, arithmetic and copies ran while one was open for 1% -> 3% of each run, Pallas kernels for 0% -> 0%
where the time goes in v10:
time: 128 us; the launch traced here: 127 us
  Pallas kernels  92 us (72%)
  local copies, waits for them, and re-layouts  13.4 us (10%)
  other arithmetic  11.2 us (9%)
  matrix products  4.8 us (4%)
  starting transfers between devices  4.08 us (3%)
    pallas_call x1, Pallas kernels, scan_pieces(): pl.pallas_call(kern, out_shape=(jax.ShapeDtypeStruct(piece, low), jax.Sha...  29.1 us
    pallas_call x1, Pallas kernels, scan_pieces(): pl.pallas_call(kern, out_shape=jax.ShapeDtypeStruct(piece, low), in_specs...  26.1 us
    pallas_call x1, Pallas kernels, exchange(): pl.pallas_call(functools.partial(exchange_kernel, axis, n), out_shape=jax...  19.7 us
    pallas_call x1, Pallas kernels, tail_exchange(): pl.pallas_call(functools.partial(tail_kernel, n, hn), out_shape=(jax.Shap...  17.1 us
    unnamed x32, local copies, waits for them, and re-layouts  5.73 us
    ppermute x1, starting transfers between devices, passed_along(): return lax.ppermute(block, axis, route)  4.08 us
  transfers between devices with their start and end apart: 1, of which 0 were waited for; matrix products, arithmetic and copies ran while one was open for 3% of the time, Pallas kernels for 0%

profile of v10, /device:TPU:1, one launch (start us, length us, event | category | flops | bytes accessed | tf_op | source)
XLA Modules:
  0.0 126.6 jit_solution(10871611973905233125)
XLA Ops:
  0.6 0.7 slice.174
  1.4 0.7 slice_bitcast_fusion.2
  2.1 4.1 %collective-permute-start = (bf16[3,1280]{1,0:T(4,128)(2,1)S(1)}, bf16[3,1280]{1,0:T(4,128)(2,1)S(1)}, u32[]{:S(2)}, u32[]{:S(2)}) collective-permute-start(bf16[3,1280]{1,0:T(4,128)(2,1)S(1)} %pad_maximum_fusion.7), channel_id=1, source_target_pairs={{0,16},{16,32},{32,48},{48,64},{64,80},{80,96},{96,112},{112,128},... | collective-permute-start | bytes 23048 | tf_op jit(solution)/shard_map/ppermute | solution.py:283
  6.2 1.0 convert_element_type.104
  7.2 0.6 copy-done.13
  7.9 0.6 copy-done.10
  8.6 0.3 reduce_window_sum.17
  9.3 0.6 copy-done.7
  9.8 0.3 multiply_convert_fusion.5
  10.3 0.7 copy-done.9
  11.2 0.6 copy-done.11
  11.7 0.2 fusion.28
  12.1 0.7 slice.223
  13.1 0.4 fusion.4
  13.5 0.8 pad_maximum_fusion.2.refs_0_
  14.3 29.1 %shard_map.147 = (bf16[32,32,128]{2,1,0:T(8,128)(2,1)}, f32[32,32,128]{2,1,0:T(8,128)}) custom-call(bf16[32,48,128]{2,1,0:T(8,128)(2,1)} %pad_maximum_fusion.2.refs_0_), custom_call_target="tpu_custom_call" | custom-call | tf_op jit(solution)/shard_map/pallas_call | solution.py:176
  43.4 1.1 copy.68
  44.5 0.2 fusion.88
  45.1 0.6 copy-done.14
  45.8 0.4 fusion.1
  46.4 0.7 copy-done.2
  47.2 0.3 multiply_reduce_fusion.5
  47.6 0.6 broadcast_in_dim.38.in_ref
  48.2 19.7 %shard_map.148 = f32[16,8,128]{2,1,0:T(8,128)} custom-call(f32[16,8,128]{2,1,0:T(8,128)} %broadcast_in_dim.38.in_ref), custom_call_target="tpu_custom_call" | custom-call | tf_op jit(solution)/shard_map/pallas_call | solution.py:55
  67.9 0.9 reduce_sum.130
  68.9 1.1 fusion.23
  70.2 0.5 multiply_reduce_fusion.6
  70.8 0.4 copy-done.1
  71.2 0.3 fusion.5
  71.5 1.3 %convolution_convert_fusion = bf16[8,128,128]{2,1,0:T(8,128)(2,1)} fusion(bf16[128,8,128]{0,2,1:T(8,128)(2,1)S(1)} %bitcast.133, f32[128,128]{1,0:T(8,128)S(1)} %get-tuple-element.32, f32[8,128]{1,0:T(8,128)S(1)} %get-tuple-element.53), kind=kOutput, calls=%fused_computation.12 | convolution fusion | flops 33947648 | bytes 593920 | tf_op jit(solution)/shard_map/htn,thp->hnp/dot_general | solution.py:442
  72.8 26.1 %shard_map.149 = bf16[32,32,128]{2,1,0:T(8,128)(2,1)} custom-call(bf16[32,32,128]{2,1,0:T(8,128)(2,1)} %bitcast.145, f32[32,32,128]{2,1,0:T(8,128)} %get-tuple-element.21.refs_1_), custom_call_target="tpu_custom_call" | custom-call | tf_op jit(solution)/shard_map/pallas_call | solution.py:184
  98.9 1.3 %multiply_reduce_fusion = f32[32]{0:T(128)S(1)} fusion(bf16[32,32,128]{2,1,0:T(8,128)(2,1)S(1)} %copy-done.1, bf16[32,32,128]{2,1,0:T(8,128)(2,1)} %shard_map.149), kind=kLoop, calls=%fused_computation.53 | loop fusion | flops 524256 | bytes 524416 | tf_op jit(solution)/shard_map/reduce_sum | solution.py:456
  100.3 0.2 multiply_reduce_fusion.1
  100.5 0.3 convolution_bitcast_fusion
  101.5 0.3 reduce_window_sum.18
  102.0 0.3 fusion.7
  102.5 0.4 fusion.3
  102.9 0.2 copy.92
  103.2 1.0 gather_fusion
  104.2 0.7 copy.85
  105.0 0.2 multiply_multiply_fusion
  105.2 0.4 copy-done.12
  105.7 0.6 select_maximum_fusion.rim_ref
  106.3 17.1 %shard_map.150 = (f32[32,128]{1,0:T(8,128)}, f32[8,1024]{1,0:T(8,128)}) custom-call(f32[16,32,128]{2,1,0:T(8,128)} %bitcast.143, f32[8,1152]{1,0:T(8,128)} %select_maximum_fusion.rim_ref), custom_call_target="tpu_custom_call" | custom-call | tf_op jit(solution)/shard_map/pallas_call | solution.py:252
  123.4 0.8 slice_multiply_fusion.8
  124.2 0.6 fusion.54
  125.0 0.9 fusion.13
  125.9 0.7 divide_multiply_fusion.1
  (81 shorter events, 3.7 us)
Async XLA Ops:
  2.1 5.1 %copy-start.4 = (bf16[2,128,128]{2,1,0:T(8,128)(2,1)S(1)}, bf16[2,128,128]{2,1,0:T(8,128)(2,1)}, u32[]{:S(2)}) copy-start(bf16[2,128,128]{2,1,0:T(8,128)(2,1)} %param.16) | copy-start | bytes 196612
  2.1 10.8 %collective-permute-start = (bf16[3,1280]{1,0:T(4,128)(2,1)S(1)}, bf16[3,1280]{1,0:T(4,128)(2,1)S(1)}, u32[]{:S(2)}, u32[]{:S(2)}) collective-permute-start(bf16[3,1280]{1,0:T(4,128)(2,1)S(1)} %pad_maximum_fusion.7), channel_id=1, source_target_pairs={{0,16},{16,32},{32,48},{48,64},{64,80},{80,96},{96,112},{112,128},... | collective-permute-start | bytes 23048 | tf_op jit(solution)/shard_map/ppermute | solution.py:283
  7.2 0.7 copy-start.6
  7.2 0.7 copy-start.13
  7.9 0.7 copy-start.10
  9.1 0.7 copy-start.7
  10.2 0.7 copy-start.9
  11.0 0.7 copy-start.11
  45.1 0.7 copy-start.14
  46.2 1.0 copy-start.2
  46.2 1.0 copy-start.3
  46.2 1.0 copy-start.5
  70.2 1.0 copy-start.1
  98.9 1.4 %copy-start = (bf16[32,32,128]{2,1,0:T(8,128)(2,1)S(1)}, bf16[32,32,128]{2,1,0:T(8,128)(2,1)}, u32[]{:S(2)}) copy-start(bf16[32,32,128]{2,1,0:T(8,128)(2,1)} %shard_map.149) | copy-start | bytes 786436
  105.0 0.7 copy-start.12
  124.2 0.8 copy-start.8

commit v11 on v9

--- a/solution.py
+++ b/solution.py
@@ -138,16 +138,16 @@
             parts = land[k, rows : rows + 3, :].astype(jnp.float32)
             grow = jnp.exp(parts[0:1] + parts[1:2] + parts[2:3])
             factor = jnp.sum(jnp.where(pick, grow, 0.0), axis=1, keepdims=True)
-            scale_out[k] = jnp.broadcast_to(factor, (rows, 128))
+            scale_out[k] = jnp.broadcast_to(factor, (8, 128))
         acc = jnp.zeros((rows, 128), jnp.float32)
         for k in range(n):
             res[k] = acc.astype(res.dtype)
-            acc = scale_out[k] * acc + land[k, :rows, :].astype(jnp.float32)
+            acc = scale_out[k][0:1, 0:1] * acc + land[k, :rows, :].astype(jnp.float32)
     else:
         acc = jnp.zeros((rows, 128), jnp.float32)
         for k in reversed(range(n)):
             res[k] = acc.astype(res.dtype)
-            acc = land[k].astype(jnp.float32) + scale_in[k] * acc
+            acc = land[k].astype(jnp.float32) + scale_in[k][0:1, 0:1] * acc
     copies = _peer_copies(axis, n, lambda p: res.at[p], land2, s2, r2)
     land2[me] = res[me]
     _peer_waits(axis, n, copies, lambda p: res.at[p], land2, s2, r2)
@@ -175,7 +175,7 @@
     if forward:
         return pl.pallas_call(
             kern,
-            out_shape=(jax.ShapeDtypeStruct(piece, low), jax.ShapeDtypeStruct(piece, jnp.float32)),
+            out_shape=(jax.ShapeDtypeStruct(piece, low), jax.ShapeDtypeStruct((n, 8, 128), jnp.float32)),
             in_specs=[vm],
             out_specs=(vm, vm),
             scratch_shapes=scratch,

time: 123 us -> 123 us (level)
  no operation moved by 1% of the time
where the time goes in v11:
time: 123 us; the launch traced here: 122 us
  Pallas kernels  91.1 us (74%)
  local copies, waits for them, and re-layouts  11.3 us (9%)
  other arithmetic  10.1 us (8%)
  matrix products  4.49 us (4%)
  starting transfers between devices  3.95 us (3%)
    pallas_call x1, Pallas kernels, scan_pieces(): pl.pallas_call(kern, out_shape=(jax.ShapeDtypeStruct(piece, low), jax.Sha...  28.1 us
    pallas_call x1, Pallas kernels, scan_pieces(): pl.pallas_call(kern, out_shape=jax.ShapeDtypeStruct(piece, low), in_specs...  22 us
    pallas_call x1, Pallas kernels, exchange(): pl.pallas_call(functools.partial(exchange_kernel, axis, n), out_shape=jax...  22 us
    pallas_call x1, Pallas kernels, tail_exchange(): pl.pallas_call(functools.partial(tail_kernel, n, hn), out_shape=(jax.Shap...  19 us
    unnamed x33, local copies, waits for them, and re-layouts  4.61 us
    ppermute x1, starting transfers between devices, passed_along(): return lax.ppermute(block, axis, route)  3.95 us
  transfers between devices with their start and end apart: 1, of which 0 were waited for; matrix products, arithmetic and copies ran while one was open for 1% of the time, Pallas kernels for 0%

profile of v11, /device:TPU:1, one launch (start us, length us, event | category | flops | bytes accessed | tf_op | source)
XLA Modules:
  0.0 122.0 jit_solution(15633646517847806634)
XLA Ops:
  0.6 0.7 slice.139
  1.4 0.7 slice_bitcast_fusion.8
  2.1 3.9 %collective-permute-start = (bf16[3,1280]{1,0:T(4,128)(2,1)S(1)}, bf16[3,1280]{1,0:T(4,128)(2,1)S(1)}, u32[]{:S(2)}, u32[]{:S(2)}) collective-permute-start(bf16[3,1280]{1,0:T(4,128)(2,1)S(1)} %pad_maximum_fusion.3), channel_id=1, source_target_pairs={{0,16},{16,32},{32,48},{48,64},{64,80},{80,96},{96,112},{112,128},... | collective-permute-start | bytes 23048 | tf_op jit(solution)/shard_map/ppermute | solution.py:283
  6.1 0.6 copy-done.14
  6.8 0.3 reduce_window_sum.17
  7.1 0.2 slice_reduce_fusion
  7.5 0.7 copy-done.12
  8.7 0.7 copy-done.4
  9.4 0.3 multiply_convert_fusion.4
  9.8 0.2 copy.88
  9.9 0.3 convolution_convert_fusion.1
  10.3 0.8 pad_maximum_fusion.1.refs_0_
  11.0 28.1 %shard_map.147 = (bf16[32,32,128]{2,1,0:T(8,128)(2,1)}, f32[32,8,128]{2,1,0:T(8,128)}) custom-call(bf16[32,48,128]{2,1,0:T(8,128)(2,1)} %pad_maximum_fusion.1.refs_0_), custom_call_target="tpu_custom_call" | custom-call | tf_op jit(solution)/shard_map/pallas_call | solution.py:176
  39.2 1.1 copy.63
  40.3 0.2 fusion.40
  40.5 0.6 copy-done.15
  41.2 0.4 fusion.1
  41.6 0.2 copy.85
  41.8 0.7 copy-done.2
  42.6 0.3 multiply_reduce_fusion.5
  43.0 0.6 broadcast_in_dim.36.in_ref
  43.6 22.0 %shard_map.148 = f32[16,8,128]{2,1,0:T(8,128)} custom-call(f32[16,8,128]{2,1,0:T(8,128)} %broadcast_in_dim.36.in_ref), custom_call_target="tpu_custom_call" | custom-call | tf_op jit(solution)/shard_map/pallas_call | solution.py:55
  65.6 0.9 reduce_sum.130
  66.5 1.1 fusion.22
  67.6 0.2 copy.89
  67.8 0.5 multiply_reduce_fusion.6
  68.4 0.4 copy-done.1
  68.8 0.3 fusion.4
  69.1 1.3 %convolution_convert_fusion = bf16[8,128,128]{2,1,0:T(8,128)(2,1)} fusion(bf16[128,8,128]{0,2,1:T(8,128)(2,1)S(1)} %bitcast.117, f32[128,128]{1,0:T(8,128)S(1)} %get-tuple-element.40, f32[8,128]{1,0:T(8,128)S(1)} %get-tuple-element.48), kind=kOutput, calls=%fused_computation.10 | convolution fusion | flops 33947648 | bytes 593920 | tf_op jit(solution)/shard_map/htn,thp->hnp/dot_general | solution.py:426
  70.4 22.0 %shard_map.149 = bf16[32,32,128]{2,1,0:T(8,128)(2,1)} custom-call(bf16[32,32,128]{2,1,0:T(8,128)(2,1)} %bitcast.130, f32[32,8,128]{2,1,0:T(8,128)} %get-tuple-element.21.refs_1_), custom_call_target="tpu_custom_call" | custom-call | tf_op jit(solution)/shard_map/pallas_call | solution.py:184
  92.4 1.3 %multiply_reduce_fusion = f32[32]{0:T(128)S(1)} fusion(bf16[32,32,128]{2,1,0:T(8,128)(2,1)S(1)} %copy-done.1, bf16[32,32,128]{2,1,0:T(8,128)(2,1)} %shard_map.149), kind=kLoop, calls=%fused_computation.51 | loop fusion | flops 524256 | bytes 524416 | tf_op jit(solution)/shard_map/reduce_sum | solution.py:440
  93.7 0.2 multiply_reduce_fusion.1
  94.0 0.3 convolution_bitcast_fusion
  95.0 0.3 reduce_window_sum.18
  95.5 0.3 fusion.6
  95.7 0.2 fusion.5
  95.9 0.4 fusion.3
  96.3 0.2 copy.86
  96.7 1.0 gather_fusion
  97.7 0.7 copy.79
  98.4 0.2 multiply_multiply_fusion
  98.6 0.5 copy-done.13
  99.1 0.6 select_maximum_fusion.rim_ref
  99.8 19.0 %shard_map.150 = (f32[32,128]{1,0:T(8,128)}, f32[8,1024]{1,0:T(8,128)}) custom-call(f32[16,32,128]{2,1,0:T(8,128)} %bitcast.131, f32[8,1152]{1,0:T(8,128)} %select_maximum_fusion.rim_ref), custom_call_target="tpu_custom_call" | custom-call | tf_op jit(solution)/shard_map/pallas_call | solution.py:252
  118.8 0.8 slice_multiply_fusion.8
  119.6 0.6 fusion.42
  120.4 0.9 fusion.12
  121.3 0.7 divide_multiply_fusion
  (69 shorter events, 2.4 us)
Async XLA Ops:
  2.1 6.2 %collective-permute-start = (bf16[3,1280]{1,0:T(4,128)(2,1)S(1)}, bf16[3,1280]{1,0:T(4,128)(2,1)S(1)}, u32[]{:S(2)}, u32[]{:S(2)}) collective-permute-start(bf16[3,1280]{1,0:T(4,128)(2,1)S(1)} %pad_maximum_fusion.3), channel_id=1, source_target_pairs={{0,16},{16,32},{32,48},{48,64},{64,80},{80,96},{96,112},{112,128},... | collective-permute-start | bytes 23048 | tf_op jit(solution)/shard_map/ppermute | solution.py:283
  6.0 0.7 copy-start.7
  6.0 0.7 copy-start.14
  6.1 0.7 copy-start.11
  6.7 0.7 copy-start.10
  6.7 0.7 copy-start.8
  6.7 1.5 %copy-start.5 = (bf16[2,128,128]{2,1,0:T(8,128)(2,1)S(1)}, bf16[2,128,128]{2,1,0:T(8,128)(2,1)}, u32[]{:S(2)}) copy-start(bf16[2,128,128]{2,1,0:T(8,128)(2,1)} %param.16) | copy-start | bytes 196612
  7.4 0.7 copy-start.12
  8.4 1.0 copy-start.4
  40.5 0.7 copy-start.15
  41.6 1.0 copy-start.2
  41.6 1.0 copy-start.3
  41.6 1.0 copy-start.6
  67.8 1.0 copy-start.1
  92.4 1.4 %copy-start = (bf16[32,32,128]{2,1,0:T(8,128)(2,1)S(1)}, bf16[32,32,128]{2,1,0:T(8,128)(2,1)}, u32[]{:S(2)}) copy-start(bf16[32,32,128]{2,1,0:T(8,128)(2,1)} %shard_map.149) | copy-start | bytes 786436
  98.4 0.7 copy-start.13
  119.6 0.8 copy-start.9

commit v12 on v11

--- a/solution.py
+++ b/solution.py
@@ -474,7 +474,7 @@
     for h in range(hcount):
         own = [h * row_share + i for i in range(row_share + 3)]
         own = [r if r < length else length for r in own]
-        picks.append(own + [length] * (16 - row_share - 3))
+        picks.append(own + [length] * (12 - row_share - 3))
     picks = jnp.array(picks, jnp.int32)
     piece_rows = picks.shape[1]
     bc_rows_z = jnp.concatenate([grad_bc_rows, jnp.zeros((2, 1, nstate), f32)], axis=1)

time: 123 us -> 122 us (level)
    reshape x0 -> x2, local copies, waits for them, and re-layouts: none -> 1.45 us  [the longest x1 0.74 us: shards(): bc_pieces.reshape(hcount, 2 * piece_rows, -1)]
where the time goes in v12:
time: 122 us; the launch traced here: 121 us
  Pallas kernels  90 us (74%)
  local copies, waits for them, and re-layouts  11.9 us (10%)
  other arithmetic  9.36 us (8%)
  matrix products  4.49 us (4%)
  starting transfers between devices  3.95 us (3%)
    pallas_call x1, Pallas kernels, scan_pieces(): pl.pallas_call(kern, out_shape=(jax.ShapeDtypeStruct(piece, low), jax.Sha...  28.1 us
    pallas_call x1, Pallas kernels, scan_pieces(): pl.pallas_call(kern, out_shape=jax.ShapeDtypeStruct(piece, low), in_specs...  22 us
    pallas_call x1, Pallas kernels, exchange(): pl.pallas_call(functools.partial(exchange_kernel, axis, n), out_shape=jax...  22 us
    pallas_call x1, Pallas kernels, tail_exchange(): pl.pallas_call(functools.partial(tail_kernel, n, hn), out_shape=(jax.Shap...  17.9 us
    unnamed x33, local copies, waits for them, and re-layouts  4.6 us
    ppermute x1, starting transfers between devices, passed_along(): return lax.ppermute(block, axis, route)  3.95 us
  transfers between devices with their start and end apart: 1, of which 0 were waited for; matrix products, arithmetic and copies ran while one was open for 1% of the time, Pallas kernels for 0%

profile of v12, /device:TPU:1, one launch (start us, length us, event | category | flops | bytes accessed | tf_op | source)
XLA Modules:
  0.0 120.8 jit_solution(7614060444206403860)
XLA Ops:
  0.6 0.7 slice.139
  1.4 0.7 slice_bitcast_fusion.8
  2.1 3.9 %collective-permute-start = (bf16[3,1280]{1,0:T(4,128)(2,1)S(1)}, bf16[3,1280]{1,0:T(4,128)(2,1)S(1)}, u32[]{:S(2)}, u32[]{:S(2)}) collective-permute-start(bf16[3,1280]{1,0:T(4,128)(2,1)S(1)} %pad_maximum_fusion.3), channel_id=1, source_target_pairs={{0,16},{16,32},{32,48},{48,64},{64,80},{80,96},{96,112},{112,128},... | collective-permute-start | bytes 23048 | tf_op jit(solution)/shard_map/ppermute | solution.py:283
  6.1 0.6 copy-done.14
  6.8 0.3 reduce_window_sum.17
  7.1 0.2 slice_reduce_fusion
  7.5 0.7 copy-done.12
  8.7 0.7 copy-done.4
  9.4 0.3 multiply_convert_fusion.4
  9.8 0.2 copy.90
  9.9 0.3 convolution_convert_fusion.1
  10.3 0.8 pad_maximum_fusion.1.refs_0_
  11.0 28.1 %shard_map.147 = (bf16[32,32,128]{2,1,0:T(8,128)(2,1)}, f32[32,8,128]{2,1,0:T(8,128)}) custom-call(bf16[32,48,128]{2,1,0:T(8,128)(2,1)} %pad_maximum_fusion.1.refs_0_), custom_call_target="tpu_custom_call" | custom-call | tf_op jit(solution)/shard_map/pallas_call | solution.py:176
  39.2 1.1 copy.64
  40.3 0.2 fusion.40
  40.5 0.6 copy-done.15
  41.2 0.4 fusion.1
  41.6 0.2 copy.87
  41.8 0.7 copy-done.2
  42.6 0.3 multiply_reduce_fusion.5
  43.0 0.6 broadcast_in_dim.36.in_ref
  43.6 22.0 %shard_map.148 = f32[16,8,128]{2,1,0:T(8,128)} custom-call(f32[16,8,128]{2,1,0:T(8,128)} %broadcast_in_dim.36.in_ref), custom_call_target="tpu_custom_call" | custom-call | tf_op jit(solution)/shard_map/pallas_call | solution.py:55
  65.6 0.9 reduce_sum.130
  66.5 1.1 fusion.22
  67.6 0.2 copy.91
  67.8 0.5 multiply_reduce_fusion.6
  68.4 0.4 copy-done.1
  68.8 0.3 fusion.4
  69.1 1.3 %convolution_convert_fusion = bf16[8,128,128]{2,1,0:T(8,128)(2,1)} fusion(bf16[128,8,128]{0,2,1:T(8,128)(2,1)S(1)} %bitcast.116, f32[128,128]{1,0:T(8,128)S(1)} %get-tuple-element.40, f32[8,128]{1,0:T(8,128)S(1)} %get-tuple-element.48), kind=kOutput, calls=%fused_computation.10 | convolution fusion | flops 33947648 | bytes 593920 | tf_op jit(solution)/shard_map/htn,thp->hnp/dot_general | solution.py:426
  70.4 22.0 %shard_map.149 = bf16[32,32,128]{2,1,0:T(8,128)(2,1)} custom-call(bf16[32,32,128]{2,1,0:T(8,128)(2,1)} %bitcast.129, f32[32,8,128]{2,1,0:T(8,128)} %get-tuple-element.21.refs_1_), custom_call_target="tpu_custom_call" | custom-call | tf_op jit(solution)/shard_map/pallas_call | solution.py:184
  92.4 1.3 %multiply_reduce_fusion = f32[32]{0:T(128)S(1)} fusion(bf16[32,32,128]{2,1,0:T(8,128)(2,1)S(1)} %copy-done.1, bf16[32,32,128]{2,1,0:T(8,128)(2,1)} %shard_map.149), kind=kLoop, calls=%fused_computation.51 | loop fusion | flops 524256 | bytes 524416 | tf_op jit(solution)/shard_map/reduce_sum | solution.py:440
  93.7 0.2 multiply_reduce_fusion.1
  94.0 0.3 convolution_bitcast_fusion
  95.0 0.3 reduce_window_sum.18
  95.5 0.3 fusion.6
  95.7 0.2 fusion.5
  95.9 0.4 fusion.3
  96.3 0.2 copy.88
  96.7 0.9 gather_fusion
  97.6 0.7 copy.81.in_ref
  98.4 0.2 multiply_multiply_fusion
  98.6 0.5 copy-done.13
  99.1 0.6 select_maximum_fusion.rim_ref
  99.7 17.9 %shard_map.150 = (f32[24,128]{1,0:T(8,128)}, f32[8,1024]{1,0:T(8,128)}) custom-call(f32[16,24,128]{2,1,0:T(8,128)} %copy.81.in_ref, f32[8,1152]{1,0:T(8,128)} %select_maximum_fusion.rim_ref), custom_call_target="tpu_custom_call" | custom-call | tf_op jit(solution)/shard_map/pallas_call | solution.py:252
  117.6 0.7 reshape.209
  118.4 0.6 fusion.42
  119.2 0.9 fusion.12
  120.1 0.7 divide_multiply_fusion
  (71 shorter events, 2.5 us)
Async XLA Ops:
  2.1 6.2 %collective-permute-start = (bf16[3,1280]{1,0:T(4,128)(2,1)S(1)}, bf16[3,1280]{1,0:T(4,128)(2,1)S(1)}, u32[]{:S(2)}, u32[]{:S(2)}) collective-permute-start(bf16[3,1280]{1,0:T(4,128)(2,1)S(1)} %pad_maximum_fusion.3), channel_id=1, source_target_pairs={{0,16},{16,32},{32,48},{48,64},{64,80},{80,96},{96,112},{112,128},... | collective-permute-start | bytes 23048 | tf_op jit(solution)/shard_map/ppermute | solution.py:283
  6.0 0.7 copy-start.7
  6.0 0.7 copy-start.14
  6.1 0.7 copy-start.11
  6.7 0.7 copy-start.10
  6.7 0.7 copy-start.8
  6.7 1.5 %copy-start.5 = (bf16[2,128,128]{2,1,0:T(8,128)(2,1)S(1)}, bf16[2,128,128]{2,1,0:T(8,128)(2,1)}, u32[]{:S(2)}) copy-start(bf16[2,128,128]{2,1,0:T(8,128)(2,1)} %param.16) | copy-start | bytes 196612
  7.4 0.7 copy-start.12
  8.4 1.0 copy-start.4
  40.5 0.7 copy-start.15
  41.6 1.0 copy-start.2
  41.6 1.0 copy-start.3
  41.6 1.0 copy-start.6
  67.8 1.0 copy-start.1
  92.4 1.4 %copy-start = (bf16[32,32,128]{2,1,0:T(8,128)(2,1)S(1)}, bf16[32,32,128]{2,1,0:T(8,128)(2,1)}, u32[]{:S(2)}) copy-start(bf16[32,32,128]{2,1,0:T(8,128)(2,1)} %shard_map.149) | copy-start | bytes 786436
  98.4 0.7 copy-start.13
  118.4 0.8 copy-start.9

commit v13 on v12

--- a/solution.py
+++ b/solution.py
@@ -196,6 +196,7 @@
     hme = lax.axis_index("head")
     prev = lax.rem(me + n - 1, n)
     nxt = lax.rem(me + 1, n)
+    last = hn - 1
     barrier = pltpu.get_barrier_semaphore()
     for i in range(1, hn):
         pl.semaphore_signal(barrier, inc=1, device_id=(me, lax.rem(hme + i, hn)), device_id_type=MESH)
@@ -207,7 +208,20 @@
         device_id=(prev, hme), device_id_type=MESH,
     )
     rim_copy.start()
-    send[...] = in_ref[...]
+
+    def piece_copy(t, src):
+        return pltpu.make_async_remote_copy(
+            src_ref=src, dst_ref=land.at[hme], send_sem=s1.at[t], recv_sem=r1.at[hme],
+            device_id=(me, t), device_id_type=MESH,
+        )
+
+    for t in range(last):
+        @pl.when(hme != t)
+        def _():
+            piece_copy(t, in_ref.at[t]).start()
+
+    land[hme] = in_ref[hme]
+    send[...] = in_ref[last]
     rim_copy.wait_send()
     rim_copy.wait_recv()
     keep = (1 - me // (n - 1)).astype(jnp.float32)
@@ -215,29 +229,31 @@
     nst = in_ref.shape[2]
     width = rim_ref.shape[1] - nst
     rim_bc = rim_land[0:8, width:] * keep
-    last = hn - 1
-    send[last, 8:11, :] = send[last, 8:11, :] + rim_bc[0:3]
-    send[last, rows + 8 : rows + 11, :] = send[last, rows + 8 : rows + 11, :] + rim_bc[3:6]
+    send[8:11, :] = send[8:11, :] + rim_bc[0:3]
+    send[rows + 8 : rows + 11, :] = send[rows + 8 : rows + 11, :] + rim_bc[3:6]
     rim_out[...] = rim_land[0:8, 0:width] * keep
-    src_of = lambda p: send.at[p]
-    copies = []
-    for i in range(1, hn):
-        peer = lax.rem(hme + i, hn)
-        copy = pltpu.make_async_remote_copy(
-            src_ref=send.at[peer], dst_ref=land.at[hme], send_sem=s1.at[i], recv_sem=r1.at[i],
-            device_id=(me, peer), device_id_type=MESH,
-        )
-        copy.start()
-        copies.append(copy)
-    land[hme] = send[hme]
-    for i in range(1, hn):
-        copies[i - 1].wait_send()
-        src = lax.rem(hme + (hn - i), hn)
-        incoming = pltpu.make_async_remote_copy(
-            src_ref=send.at[src], dst_ref=land.at[src], send_sem=s1.at[i], recv_sem=r1.at[i],
-            device_id=(me, src), device_id_type=MESH,
-        )
-        incoming.wait_recv()
+
+    @pl.when(hme != last)
+    def _():
+        piece_copy(last, send).start()
+
+    @pl.when(hme == last)
+    def _():
+        land[last] = send[...]
+
+    for t in range(hn):
+        @pl.when(hme != t)
+        def _():
+            piece_copy(t, send).wait_send()
+
+    for j in range(hn):
+        @pl.when(hme != j)
+        def _():
+            pltpu.make_async_remote_copy(
+                src_ref=send, dst_ref=land.at[j], send_sem=s1.at[j], recv_sem=r1.at[j],
+                device_id=(me, j), device_id_type=MESH,
+            ).wait_recv()
+
     total = land[0]
     for j in range(1, hn):
         total = total + land[j]
@@ -259,7 +275,7 @@
         out_specs=(vm, vm),
         scratch_shapes=[
             pltpu.VMEM(pieces.shape, jnp.float32),
-            pltpu.VMEM(pieces.shape, jnp.float32),
+            pltpu.VMEM(pieces.shape[1:], jnp.float32),
             pltpu.VMEM(rim.shape, jnp.float32),
             pltpu.SemaphoreType.DMA((hn,)),
             pltpu.SemaphoreType.DMA((hn,)),

time: 122 us -> 118 us (0.967)
  Pallas kernels: 90 us -> 86.3 us
    pallas_call x1, Pallas kernels: 17.9 us -> 14.2 us  [tail_exchange(): pl.pallas_call(functools.partial(tail_kernel, n, hn), out_shape=(jax.Shap...]
where the time goes in v13:
time: 118 us; the launch traced here: 117 us
  Pallas kernels  86.3 us (73%)
  local copies, waits for them, and re-layouts  11.9 us (10%)
  other arithmetic  9.36 us (8%)
  matrix products  4.49 us (4%)
  starting transfers between devices  3.95 us (3%)
    pallas_call x1, Pallas kernels, scan_pieces(): pl.pallas_call(kern, out_shape=(jax.ShapeDtypeStruct(piece, low), jax.Sha...  28.1 us
    pallas_call x1, Pallas kernels, scan_pieces(): pl.pallas_call(kern, out_shape=jax.ShapeDtypeStruct(piece, low), in_specs...  22 us
    pallas_call x1, Pallas kernels, exchange(): pl.pallas_call(functools.partial(exchange_kernel, axis, n), out_shape=jax...  22 us
    pallas_call x1, Pallas kernels, tail_exchange(): pl.pallas_call(functools.partial(tail_kernel, n, hn), out_shape=(jax.Shap...  14.2 us
    unnamed x33, local copies, waits for them, and re-layouts  4.6 us
    ppermute x1, starting transfers between devices, passed_along(): return lax.ppermute(block, axis, route)  3.95 us
  transfers between devices with their start and end apart: 1, of which 0 were waited for; matrix products, arithmetic and copies ran while one was open for 1% of the time, Pallas kernels for 0%

profile of v13, /device:TPU:1, one launch (start us, length us, event | category | flops | bytes accessed | tf_op | source)
XLA Modules:
  0.0 117.1 jit_solution(18383525227432402290)
XLA Ops:
  0.6 0.7 slice.139
  1.4 0.7 slice_bitcast_fusion.8
  2.1 3.9 %collective-permute-start = (bf16[3,1280]{1,0:T(4,128)(2,1)S(1)}, bf16[3,1280]{1,0:T(4,128)(2,1)S(1)}, u32[]{:S(2)}, u32[]{:S(2)}) collective-permute-start(bf16[3,1280]{1,0:T(4,128)(2,1)S(1)} %pad_maximum_fusion.3), channel_id=1, source_target_pairs={{0,16},{16,32},{32,48},{48,64},{64,80},{80,96},{96,112},{112,128},... | collective-permute-start | bytes 23048 | tf_op jit(solution)/shard_map/ppermute | solution.py:299
  6.1 0.6 copy-done.14
  6.8 0.3 reduce_window_sum.17
  7.1 0.2 slice_reduce_fusion
  7.5 0.7 copy-done.12
  8.7 0.7 copy-done.4
  9.4 0.3 multiply_convert_fusion.4
  9.8 0.2 copy.90
  9.9 0.3 convolution_convert_fusion.1
  10.3 0.8 pad_maximum_fusion.1.refs_0_
  11.0 28.1 %shard_map.147 = (bf16[32,32,128]{2,1,0:T(8,128)(2,1)}, f32[32,8,128]{2,1,0:T(8,128)}) custom-call(bf16[32,48,128]{2,1,0:T(8,128)(2,1)} %pad_maximum_fusion.1.refs_0_), custom_call_target="tpu_custom_call" | custom-call | tf_op jit(solution)/shard_map/pallas_call | solution.py:176
  39.2 1.1 copy.64
  40.3 0.2 fusion.40
  40.5 0.6 copy-done.15
  41.2 0.4 fusion.1
  41.6 0.2 copy.87
  41.8 0.7 copy-done.2
  42.6 0.3 multiply_reduce_fusion.5
  43.0 0.6 broadcast_in_dim.36.in_ref
  43.6 22.0 %shard_map.148 = f32[16,8,128]{2,1,0:T(8,128)} custom-call(f32[16,8,128]{2,1,0:T(8,128)} %broadcast_in_dim.36.in_ref), custom_call_target="tpu_custom_call" | custom-call | tf_op jit(solution)/shard_map/pallas_call | solution.py:55
  65.6 0.9 reduce_sum.130
  66.5 1.1 fusion.22
  67.6 0.2 copy.91
  67.8 0.5 multiply_reduce_fusion.6
  68.4 0.4 copy-done.1
  68.8 0.3 fusion.4
  69.1 1.3 %convolution_convert_fusion = bf16[8,128,128]{2,1,0:T(8,128)(2,1)} fusion(bf16[128,8,128]{0,2,1:T(8,128)(2,1)S(1)} %bitcast.116, f32[128,128]{1,0:T(8,128)S(1)} %get-tuple-element.40, f32[8,128]{1,0:T(8,128)S(1)} %get-tuple-element.48), kind=kOutput, calls=%fused_computation.10 | convolution fusion | flops 33947648 | bytes 593920 | tf_op jit(solution)/shard_map/htn,thp->hnp/dot_general | solution.py:442
  70.4 22.0 %shard_map.149 = bf16[32,32,128]{2,1,0:T(8,128)(2,1)} custom-call(bf16[32,32,128]{2,1,0:T(8,128)(2,1)} %bitcast.129, f32[32,8,128]{2,1,0:T(8,128)} %get-tuple-element.21.refs_1_), custom_call_target="tpu_custom_call" | custom-call | tf_op jit(solution)/shard_map/pallas_call | solution.py:184
  92.4 1.3 %multiply_reduce_fusion = f32[32]{0:T(128)S(1)} fusion(bf16[32,32,128]{2,1,0:T(8,128)(2,1)S(1)} %copy-done.1, bf16[32,32,128]{2,1,0:T(8,128)(2,1)} %shard_map.149), kind=kLoop, calls=%fused_computation.51 | loop fusion | flops 524256 | bytes 524416 | tf_op jit(solution)/shard_map/reduce_sum | solution.py:456
  93.7 0.2 multiply_reduce_fusion.1
  94.0 0.3 convolution_bitcast_fusion
  95.0 0.3 reduce_window_sum.18
  95.5 0.3 fusion.6
  95.7 0.2 fusion.5
  95.9 0.4 fusion.3
  96.3 0.2 copy.88
  96.7 0.9 gather_fusion
  97.6 0.7 copy.81.in_ref
  98.4 0.2 multiply_multiply_fusion
  98.6 0.5 copy-done.13
  99.1 0.6 select_maximum_fusion.rim_ref
  99.7 14.2 %shard_map.150 = (f32[24,128]{1,0:T(8,128)}, f32[8,1024]{1,0:T(8,128)}) custom-call(f32[16,24,128]{2,1,0:T(8,128)} %copy.81.in_ref, f32[8,1152]{1,0:T(8,128)} %select_maximum_fusion.rim_ref), custom_call_target="tpu_custom_call" | custom-call | tf_op jit(solution)/shard_map/pallas_call | solution.py:268
  113.9 0.7 reshape.209
  114.7 0.6 fusion.42
  115.5 0.9 fusion.12
  116.4 0.7 divide_multiply_fusion
  (71 shorter events, 2.5 us)
Async XLA Ops:
  2.1 6.2 %collective-permute-start = (bf16[3,1280]{1,0:T(4,128)(2,1)S(1)}, bf16[3,1280]{1,0:T(4,128)(2,1)S(1)}, u32[]{:S(2)}, u32[]{:S(2)}) collective-permute-start(bf16[3,1280]{1,0:T(4,128)(2,1)S(1)} %pad_maximum_fusion.3), channel_id=1, source_target_pairs={{0,16},{16,32},{32,48},{48,64},{64,80},{80,96},{96,112},{112,128},... | collective-permute-start | bytes 23048 | tf_op jit(solution)/shard_map/ppermute | solution.py:299
  6.0 0.7 copy-start.7
  6.0 0.7 copy-start.14
  6.1 0.7 copy-start.11
  6.7 0.7 copy-start.10
  6.7 0.7 copy-start.8
  6.7 1.5 %copy-start.5 = (bf16[2,128,128]{2,1,0:T(8,128)(2,1)S(1)}, bf16[2,128,128]{2,1,0:T(8,128)(2,1)}, u32[]{:S(2)}) copy-start(bf16[2,128,128]{2,1,0:T(8,128)(2,1)} %param.16) | copy-start | bytes 196612
  7.4 0.7 copy-start.12
  8.4 1.0 copy-start.4
  40.5 0.7 copy-start.15
  41.6 1.0 copy-start.2
  41.6 1.0 copy-start.3
  41.6 1.0 copy-start.6
  67.8 1.0 copy-start.1
  92.4 1.4 %copy-start = (bf16[32,32,128]{2,1,0:T(8,128)(2,1)S(1)}, bf16[32,32,128]{2,1,0:T(8,128)(2,1)}, u32[]{:S(2)}) copy-start(bf16[32,32,128]{2,1,0:T(8,128)(2,1)} %shard_map.149) | copy-start | bytes 786436
  98.4 0.7 copy-start.13
  114.7 0.8 copy-start.9

commit v14 on v13

--- a/solution.py
+++ b/solution.py
@@ -130,27 +130,66 @@
     _barrier(axis, n)
     copies = _peer_copies(axis, n, lambda p: in_ref.at[p], land, s1, r1)
     land[me] = in_ref[me]
-    _peer_waits(axis, n, copies, lambda p: in_ref.at[p], land, s1, r1)
+    coords = {a: lax.axis_index(a) for a in AXES}
+
+    def dev(k):
+        return tuple(k if a == axis else coords[a] for a in AXES)
+
+    def arrive(k):
+        @pl.when(me != k)
+        def _():
+            pltpu.make_async_remote_copy(
+                src_ref=in_ref.at[k], dst_ref=land.at[k], send_sem=s1.at[0],
+                recv_sem=r1.at[lax.rem(me - k + n, n)], device_id=dev(k), device_id_type=MESH,
+            ).wait_recv()
+
+    def result_copy(k):
+        return pltpu.make_async_remote_copy(
+            src_ref=res.at[k], dst_ref=land2.at[me], send_sem=s2.at[k], recv_sem=r2.at[me],
+            device_id=dev(k), device_id_type=MESH,
+        )
+
+    def give(k):
+        @pl.when(me != k)
+        def _():
+            result_copy(k).start()
+
+        @pl.when(me == k)
+        def _():
+            land2[k] = res[k]
+
+    acc = jnp.zeros((rows, 128), jnp.float32)
     if forward:
         lane = lax.broadcasted_iota(jnp.int32, (1, 128), 1)
         pick = lane == me // (n // heads)
         for k in range(n):
+            res[k] = acc.astype(res.dtype)
+            give(k)
+            arrive(k)
             parts = land[k, rows : rows + 3, :].astype(jnp.float32)
             grow = jnp.exp(parts[0:1] + parts[1:2] + parts[2:3])
             factor = jnp.sum(jnp.where(pick, grow, 0.0), axis=1, keepdims=True)
             scale_out[k] = jnp.broadcast_to(factor, (8, 128))
-        acc = jnp.zeros((rows, 128), jnp.float32)
-        for k in range(n):
-            res[k] = acc.astype(res.dtype)
-            acc = scale_out[k][0:1, 0:1] * acc + land[k, :rows, :].astype(jnp.float32)
+            acc = factor * acc + land[k, :rows, :].astype(jnp.float32)
     else:
-        acc = jnp.zeros((rows, 128), jnp.float32)
         for k in reversed(range(n)):
             res[k] = acc.astype(res.dtype)
+            give(k)
+            arrive(k)
             acc = land[k].astype(jnp.float32) + scale_in[k][0:1, 0:1] * acc
-    copies = _peer_copies(axis, n, lambda p: res.at[p], land2, s2, r2)
-    land2[me] = res[me]
-    _peer_waits(axis, n, copies, lambda p: res.at[p], land2, s2, r2)
+    for c in copies:
+        c.wait_send()
+    for k in range(n):
+        @pl.when(me != k)
+        def _():
+            result_copy(k).wait_send()
+
+        @pl.when(me != k)
+        def _():
+            pltpu.make_async_remote_copy(
+                src_ref=res.at[k], dst_ref=land2.at[k], send_sem=s2.at[k], recv_sem=r2.at[k],
+                device_id=dev(k), device_id_type=MESH,
+            ).wait_recv()
     out_ref[...] = land2[...]
 
 

time: 118 us -> 117 us (level)
    pallas_call x1, Pallas kernels: 22 us -> 26.3 us  [scan_pieces(): pl.pallas_call(kern, out_shape=jax.ShapeDtypeStruct(piece, low), in_specs...]
    pallas_call x1, Pallas kernels: 28.1 us -> 25.5 us  [scan_pieces(): pl.pallas_call(kern, out_shape=(jax.ShapeDtypeStruct(piece, low), jax.Sha...]
    pallas_call x1, Pallas kernels: 14.2 us -> 12.9 us  [tail_exchange(): pl.pallas_call(functools.partial(tail_kernel, n, hn), out_shape=(jax.Shap...]
where the time goes in v14:
time: 117 us
  Pallas kernels  85.9 us (73%)
  local copies, waits for them, and re-layouts  11.9 us (10%)
  other arithmetic  9.36 us (8%)
  matrix products  4.49 us (4%)
  starting transfers between devices  3.95 us (3%)
    pallas_call x1, Pallas kernels, scan_pieces(): pl.pallas_call(kern, out_shape=jax.ShapeDtypeStruct(piece, low), in_specs...  26.3 us
    pallas_call x1, Pallas kernels, scan_pieces(): pl.pallas_call(kern, out_shape=(jax.ShapeDtypeStruct(piece, low), jax.Sha...  25.5 us
    pallas_call x1, Pallas kernels, exchange(): pl.pallas_call(functools.partial(exchange_kernel, axis, n), out_shape=jax...  21.2 us
    pallas_call x1, Pallas kernels, tail_exchange(): pl.pallas_call(functools.partial(tail_kernel, n, hn), out_shape=(jax.Shap...  12.9 us
    unnamed x33, local copies, waits for them, and re-layouts  4.6 us
    ppermute x1, starting transfers between devices, passed_along(): return lax.ppermute(block, axis, route)  3.95 us
  transfers between devices with their start and end apart: 1, of which 0 were waited for; matrix products, arithmetic and copies ran while one was open for 1% of the time, Pallas kernels for 0%

profile of v14, /device:TPU:1, one launch (start us, length us, event | category | flops | bytes accessed | tf_op | source)
XLA Modules:
  0.0 116.7 jit_solution(15907741861671664649)
XLA Ops:
  0.6 0.7 slice.139
  1.4 0.7 slice_bitcast_fusion.8
  2.1 3.9 %collective-permute-start = (bf16[3,1280]{1,0:T(4,128)(2,1)S(1)}, bf16[3,1280]{1,0:T(4,128)(2,1)S(1)}, u32[]{:S(2)}, u32[]{:S(2)}) collective-permute-start(bf16[3,1280]{1,0:T(4,128)(2,1)S(1)} %pad_maximum_fusion.3), channel_id=1, source_target_pairs={{0,16},{16,32},{32,48},{48,64},{64,80},{80,96},{96,112},{112,128},... | collective-permute-start | bytes 23048 | tf_op jit(solution)/shard_map/ppermute | solution.py:338
  6.1 0.6 copy-done.14
  6.8 0.3 reduce_window_sum.17
  7.1 0.2 slice_reduce_fusion
  7.5 0.7 copy-done.12
  8.7 0.7 copy-done.4
  9.4 0.3 multiply_convert_fusion.4
  9.8 0.2 copy.90
  9.9 0.3 convolution_convert_fusion.1
  10.3 0.8 pad_maximum_fusion.1.refs_0_
  11.0 25.5 %shard_map.147 = (bf16[32,32,128]{2,1,0:T(8,128)(2,1)}, f32[32,8,128]{2,1,0:T(8,128)}) custom-call(bf16[32,48,128]{2,1,0:T(8,128)(2,1)} %pad_maximum_fusion.1.refs_0_), custom_call_target="tpu_custom_call" | custom-call | tf_op jit(solution)/shard_map/pallas_call | solution.py:215
  36.5 1.1 copy.64
  37.6 0.2 fusion.40
  37.9 0.6 copy-done.15
  38.5 0.4 fusion.1
  38.9 0.2 copy.87
  39.1 0.7 copy-done.2
  39.9 0.3 multiply_reduce_fusion.5
  40.3 0.6 broadcast_in_dim.36.in_ref
  41.0 21.2 %shard_map.148 = f32[16,8,128]{2,1,0:T(8,128)} custom-call(f32[16,8,128]{2,1,0:T(8,128)} %broadcast_in_dim.36.in_ref), custom_call_target="tpu_custom_call" | custom-call | tf_op jit(solution)/shard_map/pallas_call | solution.py:55
  62.2 0.9 reduce_sum.130
  63.1 1.1 fusion.22
  64.2 0.2 copy.91
  64.4 0.5 multiply_reduce_fusion.6
  65.0 0.4 copy-done.1
  65.4 0.3 fusion.4
  65.7 1.3 %convolution_convert_fusion = bf16[8,128,128]{2,1,0:T(8,128)(2,1)} fusion(bf16[128,8,128]{0,2,1:T(8,128)(2,1)S(1)} %bitcast.116, f32[128,128]{1,0:T(8,128)S(1)} %get-tuple-element.40, f32[8,128]{1,0:T(8,128)S(1)} %get-tuple-element.48), kind=kOutput, calls=%fused_computation.10 | convolution fusion | flops 33947648 | bytes 593920 | tf_op jit(solution)/shard_map/htn,thp->hnp/dot_general | solution.py:481
  67.0 26.3 %shard_map.149 = bf16[32,32,128]{2,1,0:T(8,128)(2,1)} custom-call(bf16[32,32,128]{2,1,0:T(8,128)(2,1)} %bitcast.129, f32[32,8,128]{2,1,0:T(8,128)} %get-tuple-element.21.refs_1_), custom_call_target="tpu_custom_call" | custom-call | tf_op jit(solution)/shard_map/pallas_call | solution.py:223
  93.3 1.3 %multiply_reduce_fusion = f32[32]{0:T(128)S(1)} fusion(bf16[32,32,128]{2,1,0:T(8,128)(2,1)S(1)} %copy-done.1, bf16[32,32,128]{2,1,0:T(8,128)(2,1)} %shard_map.149), kind=kLoop, calls=%fused_computation.51 | loop fusion | flops 524256 | bytes 524416 | tf_op jit(solution)/shard_map/reduce_sum | solution.py:495
  94.6 0.2 multiply_reduce_fusion.1
  94.9 0.3 convolution_bitcast_fusion
  95.9 0.3 reduce_window_sum.18
  96.3 0.3 fusion.6
  96.6 0.2 fusion.5
  96.8 0.4 fusion.3
  97.2 0.2 copy.88
  97.6 0.9 gather_fusion
  98.5 0.7 copy.81.in_ref
  99.3 0.2 multiply_multiply_fusion
  99.4 0.5 copy-done.13
  100.0 0.6 select_maximum_fusion.rim_ref
  100.6 12.9 %shard_map.150 = (f32[24,128]{1,0:T(8,128)}, f32[8,1024]{1,0:T(8,128)}) custom-call(f32[16,24,128]{2,1,0:T(8,128)} %copy.81.in_ref, f32[8,1152]{1,0:T(8,128)} %select_maximum_fusion.rim_ref), custom_call_target="tpu_custom_call" | custom-call | tf_op jit(solution)/shard_map/pallas_call | solution.py:307
  113.5 0.7 reshape.209
  114.3 0.6 fusion.42
  115.0 0.9 fusion.12
  116.0 0.7 divide_multiply_fusion
  (71 shorter events, 2.5 us)
Async XLA Ops:
  2.1 6.2 %collective-permute-start = (bf16[3,1280]{1,0:T(4,128)(2,1)S(1)}, bf16[3,1280]{1,0:T(4,128)(2,1)S(1)}, u32[]{:S(2)}, u32[]{:S(2)}) collective-permute-start(bf16[3,1280]{1,0:T(4,128)(2,1)S(1)} %pad_maximum_fusion.3), channel_id=1, source_target_pairs={{0,16},{16,32},{32,48},{48,64},{64,80},{80,96},{96,112},{112,128},... | collective-permute-start | bytes 23048 | tf_op jit(solution)/shard_map/ppermute | solution.py:338
  6.0 0.7 copy-start.7
  6.0 0.7 copy-start.14
  6.1 0.7 copy-start.11
  6.7 0.7 copy-start.10
  6.7 0.7 copy-start.8
  6.7 1.5 %copy-start.5 = (bf16[2,128,128]{2,1,0:T(8,128)(2,1)S(1)}, bf16[2,128,128]{2,1,0:T(8,128)(2,1)}, u32[]{:S(2)}) copy-start(bf16[2,128,128]{2,1,0:T(8,128)(2,1)} %param.16) | copy-start | bytes 196612
  7.4 0.7 copy-start.12
  8.4 1.0 copy-start.4
  37.8 0.7 copy-start.15
  38.9 1.0 copy-start.2
  38.9 1.0 copy-start.3
  38.9 1.0 copy-start.6
  64.4 1.0 copy-start.1
  93.3 1.4 %copy-start = (bf16[32,32,128]{2,1,0:T(8,128)(2,1)S(1)}, bf16[32,32,128]{2,1,0:T(8,128)(2,1)}, u32[]{:S(2)}) copy-start(bf16[32,32,128]{2,1,0:T(8,128)(2,1)} %shard_map.149) | copy-start | bytes 786436
  99.3 0.7 copy-start.13
  114.3 0.8 copy-start.9

commit v15 on v14

--- a/solution.py
+++ b/solution.py
@@ -73,7 +73,7 @@
         return tuple(k if a == axis else coords[a] for a in AXES)
 
     copies = []
-    for i in range(1, n):
+    for i in sorted(range(1, n), key=lambda i: -min(i, n - i)):
         peer = lax.rem(me + i, n)
         copy = pltpu.make_async_remote_copy(
             src_ref=src_of(peer),

time: 117 us -> 118 us (level)
    pallas_call x1, Pallas kernels: 26.3 us -> 27.9 us  [scan_pieces(): pl.pallas_call(kern, out_shape=jax.ShapeDtypeStruct(piece, low), in_specs...]
where the time goes in v15:
time: 118 us; the launch traced here: 117 us
  Pallas kernels  85.9 us (73%)
  local copies, waits for them, and re-layouts  11.9 us (10%)
  other arithmetic  9.36 us (8%)
  matrix products  4.5 us (4%)
  starting transfers between devices  3.95 us (3%)
    pallas_call x1, Pallas kernels, scan_pieces(): pl.pallas_call(kern, out_shape=jax.ShapeDtypeStruct(piece, low), in_specs...  27.9 us
    pallas_call x1, Pallas kernels, scan_pieces(): pl.pallas_call(kern, out_shape=(jax.ShapeDtypeStruct(piece, low), jax.Sha...  24.5 us
    pallas_call x1, Pallas kernels, exchange(): pl.pallas_call(functools.partial(exchange_kernel, axis, n), out_shape=jax...  20.5 us
    pallas_call x1, Pallas kernels, tail_exchange(): pl.pallas_call(functools.partial(tail_kernel, n, hn), out_shape=(jax.Shap...  13.1 us
    unnamed x33, local copies, waits for them, and re-layouts  4.6 us
    ppermute x1, starting transfers between devices, passed_along(): return lax.ppermute(block, axis, route)  3.95 us
  transfers between devices with their start and end apart: 1, of which 0 were waited for; matrix products, arithmetic and copies ran while one was open for 1% of the time, Pallas kernels for 0%

profile of v15, /device:TPU:1, one launch (start us, length us, event | category | flops | bytes accessed | tf_op | source)
XLA Modules:
  0.0 116.7 jit_solution(17077188842598508991)
XLA Ops:
  0.6 0.7 slice.139
  1.4 0.7 slice_bitcast_fusion.8
  2.1 3.9 %collective-permute-start = (bf16[3,1280]{1,0:T(4,128)(2,1)S(1)}, bf16[3,1280]{1,0:T(4,128)(2,1)S(1)}, u32[]{:S(2)}, u32[]{:S(2)}) collective-permute-start(bf16[3,1280]{1,0:T(4,128)(2,1)S(1)} %pad_maximum_fusion.3), channel_id=1, source_target_pairs={{0,16},{16,32},{32,48},{48,64},{64,80},{80,96},{96,112},{112,128},... | collective-permute-start | bytes 23048 | tf_op jit(solution)/shard_map/ppermute | solution.py:338
  6.1 0.6 copy-done.14
  6.8 0.3 reduce_window_sum.17
  7.1 0.2 slice_reduce_fusion
  7.5 0.7 copy-done.12
  8.7 0.7 copy-done.4
  9.4 0.3 multiply_convert_fusion.4
  9.8 0.2 copy.90
  9.9 0.3 convolution_convert_fusion.1
  10.3 0.8 pad_maximum_fusion.1.refs_0_
  11.0 24.5 %shard_map.147 = (bf16[32,32,128]{2,1,0:T(8,128)(2,1)}, f32[32,8,128]{2,1,0:T(8,128)}) custom-call(bf16[32,48,128]{2,1,0:T(8,128)(2,1)} %pad_maximum_fusion.1.refs_0_), custom_call_target="tpu_custom_call" | custom-call | tf_op jit(solution)/shard_map/pallas_call | solution.py:215
  35.5 1.1 copy.64
  36.7 0.2 fusion.40
  36.9 0.6 copy-done.15
  37.6 0.4 fusion.1
  38.0 0.2 copy.87
  38.2 0.7 copy-done.2
  39.0 0.3 multiply_reduce_fusion.5
  39.4 0.6 broadcast_in_dim.36.in_ref
  40.0 20.5 %shard_map.148 = f32[16,8,128]{2,1,0:T(8,128)} custom-call(f32[16,8,128]{2,1,0:T(8,128)} %broadcast_in_dim.36.in_ref), custom_call_target="tpu_custom_call" | custom-call | tf_op jit(solution)/shard_map/pallas_call | solution.py:55
  60.5 0.9 reduce_sum.130
  61.4 1.1 fusion.22
  62.5 0.2 copy.91
  62.7 0.5 multiply_reduce_fusion.6
  63.3 0.4 copy-done.1
  63.7 0.3 fusion.4
  64.0 1.3 %convolution_convert_fusion = bf16[8,128,128]{2,1,0:T(8,128)(2,1)} fusion(bf16[128,8,128]{0,2,1:T(8,128)(2,1)S(1)} %bitcast.116, f32[128,128]{1,0:T(8,128)S(1)} %get-tuple-element.40, f32[8,128]{1,0:T(8,128)S(1)} %get-tuple-element.48), kind=kOutput, calls=%fused_computation.10 | convolution fusion | flops 33947648 | bytes 593920 | tf_op jit(solution)/shard_map/htn,thp->hnp/dot_general | solution.py:481
  65.3 27.9 %shard_map.149 = bf16[32,32,128]{2,1,0:T(8,128)(2,1)} custom-call(bf16[32,32,128]{2,1,0:T(8,128)(2,1)} %bitcast.129, f32[32,8,128]{2,1,0:T(8,128)} %get-tuple-element.21.refs_1_), custom_call_target="tpu_custom_call" | custom-call | tf_op jit(solution)/shard_map/pallas_call | solution.py:223
  93.2 1.3 %multiply_reduce_fusion = f32[32]{0:T(128)S(1)} fusion(bf16[32,32,128]{2,1,0:T(8,128)(2,1)S(1)} %copy-done.1, bf16[32,32,128]{2,1,0:T(8,128)(2,1)} %shard_map.149), kind=kLoop, calls=%fused_computation.51 | loop fusion | flops 524256 | bytes 524416 | tf_op jit(solution)/shard_map/reduce_sum | solution.py:495
  94.5 0.2 multiply_reduce_fusion.1
  94.7 0.3 convolution_bitcast_fusion
  95.8 0.3 reduce_window_sum.18
  96.2 0.3 fusion.6
  96.5 0.2 fusion.5
  96.7 0.4 fusion.3
  97.1 0.2 copy.88
  97.5 0.9 gather_fusion
  98.4 0.7 copy.81.in_ref
  99.1 0.2 multiply_multiply_fusion
  99.3 0.5 copy-done.13
  99.9 0.6 select_maximum_fusion.rim_ref
  100.5 13.1 %shard_map.150 = (f32[24,128]{1,0:T(8,128)}, f32[8,1024]{1,0:T(8,128)}) custom-call(f32[16,24,128]{2,1,0:T(8,128)} %copy.81.in_ref, f32[8,1152]{1,0:T(8,128)} %select_maximum_fusion.rim_ref), custom_call_target="tpu_custom_call" | custom-call | tf_op jit(solution)/shard_map/pallas_call | solution.py:307
  113.5 0.7 reshape.209
  114.3 0.6 fusion.42
  115.1 0.9 fusion.12
  116.0 0.7 divide_multiply_fusion
  (71 shorter events, 2.5 us)
Async XLA Ops:
  2.1 6.2 %collective-permute-start = (bf16[3,1280]{1,0:T(4,128)(2,1)S(1)}, bf16[3,1280]{1,0:T(4,128)(2,1)S(1)}, u32[]{:S(2)}, u32[]{:S(2)}) collective-permute-start(bf16[3,1280]{1,0:T(4,128)(2,1)S(1)} %pad_maximum_fusion.3), channel_id=1, source_target_pairs={{0,16},{16,32},{32,48},{48,64},{64,80},{80,96},{96,112},{112,128},... | collective-permute-start | bytes 23048 | tf_op jit(solution)/shard_map/ppermute | solution.py:338
  6.0 0.7 copy-start.7
  6.0 0.7 copy-start.14
  6.1 0.7 copy-start.11
  6.7 0.7 copy-start.10
  6.7 0.7 copy-start.8
  6.7 1.5 %copy-start.5 = (bf16[2,128,128]{2,1,0:T(8,128)(2,1)S(1)}, bf16[2,128,128]{2,1,0:T(8,128)(2,1)}, u32[]{:S(2)}) copy-start(bf16[2,128,128]{2,1,0:T(8,128)(2,1)} %param.16) | copy-start | bytes 196612
  7.4 0.7 copy-start.12
  8.4 1.0 copy-start.4
  36.9 0.7 copy-start.15
  37.9 1.0 copy-start.2
  38.0 1.0 copy-start.3
  38.0 1.0 copy-start.6
  62.7 1.0 copy-start.1
  93.2 1.4 %copy-start = (bf16[32,32,128]{2,1,0:T(8,128)(2,1)S(1)}, bf16[32,32,128]{2,1,0:T(8,128)(2,1)}, u32[]{:S(2)}) copy-start(bf16[32,32,128]{2,1,0:T(8,128)(2,1)} %shard_map.149) | copy-start | bytes 786436
  99.1 0.7 copy-start.13
  114.3 0.8 copy-start.9

commit v16 on v15

--- a/solution.py
+++ b/solution.py
@@ -22,7 +22,8 @@
         pl.semaphore_signal(barrier, inc=1, device_id=dev(lax.rem(me + i, n)), device_id_type=MESH)
     pl.semaphore_wait(barrier, n - 1)
     copies = []
-    for i in range(1, n):
+    order = sorted(range(1, n), key=lambda i: -min(i, n - i))
+    for i in order:
         peer = lax.rem(me + i, n)
         copy = pltpu.make_async_remote_copy(
             src_ref=in_ref.at[peer],
@@ -35,8 +36,9 @@
         copy.start()
         copies.append(copy)
     land[me] = in_ref[me]
+    for c in copies:
+        c.wait_send()
     for i in range(1, n):
-        copies[i - 1].wait_send()
         src = lax.rem(me + (n - i), n)
         incoming = pltpu.make_async_remote_copy(
             src_ref=in_ref.at[src],

time: 118 us -> 117 us (level)
  no operation moved by 1% of the time
where the time goes in v16:
time: 117 us; the launch traced here: 116 us
  Pallas kernels  85 us (73%)
  local copies, waits for them, and re-layouts  11.9 us (10%)
  other arithmetic  9.36 us (8%)
  matrix products  4.5 us (4%)
  starting transfers between devices  3.95 us (3%)
    pallas_call x1, Pallas kernels, scan_pieces(): pl.pallas_call(kern, out_shape=jax.ShapeDtypeStruct(piece, low), in_specs...  27.9 us
    pallas_call x1, Pallas kernels, scan_pieces(): pl.pallas_call(kern, out_shape=(jax.ShapeDtypeStruct(piece, low), jax.Sha...  24.5 us
    pallas_call x1, Pallas kernels, exchange(): pl.pallas_call(functools.partial(exchange_kernel, axis, n), out_shape=jax...  20.5 us
    pallas_call x1, Pallas kernels, tail_exchange(): pl.pallas_call(functools.partial(tail_kernel, n, hn), out_shape=(jax.Shap...  12.2 us
    unnamed x33, local copies, waits for them, and re-layouts  4.6 us
    ppermute x1, starting transfers between devices, passed_along(): return lax.ppermute(block, axis, route)  3.95 us
  transfers between devices with their start and end apart: 1, of which 0 were waited for; matrix products, arithmetic and copies ran while one was open for 1% of the time, Pallas kernels for 0%

profile of v16, /device:TPU:1, one launch (start us, length us, event | category | flops | bytes accessed | tf_op | source)
XLA Modules:
  0.0 115.8 jit_solution(7417922683838878373)
XLA Ops:
  0.6 0.7 slice.139
  1.4 0.7 slice_bitcast_fusion.8
  2.1 3.9 %collective-permute-start = (bf16[3,1280]{1,0:T(4,128)(2,1)S(1)}, bf16[3,1280]{1,0:T(4,128)(2,1)S(1)}, u32[]{:S(2)}, u32[]{:S(2)}) collective-permute-start(bf16[3,1280]{1,0:T(4,128)(2,1)S(1)} %pad_maximum_fusion.3), channel_id=1, source_target_pairs={{0,16},{16,32},{32,48},{48,64},{64,80},{80,96},{96,112},{112,128},... | collective-permute-start | bytes 23048 | tf_op jit(solution)/shard_map/ppermute | solution.py:340
  6.1 0.6 copy-done.14
  6.8 0.3 reduce_window_sum.17
  7.1 0.2 slice_reduce_fusion
  7.5 0.7 copy-done.12
  8.7 0.7 copy-done.4
  9.4 0.3 multiply_convert_fusion.4
  9.8 0.2 copy.90
  9.9 0.3 convolution_convert_fusion.1
  10.3 0.8 pad_maximum_fusion.1.refs_0_
  11.0 24.5 %shard_map.147 = (bf16[32,32,128]{2,1,0:T(8,128)(2,1)}, f32[32,8,128]{2,1,0:T(8,128)}) custom-call(bf16[32,48,128]{2,1,0:T(8,128)(2,1)} %pad_maximum_fusion.1.refs_0_), custom_call_target="tpu_custom_call" | custom-call | tf_op jit(solution)/shard_map/pallas_call | solution.py:217
  35.5 1.1 copy.64
  36.7 0.2 fusion.40
  36.9 0.6 copy-done.15
  37.6 0.4 fusion.1
  38.0 0.2 copy.87
  38.2 0.7 copy-done.2
  39.0 0.3 multiply_reduce_fusion.5
  39.4 0.6 broadcast_in_dim.36.in_ref
  40.0 20.5 %shard_map.148 = f32[16,8,128]{2,1,0:T(8,128)} custom-call(f32[16,8,128]{2,1,0:T(8,128)} %broadcast_in_dim.36.in_ref), custom_call_target="tpu_custom_call" | custom-call | tf_op jit(solution)/shard_map/pallas_call | solution.py:57
  60.5 0.9 reduce_sum.130
  61.4 1.1 fusion.22
  62.5 0.2 copy.91
  62.7 0.5 multiply_reduce_fusion.6
  63.3 0.4 copy-done.1
  63.7 0.3 fusion.4
  64.0 1.3 %convolution_convert_fusion = bf16[8,128,128]{2,1,0:T(8,128)(2,1)} fusion(bf16[128,8,128]{0,2,1:T(8,128)(2,1)S(1)} %bitcast.116, f32[128,128]{1,0:T(8,128)S(1)} %get-tuple-element.40, f32[8,128]{1,0:T(8,128)S(1)} %get-tuple-element.48), kind=kOutput, calls=%fused_computation.10 | convolution fusion | flops 33947648 | bytes 593920 | tf_op jit(solution)/shard_map/htn,thp->hnp/dot_general | solution.py:483
  65.3 27.9 %shard_map.149 = bf16[32,32,128]{2,1,0:T(8,128)(2,1)} custom-call(bf16[32,32,128]{2,1,0:T(8,128)(2,1)} %bitcast.129, f32[32,8,128]{2,1,0:T(8,128)} %get-tuple-element.21.refs_1_), custom_call_target="tpu_custom_call" | custom-call | tf_op jit(solution)/shard_map/pallas_call | solution.py:225
  93.2 1.3 %multiply_reduce_fusion = f32[32]{0:T(128)S(1)} fusion(bf16[32,32,128]{2,1,0:T(8,128)(2,1)S(1)} %copy-done.1, bf16[32,32,128]{2,1,0:T(8,128)(2,1)} %shard_map.149), kind=kLoop, calls=%fused_computation.51 | loop fusion | flops 524256 | bytes 524416 | tf_op jit(solution)/shard_map/reduce_sum | solution.py:497
  94.5 0.2 multiply_reduce_fusion.1
  94.7 0.3 convolution_bitcast_fusion
  95.8 0.3 reduce_window_sum.18
  96.2 0.3 fusion.6
  96.5 0.2 fusion.5
  96.7 0.4 fusion.3
  97.1 0.2 copy.88
  97.5 0.9 gather_fusion
  98.4 0.7 copy.81.in_ref
  99.1 0.2 multiply_multiply_fusion
  99.3 0.5 copy-done.13
  99.9 0.6 select_maximum_fusion.rim_ref
  100.5 12.2 %shard_map.150 = (f32[24,128]{1,0:T(8,128)}, f32[8,1024]{1,0:T(8,128)}) custom-call(f32[16,24,128]{2,1,0:T(8,128)} %copy.81.in_ref, f32[8,1152]{1,0:T(8,128)} %select_maximum_fusion.rim_ref), custom_call_target="tpu_custom_call" | custom-call | tf_op jit(solution)/shard_map/pallas_call | solution.py:309
  112.7 0.7 reshape.209
  113.4 0.6 fusion.42
  114.2 0.9 fusion.12
  115.2 0.7 divide_multiply_fusion
  (71 shorter events, 2.5 us)
Async XLA Ops:
  2.1 6.2 %collective-permute-start = (bf16[3,1280]{1,0:T(4,128)(2,1)S(1)}, bf16[3,1280]{1,0:T(4,128)(2,1)S(1)}, u32[]{:S(2)}, u32[]{:S(2)}) collective-permute-start(bf16[3,1280]{1,0:T(4,128)(2,1)S(1)} %pad_maximum_fusion.3), channel_id=1, source_target_pairs={{0,16},{16,32},{32,48},{48,64},{64,80},{80,96},{96,112},{112,128},... | collective-permute-start | bytes 23048 | tf_op jit(solution)/shard_map/ppermute | solution.py:340
  6.0 0.7 copy-start.7
  6.0 0.7 copy-start.14
  6.1 0.7 copy-start.11
  6.7 0.7 copy-start.10
  6.7 0.7 copy-start.8
  6.7 1.5 %copy-start.5 = (bf16[2,128,128]{2,1,0:T(8,128)(2,1)S(1)}, bf16[2,128,128]{2,1,0:T(8,128)(2,1)}, u32[]{:S(2)}) copy-start(bf16[2,128,128]{2,1,0:T(8,128)(2,1)} %param.16) | copy-start | bytes 196612
  7.4 0.7 copy-start.12
  8.4 1.0 copy-start.4
  36.9 0.7 copy-start.15
  37.9 1.0 copy-start.2
  38.0 1.0 copy-start.3
  38.0 1.0 copy-start.6
  62.7 1.0 copy-start.1
  93.2 1.4 %copy-start = (bf16[32,32,128]{2,1,0:T(8,128)(2,1)S(1)}, bf16[32,32,128]{2,1,0:T(8,128)(2,1)}, u32[]{:S(2)}) copy-start(bf16[32,32,128]{2,1,0:T(8,128)(2,1)} %shard_map.149) | copy-start | bytes 786436
  99.1 0.7 copy-start.13
  113.4 0.8 copy-start.9

commit v17 on v16

--- a/solution.py
+++ b/solution.py
@@ -10,7 +10,7 @@
 AXES = ("seq", "head")
 
 
-def exchange_kernel(axis, n, in_ref, out_ref, land, send_sem, recv_sem):
+def gather_sum_kernel(axis, n, in_ref, out_ref, land, send_sem, recv_sem):
     me = lax.axis_index(axis)
     coords = {a: lax.axis_index(a) for a in AXES}
 
@@ -26,7 +26,7 @@
     for i in order:
         peer = lax.rem(me + i, n)
         copy = pltpu.make_async_remote_copy(
-            src_ref=in_ref.at[peer],
+            src_ref=in_ref,
             dst_ref=land.at[me],
             send_sem=send_sem.at[i],
             recv_sem=recv_sem.at[i],
@@ -35,13 +35,13 @@
         )
         copy.start()
         copies.append(copy)
-    land[me] = in_ref[me]
+    land[me] = in_ref[...]
     for c in copies:
         c.wait_send()
     for i in range(1, n):
         src = lax.rem(me + (n - i), n)
         incoming = pltpu.make_async_remote_copy(
-            src_ref=in_ref.at[src],
+            src_ref=in_ref,
             dst_ref=land.at[src],
             send_sem=send_sem.at[i],
             recv_sem=recv_sem.at[i],
@@ -49,18 +49,21 @@
             device_id_type=MESH,
         )
         incoming.wait_recv()
-    out_ref[...] = land[...]
-
-
-def exchange(x, axis, cid):
+    total = land[0]
+    for j in range(1, n):
+        total = total + land[j]
+    out_ref[...] = total
+
+
+def gather_sum(x, axis, cid):
     n = lax.axis_size(axis)
     return pl.pallas_call(
-        functools.partial(exchange_kernel, axis, n),
+        functools.partial(gather_sum_kernel, axis, n),
         out_shape=jax.ShapeDtypeStruct(x.shape, x.dtype),
         in_specs=[pl.BlockSpec(memory_space=pltpu.VMEM)],
         out_specs=pl.BlockSpec(memory_space=pltpu.VMEM),
         scratch_shapes=[
-            pltpu.VMEM(x.shape, x.dtype),
+            pltpu.VMEM((n,) + x.shape, x.dtype),
             pltpu.SemaphoreType.DMA((n,)),
             pltpu.SemaphoreType.DMA((n,)),
         ],
@@ -470,7 +473,7 @@
     hcount = lax.axis_size("head")
     own_sums = jnp.stack([jnp.sum(gated * gated, axis=1), jnp.sum(scaled * gated, axis=1)])
     own_sums = jnp.concatenate([own_sums, jnp.zeros((6, length), f32)], axis=0)
-    sums = jnp.sum(exchange(jnp.broadcast_to(own_sums, (hcount,) + own_sums.shape), "head", 3), axis=0)
+    sums = gather_sum(own_sums, "head", 3)
     inv_rms = lax.rsqrt(sums[0] / INNER + EPS)
     normed = gated * inv_rms[:, None]
     mean_dot = inv_rms * sums[1] / INNER

time: 117 us -> 122 us (1.043)
  local copies, waits for them, and re-layouts: 11.9 us -> 14.5 us
  other arithmetic: 9.36 us -> 11.7 us
    unnamed x33 -> x75, local copies, waits for them, and re-layouts: 4.6 us -> 7.62 us
  transfers between devices with their start and end apart: 1 -> 1, of which waited for: 0 -> 0; matrix products, arithmetic and copies ran while one was open for 1% -> 2% of each run, Pallas kernels for 0% -> 0%
where the time goes in v17:
time: 122 us; the launch traced here: 121 us
  Pallas kernels  85.1 us (70%)
  local copies, waits for them, and re-layouts  14.5 us (12%)
  other arithmetic  11.7 us (10%)
  matrix products  4.48 us (4%)
  starting transfers between devices  3.95 us (3%)
  between operations  1.22 us (1%)
    pallas_call x1, Pallas kernels, scan_pieces(): pl.pallas_call(kern, out_shape=jax.ShapeDtypeStruct(piece, low), in_specs...  27.9 us
    pallas_call x1, Pallas kernels, scan_pieces(): pl.pallas_call(kern, out_shape=(jax.ShapeDtypeStruct(piece, low), jax.Sha...  24.3 us
    pallas_call x1, Pallas kernels, gather_sum(): pl.pallas_call(functools.partial(gather_sum_kernel, axis, n), out_shape=j...  20.9 us
    pallas_call x1, Pallas kernels, tail_exchange(): pl.pallas_call(functools.partial(tail_kernel, n, hn), out_shape=(jax.Shap...  11.9 us
    unnamed x75, local copies, waits for them, and re-layouts  7.62 us
    ppermute x1, starting transfers between devices, passed_along(): return lax.ppermute(block, axis, route)  3.95 us
  transfers between devices with their start and end apart: 1, of which 0 were waited for; matrix products, arithmetic and copies ran while one was open for 2% of the time, Pallas kernels for 0%

profile of v17, /device:TPU:1, one launch (start us, length us, event | category | flops | bytes accessed | tf_op | source)
XLA Modules:
  0.0 120.9 jit_solution(305396365272618396)
XLA Ops:
  0.6 0.7 slice.139
  1.4 0.7 slice_bitcast_fusion.8
  2.1 3.9 %collective-permute-start = (bf16[3,1280]{1,0:T(4,128)(2,1)S(1)}, bf16[3,1280]{1,0:T(4,128)(2,1)S(1)}, u32[]{:S(2)}, u32[]{:S(2)}) collective-permute-start(bf16[3,1280]{1,0:T(4,128)(2,1)S(1)} %pad_maximum_fusion.3), channel_id=1, source_target_pairs={{0,16},{16,32},{32,48},{48,64},{64,80},{80,96},{96,112},{112,128},... | collective-permute-start | bytes 23048 | tf_op jit(solution)/shard_map/ppermute | solution.py:343
  6.1 0.6 copy-done.35
  6.8 0.3 reduce_window_sum.17
  7.3 0.5 copy-done.29
  7.8 0.6 fusion.59
  8.5 0.6 copy-done.33
  9.2 0.6 pad_clamp_fusion
  10.4 0.7 copy-done.4
  11.1 0.3 multiply_convert_fusion.4
  11.6 0.3 convolution_convert_fusion.1
  12.0 0.8 pad_maximum_fusion.1.refs_0_
  12.8 24.3 %shard_map.147 = (bf16[32,32,128]{2,1,0:T(8,128)(2,1)}, f32[32,8,128]{2,1,0:T(8,128)}) custom-call(bf16[32,48,128]{2,1,0:T(8,128)(2,1)} %pad_maximum_fusion.1.refs_0_), custom_call_target="tpu_custom_call" | custom-call | tf_op jit(solution)/shard_map/pallas_call | solution.py:220
  37.1 1.1 copy.64
  38.5 0.6 copy-done.36
  39.1 0.4 fusion.1
  39.8 0.7 copy-done.2
  40.6 0.3 multiply_reduce_fusion.5
  40.9 0.7 maximum_maximum_fusion.in_ref
  41.5 20.9 %shard_map.148 = f32[8,128]{1,0:T(8,128)} custom-call(f32[8,128]{1,0:T(8,128)} %maximum_maximum_fusion.in_ref), custom_call_target="tpu_custom_call" | custom-call | tf_op jit(solution)/shard_map/pallas_call | solution.py:60
  62.4 0.8 fusion.51
  63.2 0.7 rsqrt_bitcast_fusion
  63.9 1.1 fusion.22
  65.3 0.6 copy-done.17
  65.9 0.5 multiply_reduce_fusion.6
  66.5 0.4 copy-done.1
  66.9 0.3 fusion.4
  67.2 1.3 %convolution_convert_fusion = bf16[8,128,128]{2,1,0:T(8,128)(2,1)} fusion(bf16[128,8,128]{0,2,1:T(8,128)(2,1)S(1)} %bitcast.116, f32[128,128]{1,0:T(8,128)S(1)} %get-tuple-element.40, f32[8,128]{1,0:T(8,128)S(1)} %copy-done.12), kind=kOutput, calls=%fused_computation.10 | convolution fusion | flops 33947648 | bytes 593920 | tf_op jit(solution)/shard_map/htn,thp->hnp/dot_general | solution.py:486
  68.5 27.9 %shard_map.149 = bf16[32,32,128]{2,1,0:T(8,128)(2,1)} custom-call(bf16[32,32,128]{2,1,0:T(8,128)(2,1)} %bitcast.129, f32[32,8,128]{2,1,0:T(8,128)} %get-tuple-element.21.refs_1_), custom_call_target="tpu_custom_call" | custom-call | tf_op jit(solution)/shard_map/pallas_call | solution.py:228
  96.4 1.3 %multiply_reduce_fusion = f32[32]{0:T(128)S(1)} fusion(bf16[32,32,128]{2,1,0:T(8,128)(2,1)S(1)} %copy-done.1, bf16[32,32,128]{2,1,0:T(8,128)(2,1)} %shard_map.149), kind=kLoop, calls=%fused_computation.51 | loop fusion | flops 524256 | bytes 524416 | tf_op jit(solution)/shard_map/reduce_sum | solution.py:500
  97.8 0.2 multiply_reduce_fusion.1
  98.0 0.3 convolution_bitcast_fusion
  99.0 0.3 reduce_window_sum.18
  99.5 0.3 fusion.6
  100.0 0.4 fusion.3
  100.7 1.0 gather_fusion
  101.8 0.7 copy.81.in_ref
  102.7 0.5 copy-done.34
  103.2 0.6 select_maximum_fusion.rim_ref
  103.9 11.9 %shard_map.150 = (f32[24,128]{1,0:T(8,128)}, f32[8,1024]{1,0:T(8,128)}) custom-call(f32[16,24,128]{2,1,0:T(8,128)} %copy.81.in_ref, f32[8,1152]{1,0:T(8,128)} %select_maximum_fusion.rim_ref), custom_call_target="tpu_custom_call" | custom-call | tf_op jit(solution)/shard_map/pallas_call | solution.py:312
  115.8 0.7 reshape.209
  116.6 0.6 copy-done.21
  117.2 0.6 fusion.42
  118.0 0.7 copy-done.7
  118.6 0.9 fusion.12
  119.6 0.6 copy-done.30
  120.2 0.7 divide_multiply_fusion
  (111 shorter events, 3.9 us)
Async XLA Ops:
  2.1 7.8 %collective-permute-start = (bf16[3,1280]{1,0:T(4,128)(2,1)S(1)}, bf16[3,1280]{1,0:T(4,128)(2,1)S(1)}, u32[]{:S(2)}, u32[]{:S(2)}) collective-permute-start(bf16[3,1280]{1,0:T(4,128)(2,1)S(1)} %pad_maximum_fusion.3), channel_id=1, source_target_pairs={{0,16},{16,32},{32,48},{48,64},{64,80},{80,96},{96,112},{112,128},... | collective-permute-start | bytes 23048 | tf_op jit(solution)/shard_map/ppermute | solution.py:343
  6.0 0.7 copy-start.13
  6.0 32.4 %copy-start.16 = (pred[128,128]{1,0:T(8,128)(4,1)}, pred[128,128]{1,0:T(8,128)(4,1)S(1)}, u32[]{:S(2)}) copy-start(pred[128,128]{1,0:T(8,128)(4,1)S(1)} %iota_compare_fusion) | copy-start | bytes 49156
  6.1 0.7 copy-start.35
  6.1 0.7 copy-start.32
  6.7 1.7 %copy-start.31 = (f32[2,4,128]{2,1,0:T(4,128)S(1)}, f32[2,4,128]{2,1,0:T(4,128)}, u32[]{:S(2)}) copy-start(f32[2,4,128]{2,1,0:T(4,128)} %param.22) | copy-start | bytes 12292
  6.7 1.7 %copy-start.15 = (f32[4,1024]{1,0:T(4,128)S(1)}, f32[4,1024]{1,0:T(4,128)}, u32[]{:S(2)}) copy-start(f32[4,1024]{1,0:T(4,128)} %param.21) | copy-start | bytes 49156
  6.8 3.1 %copy-start.5 = (bf16[2,128,128]{2,1,0:T(8,128)(2,1)S(1)}, bf16[2,128,128]{2,1,0:T(8,128)(2,1)}, u32[]{:S(2)}) copy-start(bf16[2,128,128]{2,1,0:T(8,128)(2,1)} %param.16) | copy-start | bytes 196612
  6.8 31.7 %copy-start.18 = (f32[8,128]{1,0:T(8,128)}, f32[8,128]{1,0:T(8,128)S(1)}, u32[]{:S(2)}) copy-start(f32[8,128]{1,0:T(8,128)S(1)} %get-tuple-element.35) | copy-start | bytes 12292
  7.3 0.5 copy-start.29
  8.4 1.5 %copy-start.20 = (f32[2,1,128]{2,1,0:T(1,128)}, f32[2,1,128]{2,1,0:T(1,128)S(1)}, u32[]{:S(2)}) copy-start(f32[2,1,128]{2,1,0:T(1,128)S(1)} %get-tuple-element.51) | copy-start | bytes 3076
  8.5 1.5 %copy-start.22 = (f32[2,1,128]{2,1,0:T(1,128)}, f32[2,1,128]{2,1,0:T(1,128)S(1)}, u32[]{:S(2)}) copy-start(f32[2,1,128]{2,1,0:T(1,128)S(1)} %get-tuple-element.52) | copy-start | bytes 3076
  8.5 1.5 %copy-start.24 = (f32[2,1,128]{2,1,0:T(1,128)}, f32[2,1,128]{2,1,0:T(1,128)S(1)}, u32[]{:S(2)}) copy-start(f32[2,1,128]{2,1,0:T(1,128)S(1)} %get-tuple-element.53) | copy-start | bytes 3076
  8.5 1.5 %copy-start.26 = (f32[2,1,128]{2,1,0:T(1,128)}, f32[2,1,128]{2,1,0:T(1,128)S(1)}, u32[]{:S(2)}) copy-start(f32[2,1,128]{2,1,0:T(1,128)S(1)} %get-tuple-element.54) | copy-start | bytes 3076
  8.5 0.7 copy-start.33
  9.2 1.9 %copy-start.6 = (f32[1,1024]{1,0:T(1,128)}, f32[1,1024]{1,0:T(1,128)S(1)}, u32[]{:S(2)}) copy-start(f32[1,1024]{1,0:T(1,128)S(1)} %get-tuple-element.44) | copy-start | bytes 12292
  9.2 1.9 %copy-start.8 = (f32[1,1024]{1,0:T(1,128)}, f32[1,1024]{1,0:T(1,128)S(1)}, u32[]{:S(2)}) copy-start(f32[1,1024]{1,0:T(1,128)S(1)} %get-tuple-element.45) | copy-start | bytes 12292
  10.1 1.0 copy-start.4
  38.5 0.7 copy-start.36
  39.5 1.0 copy-start.2
  39.5 1.0 copy-start.3
  39.5 1.0 copy-start.10
  41.5 22.4 %copy-start.11 = (f32[1024]{0:T(1024)S(1)}, f32[1024]{0:T(1024)}, u32[]{:S(2)}) copy-start(f32[1024]{0:T(1024)} %param.23) | copy-start | bytes 12292
  65.2 0.7 copy-start.17
  65.2 0.7 copy-start.19
  65.9 1.0 copy-start.1
  65.9 1.0 copy-start.12
  96.4 1.4 %copy-start = (bf16[32,32,128]{2,1,0:T(8,128)(2,1)S(1)}, bf16[32,32,128]{2,1,0:T(8,128)(2,1)}, u32[]{:S(2)}) copy-start(bf16[32,32,128]{2,1,0:T(8,128)(2,1)} %shard_map.149) | copy-start | bytes 786436
  102.5 0.7 copy-start.34
  116.5 0.7 copy-start.21
  116.5 0.7 copy-start.23
  116.5 0.7 copy-start.25
  116.5 0.7 copy-start.27
  117.2 0.8 copy-start.28
  117.9 0.7 copy-start.7
  117.9 0.7 copy-start.9
  118.6 1.0 copy-start.14
  119.6 0.6 copy-start.30

commit v18 on v16

--- a/solution.py
+++ b/solution.py
@@ -535,7 +535,8 @@
     picks = jnp.array(picks, jnp.int32)
     piece_rows = picks.shape[1]
     bc_rows_z = jnp.concatenate([grad_bc_rows, jnp.zeros((2, 1, nstate), f32)], axis=1)
-    bc_pieces = jnp.moveaxis(jnp.take(bc_rows_z, picks.reshape(-1), axis=1).reshape(2, hcount, piece_rows, -1), 1, 0)
+    both = jnp.concatenate([picks, picks + (length + 1)], axis=1)
+    bc_pieces = jnp.take(bc_rows_z.reshape(2 * (length + 1), nstate), both.reshape(-1), axis=0)
     top = (grad_bc_rows[:, :3] * silu_grad(bc_pre[:, :3])).reshape(6, nstate)
     rim_send = jnp.concatenate(
         [jnp.pad(grad_x_pre[:3], ((0, 5), (0, 0))), jnp.pad(top, ((0, 2), (0, 0)))], axis=1

time: 117 us -> 116 us (level)
    unnamed x33 -> x32, local copies, waits for them, and re-layouts: 4.6 us -> 4.48 us
where the time goes in v18:
time: 116 us
  Pallas kernels  85 us (73%)
  local copies, waits for them, and re-layouts  11.8 us (10%)
  other arithmetic  9.38 us (8%)
  matrix products  4.49 us (4%)
  starting transfers between devices  3.95 us (3%)
    pallas_call x1, Pallas kernels, scan_pieces(): pl.pallas_call(kern, out_shape=jax.ShapeDtypeStruct(piece, low), in_specs...  27.7 us
    pallas_call x1, Pallas kernels, scan_pieces(): pl.pallas_call(kern, out_shape=(jax.ShapeDtypeStruct(piece, low), jax.Sha...  24.5 us
    pallas_call x1, Pallas kernels, exchange(): pl.pallas_call(functools.partial(exchange_kernel, axis, n), out_shape=jax...  20.5 us
    pallas_call x1, Pallas kernels, tail_exchange(): pl.pallas_call(functools.partial(tail_kernel, n, hn), out_shape=(jax.Shap...  12.4 us
    unnamed x32, local copies, waits for them, and re-layouts  4.48 us
    ppermute x1, starting transfers between devices, passed_along(): return lax.ppermute(block, axis, route)  3.95 us
  transfers between devices with their start and end apart: 1, of which 0 were waited for; matrix products, arithmetic and copies ran while one was open for 1% of the time, Pallas kernels for 0%

profile of v18, /device:TPU:1, one launch (start us, length us, event | category | flops | bytes accessed | tf_op | source)
XLA Modules:
  0.0 115.7 jit_solution(14821510744642133597)
XLA Ops:
  0.6 0.7 slice.139
  1.4 0.7 slice_bitcast_fusion.8
  2.1 3.9 %collective-permute-start = (bf16[3,1280]{1,0:T(4,128)(2,1)S(1)}, bf16[3,1280]{1,0:T(4,128)(2,1)S(1)}, u32[]{:S(2)}, u32[]{:S(2)}) collective-permute-start(bf16[3,1280]{1,0:T(4,128)(2,1)S(1)} %pad_maximum_fusion.3), channel_id=1, source_target_pairs={{0,16},{16,32},{32,48},{48,64},{64,80},{80,96},{96,112},{112,128},... | collective-permute-start | bytes 23048 | tf_op jit(solution)/shard_map/ppermute | solution.py:340
  6.1 0.6 copy-done.14
  6.8 0.3 reduce_window_sum.17
  7.1 0.2 slice_reduce_fusion
  7.5 0.7 copy-done.11
  8.7 0.7 copy-done.4
  9.4 0.3 multiply_convert_fusion.4
  9.8 0.2 copy.82
  9.9 0.3 convolution_convert_fusion.1
  10.3 0.8 pad_maximum_fusion.1.refs_0_
  11.0 24.5 %shard_map.147 = (bf16[32,32,128]{2,1,0:T(8,128)(2,1)}, f32[32,8,128]{2,1,0:T(8,128)}) custom-call(bf16[32,48,128]{2,1,0:T(8,128)(2,1)} %pad_maximum_fusion.1.refs_0_), custom_call_target="tpu_custom_call" | custom-call | tf_op jit(solution)/shard_map/pallas_call | solution.py:217
  35.5 1.1 copy.60
  36.7 0.2 fusion.40
  36.9 0.6 copy-done.15
  37.6 0.4 fusion.1
  38.0 0.2 copy.80
  38.2 0.7 copy-done.2
  39.0 0.3 multiply_reduce_fusion.5
  39.4 0.6 broadcast_in_dim.36.in_ref
  40.0 20.5 %shard_map.148 = f32[16,8,128]{2,1,0:T(8,128)} custom-call(f32[16,8,128]{2,1,0:T(8,128)} %broadcast_in_dim.36.in_ref), custom_call_target="tpu_custom_call" | custom-call | tf_op jit(solution)/shard_map/pallas_call | solution.py:57
  60.5 0.9 reduce_sum.130
  61.4 1.1 fusion.22
  62.5 0.2 copy.83
  62.7 0.5 multiply_reduce_fusion.6
  63.3 0.4 copy-done.1
  63.7 0.3 fusion.4
  64.0 1.3 %convolution_convert_fusion = bf16[8,128,128]{2,1,0:T(8,128)(2,1)} fusion(bf16[128,8,128]{0,2,1:T(8,128)(2,1)S(1)} %bitcast.111, f32[128,128]{1,0:T(8,128)S(1)} %get-tuple-element.40, f32[8,128]{1,0:T(8,128)S(1)} %get-tuple-element.48), kind=kOutput, calls=%fused_computation.10 | convolution fusion | flops 33947648 | bytes 593920 | tf_op jit(solution)/shard_map/htn,thp->hnp/dot_general | solution.py:483
  65.3 27.7 %shard_map.149 = bf16[32,32,128]{2,1,0:T(8,128)(2,1)} custom-call(bf16[32,32,128]{2,1,0:T(8,128)(2,1)} %bitcast.124, f32[32,8,128]{2,1,0:T(8,128)} %get-tuple-element.21.refs_1_), custom_call_target="tpu_custom_call" | custom-call | tf_op jit(solution)/shard_map/pallas_call | solution.py:225
  93.0 1.3 %multiply_reduce_fusion = f32[32]{0:T(128)S(1)} fusion(bf16[32,32,128]{2,1,0:T(8,128)(2,1)S(1)} %copy-done.1, bf16[32,32,128]{2,1,0:T(8,128)(2,1)} %shard_map.149), kind=kLoop, calls=%fused_computation.51 | loop fusion | flops 524256 | bytes 524416 | tf_op jit(solution)/shard_map/reduce_sum | solution.py:497
  94.3 0.2 multiply_reduce_fusion.1
  94.5 0.3 convolution_bitcast_fusion
  95.6 0.3 reduce_window_sum.18
  96.0 0.3 fusion.6
  96.3 0.2 fusion.5
  96.5 0.4 fusion.3
  96.9 0.2 copy.81
  97.2 0.2 multiply_multiply_fusion
  97.4 0.4 copy-done.13
  97.9 0.6 select_maximum_fusion.rim_ref
  98.5 1.6 %gather_fusion = f32[384,128]{1,0:T(8,128)} fusion(f32[258,128]{1,0:T(8,128)S(1)} %reshape.209, s32[1024]{0:T(1024)S(1)} %pad_clamp_fusion), kind=kCustom, calls=%fused_computation | custom fusion | bytes 394752 | tf_op jit(solution)/shard_map/jit(_take)/gather | solution.py:539
  100.1 12.4 %shard_map.150 = (f32[24,128]{1,0:T(8,128)}, f32[8,1024]{1,0:T(8,128)}) custom-call(f32[16,24,128]{2,1,0:T(8,128)} %bitcast.125, f32[8,1152]{1,0:T(8,128)} %select_maximum_fusion.rim_ref), custom_call_target="tpu_custom_call" | custom-call | tf_op jit(solution)/shard_map/pallas_call | solution.py:309
  112.5 0.7 reshape.212
  113.3 0.6 fusion.42
  113.9 0.2 copy-done.9
  114.0 0.9 fusion.12
  115.0 0.7 divide_multiply_fusion
  (69 shorter events, 2.2 us)
Async XLA Ops:
  2.1 6.2 %collective-permute-start = (bf16[3,1280]{1,0:T(4,128)(2,1)S(1)}, bf16[3,1280]{1,0:T(4,128)(2,1)S(1)}, u32[]{:S(2)}, u32[]{:S(2)}) collective-permute-start(bf16[3,1280]{1,0:T(4,128)(2,1)S(1)} %pad_maximum_fusion.3), channel_id=1, source_target_pairs={{0,16},{16,32},{32,48},{48,64},{64,80},{80,96},{96,112},{112,128},... | collective-permute-start | bytes 23048 | tf_op jit(solution)/shard_map/ppermute | solution.py:340
  6.0 0.7 copy-start.7
  6.0 0.7 copy-start.14
  6.1 0.7 copy-start.12
  6.7 0.7 copy-start.10
  6.7 0.7 copy-start.8
  6.7 1.5 %copy-start.5 = (bf16[2,128,128]{2,1,0:T(8,128)(2,1)S(1)}, bf16[2,128,128]{2,1,0:T(8,128)(2,1)}, u32[]{:S(2)}) copy-start(bf16[2,128,128]{2,1,0:T(8,128)(2,1)} %param.16) | copy-start | bytes 196612
  7.4 0.7 copy-start.11
  8.4 1.0 copy-start.4
  36.9 0.7 copy-start.15
  37.9 1.0 copy-start.2
  38.0 1.0 copy-start.3
  38.0 1.0 copy-start.6
  62.7 1.0 copy-start.1
  93.0 1.4 %copy-start = (bf16[32,32,128]{2,1,0:T(8,128)(2,1)S(1)}, bf16[32,32,128]{2,1,0:T(8,128)(2,1)}, u32[]{:S(2)}) copy-start(bf16[32,32,128]{2,1,0:T(8,128)(2,1)} %shard_map.149) | copy-start | bytes 786436
  97.2 0.7 copy-start.13
  113.3 0.8 copy-start.9

commit v19 on v18

--- a/solution.py
+++ b/solution.py
@@ -256,8 +256,10 @@
             device_id=(me, t), device_id_type=MESH,
         )
 
-    for t in range(last):
-        @pl.when(hme != t)
+    for i in sorted(range(1, hn), key=lambda i: -min(i, hn - i)):
+        t = lax.rem(hme + i, hn)
+
+        @pl.when(t != last)
         def _():
             piece_copy(t, in_ref.at[t]).start()
 

time: 116 us -> 117 us (level)
  no operation moved by 1% of the time
where the time goes in v19:
time: 117 us
  Pallas kernels  86 us (74%)
  local copies, waits for them, and re-layouts  11.8 us (10%)
  other arithmetic  9.38 us (8%)
  matrix products  4.49 us (4%)
  starting transfers between devices  3.95 us (3%)
    pallas_call x1, Pallas kernels, scan_pieces(): pl.pallas_call(kern, out_shape=jax.ShapeDtypeStruct(piece, low), in_specs...  27.7 us
    pallas_call x1, Pallas kernels, scan_pieces(): pl.pallas_call(kern, out_shape=(jax.ShapeDtypeStruct(piece, low), jax.Sha...  24.5 us
    pallas_call x1, Pallas kernels, exchange(): pl.pallas_call(functools.partial(exchange_kernel, axis, n), out_shape=jax...  20.5 us
    pallas_call x1, Pallas kernels, tail_exchange(): pl.pallas_call(functools.partial(tail_kernel, n, hn), out_shape=(jax.Shap...  13.3 us
    unnamed x32, local copies, waits for them, and re-layouts  4.48 us
    ppermute x1, starting transfers between devices, passed_along(): return lax.ppermute(block, axis, route)  3.95 us
  transfers between devices with their start and end apart: 1, of which 0 were waited for; matrix products, arithmetic and copies ran while one was open for 1% of the time, Pallas kernels for 0%

profile of v19, /device:TPU:1, one launch (start us, length us, event | category | flops | bytes accessed | tf_op | source)
XLA Modules:
  0.0 116.6 jit_solution(130245841168685681)
XLA Ops:
  0.6 0.7 slice.139
  1.4 0.7 slice_bitcast_fusion.8
  2.1 3.9 %collective-permute-start = (bf16[3,1280]{1,0:T(4,128)(2,1)S(1)}, bf16[3,1280]{1,0:T(4,128)(2,1)S(1)}, u32[]{:S(2)}, u32[]{:S(2)}) collective-permute-start(bf16[3,1280]{1,0:T(4,128)(2,1)S(1)} %pad_maximum_fusion.3), channel_id=1, source_target_pairs={{0,16},{16,32},{32,48},{48,64},{64,80},{80,96},{96,112},{112,128},... | collective-permute-start | bytes 23048 | tf_op jit(solution)/shard_map/ppermute | solution.py:342
  6.1 0.6 copy-done.14
  6.8 0.3 reduce_window_sum.17
  7.1 0.2 slice_reduce_fusion
  7.5 0.7 copy-done.11
  8.7 0.7 copy-done.4
  9.4 0.3 multiply_convert_fusion.4
  9.8 0.2 copy.82
  9.9 0.3 convolution_convert_fusion.1
  10.3 0.8 pad_maximum_fusion.1.refs_0_
  11.0 24.5 %shard_map.147 = (bf16[32,32,128]{2,1,0:T(8,128)(2,1)}, f32[32,8,128]{2,1,0:T(8,128)}) custom-call(bf16[32,48,128]{2,1,0:T(8,128)(2,1)} %pad_maximum_fusion.1.refs_0_), custom_call_target="tpu_custom_call" | custom-call | tf_op jit(solution)/shard_map/pallas_call | solution.py:217
  35.5 1.1 copy.60
  36.7 0.2 fusion.40
  36.9 0.6 copy-done.15
  37.6 0.4 fusion.1
  38.0 0.2 copy.80
  38.2 0.7 copy-done.2
  39.0 0.3 multiply_reduce_fusion.5
  39.4 0.6 broadcast_in_dim.36.in_ref
  40.0 20.5 %shard_map.148 = f32[16,8,128]{2,1,0:T(8,128)} custom-call(f32[16,8,128]{2,1,0:T(8,128)} %broadcast_in_dim.36.in_ref), custom_call_target="tpu_custom_call" | custom-call | tf_op jit(solution)/shard_map/pallas_call | solution.py:57
  60.5 0.9 reduce_sum.130
  61.4 1.1 fusion.22
  62.5 0.2 copy.83
  62.7 0.5 multiply_reduce_fusion.6
  63.3 0.4 copy-done.1
  63.7 0.3 fusion.4
  64.0 1.3 %convolution_convert_fusion = bf16[8,128,128]{2,1,0:T(8,128)(2,1)} fusion(bf16[128,8,128]{0,2,1:T(8,128)(2,1)S(1)} %bitcast.111, f32[128,128]{1,0:T(8,128)S(1)} %get-tuple-element.40, f32[8,128]{1,0:T(8,128)S(1)} %get-tuple-element.48), kind=kOutput, calls=%fused_computation.10 | convolution fusion | flops 33947648 | bytes 593920 | tf_op jit(solution)/shard_map/htn,thp->hnp/dot_general | solution.py:485
  65.3 27.7 %shard_map.149 = bf16[32,32,128]{2,1,0:T(8,128)(2,1)} custom-call(bf16[32,32,128]{2,1,0:T(8,128)(2,1)} %bitcast.124, f32[32,8,128]{2,1,0:T(8,128)} %get-tuple-element.21.refs_1_), custom_call_target="tpu_custom_call" | custom-call | tf_op jit(solution)/shard_map/pallas_call | solution.py:225
  93.0 1.3 %multiply_reduce_fusion = f32[32]{0:T(128)S(1)} fusion(bf16[32,32,128]{2,1,0:T(8,128)(2,1)S(1)} %copy-done.1, bf16[32,32,128]{2,1,0:T(8,128)(2,1)} %shard_map.149), kind=kLoop, calls=%fused_computation.51 | loop fusion | flops 524256 | bytes 524416 | tf_op jit(solution)/shard_map/reduce_sum | solution.py:499
  94.3 0.2 multiply_reduce_fusion.1
  94.5 0.3 convolution_bitcast_fusion
  95.6 0.3 reduce_window_sum.18
  96.0 0.3 fusion.6
  96.3 0.2 fusion.5
  96.5 0.4 fusion.3
  96.9 0.2 copy.81
  97.2 0.2 multiply_multiply_fusion
  97.4 0.4 copy-done.13
  97.9 0.6 select_maximum_fusion.rim_ref
  98.5 1.6 %gather_fusion = f32[384,128]{1,0:T(8,128)} fusion(f32[258,128]{1,0:T(8,128)S(1)} %reshape.209, s32[1024]{0:T(1024)S(1)} %pad_clamp_fusion), kind=kCustom, calls=%fused_computation | custom fusion | bytes 394752 | tf_op jit(solution)/shard_map/jit(_take)/gather | solution.py:541
  100.1 13.3 %shard_map.150 = (f32[24,128]{1,0:T(8,128)}, f32[8,1024]{1,0:T(8,128)}) custom-call(f32[16,24,128]{2,1,0:T(8,128)} %bitcast.125, f32[8,1152]{1,0:T(8,128)} %select_maximum_fusion.rim_ref), custom_call_target="tpu_custom_call" | custom-call | tf_op jit(solution)/shard_map/pallas_call | solution.py:311
  113.4 0.7 reshape.212
  114.2 0.6 fusion.42
  114.8 0.2 copy-done.9
  115.0 0.9 fusion.12
  115.9 0.7 divide_multiply_fusion
  (69 shorter events, 2.2 us)
Async XLA Ops:
  2.1 6.2 %collective-permute-start = (bf16[3,1280]{1,0:T(4,128)(2,1)S(1)}, bf16[3,1280]{1,0:T(4,128)(2,1)S(1)}, u32[]{:S(2)}, u32[]{:S(2)}) collective-permute-start(bf16[3,1280]{1,0:T(4,128)(2,1)S(1)} %pad_maximum_fusion.3), channel_id=1, source_target_pairs={{0,16},{16,32},{32,48},{48,64},{64,80},{80,96},{96,112},{112,128},... | collective-permute-start | bytes 23048 | tf_op jit(solution)/shard_map/ppermute | solution.py:342
  6.0 0.7 copy-start.7
  6.0 0.7 copy-start.14
  6.1 0.7 copy-start.12
  6.7 0.7 copy-start.10
  6.7 0.7 copy-start.8
  6.7 1.5 %copy-start.5 = (bf16[2,128,128]{2,1,0:T(8,128)(2,1)S(1)}, bf16[2,128,128]{2,1,0:T(8,128)(2,1)}, u32[]{:S(2)}) copy-start(bf16[2,128,128]{2,1,0:T(8,128)(2,1)} %param.16) | copy-start | bytes 196612
  7.4 0.7 copy-start.11
  8.4 1.0 copy-start.4
  36.9 0.7 copy-start.15
  37.9 1.0 copy-start.2
  38.0 1.0 copy-start.3
  38.0 1.0 copy-start.6
  62.7 1.0 copy-start.1
  93.0 1.4 %copy-start = (bf16[32,32,128]{2,1,0:T(8,128)(2,1)S(1)}, bf16[32,32,128]{2,1,0:T(8,128)(2,1)}, u32[]{:S(2)}) copy-start(bf16[32,32,128]{2,1,0:T(8,128)(2,1)} %shard_map.149) | copy-start | bytes 786436
  97.2 0.7 copy-start.13
  114.2 0.8 copy-start.9
